TPU v7x, 128 devices: a whole 4x4x4 slice. The times are simulated.
128 devices in a mesh: gz: 8 (over x, core), xy: 16 (over y, z).
Axes of the slice: x: 4, y: 4, z: 4, core: 2. Of those that a mesh axis runs over, the one named last changes fastest.
Arguments:
- parent_feat: bfloat16 [128, 64, 2048], P(('gz', 'xy')), may hold values from -6 to 6
- parent_cell: int32 [128, 2048], P(('gz', 'xy')), may hold values from 0 to 255
- send_count: int32 [128, 128], P(('gz', 'xy')), may hold values from 1 to 16, as said below
- up_weight: bfloat16 [8, 64, 64], replicated, may hold values from -0.75 to 0.75
- conv_one: bfloat16 [27, 64, 64], replicated, may hold values from -0.15625 to 0.15625
- conv_two: bfloat16 [27, 64, 64], replicated, may hold values from -0.15625 to 0.15625
- child_mask: int32 [32, 8, 1024], P('xy', None, 'gz'), may hold values 0 or 1
- cotangent: bfloat16 [64, 32, 8, 1024], P(None, 'xy', None, 'gz'), may hold values from -6 to 6
Outputs:
- decoded: bfloat16 [64, 32, 8, 1024], P(None, 'xy', None, 'gz')
- grad_parent: bfloat16 [128, 64, 2048], P(('gz', 'xy'))
- grad_one: float32 [27, 64, 64], replicated
- grad_two: float32 [27, 64, 64], replicated
- grad_up: float32 [8, 64, 64], replicated
Inputs may be any that keep to these rules, and one draw needn't show every extreme that they name: `send_count`: some receiver gets 16 live slots from every sender, and every sender fills all 16 slots to some receiver. `parent_cell`: several slots may name the same parent voxel; their features add.
All inputs are finite; a program needn't handle non-finite values. No bound on the sum of `child_mask` on one device may be relied on, other than what follows from the above.
Results may differ from a plain program's by a relative error of at most 0.008.
Values may be sent and summed in bfloat16 or wider, within the bound.
No kernel may reach another device: no remote copies, remote signals or barrier semaphores. Data moves between devices by JAX's collectives and lax.ppermute only.
A program may use at most 64 MiB of HBM per device.

v0:
```python
import math

import jax
import jax.numpy as jnp
from jax import lax
from jax.sharding import PartitionSpec as P

OFFSETS = [(a, b, c) for a in (-1, 0, 1) for b in (-1, 0, 1) for c in (-1, 0, 1)]


def with_halo(shard, sides, width):
    for axis, dim in sides:
        devices, length = (lax.axis_size(axis), shard.shape[dim])
        up = [(i, (i + 1) % devices) for i in range(devices - 1)]
        down = [(j, i) for i, j in up]
        last = lax.slice_in_dim(shard, length - width, length, axis=dim)
        first = lax.slice_in_dim(shard, 0, width, axis=dim)
        before = lax.ppermute(last, axis, up)
        after = lax.ppermute(first, axis, down)
        shard = jnp.concatenate([before, shard, after], axis=dim)
    return shard


def extend(field):
    bordered = with_halo(field, (("xy", 1), ("gz", 3)), 1)
    return jnp.pad(bordered, ((0, 0), (0, 0), (1, 1), (0, 0)))


def window(padded, offset, direction, shape):
    nx, ny, nz = (shape[1], shape[2], shape[3])
    ox, oy, oz = (offset[0] * direction, offset[1] * direction, offset[2] * direction)
    part = padded[:, 1 + ox : 1 + ox + nx, 1 + oy : 1 + oy + ny, 1 + oz : 1 + oz + nz]
    return part.reshape(shape[0], -1)


def orient(matrix, direction):
    return matrix if direction > 0 else matrix.T


def convolve(padded, weights, direction, shape):
    total = jnp.zeros((shape[0], shape[1] * shape[2] * shape[3]), jnp.float32)
    for index, offset in enumerate(OFFSETS):
        total = total + jnp.dot(
            orient(weights[index], direction),
            window(padded, offset, direction, shape),
            preferred_element_type=jnp.float32,
        )
    return total.reshape(shape)


def weight_terms(delta, padded, shape):
    flat = delta.reshape(shape[0], -1)
    terms = [
        lax.dot_general(
            flat,
            window(padded, offset, 1, shape),
            (((1,), (1,)), ((), ())),
            preferred_element_type=jnp.float32,
        )
        for offset in OFFSETS
    ]
    return jnp.stack(terms)


def silu_slope(value):
    sig = jax.nn.sigmoid(value)
    return sig * (1.0 + value * (1.0 - sig))


def local(
    parent_feat, parent_cell, send_count, up_weight, conv_one, conv_two, child_mask, cotangent
):
    channels, size_x, size_y, size_z = cotangent.shape
    shape = cotangent.shape
    count_gz = lax.axis_size("gz")
    count_xy = lax.axis_size("xy")
    devices_all = count_gz * count_xy
    slot_total = parent_feat.shape[2]
    capacity = slot_total // devices_all
    half_x, half_y, half_z = (size_x // 2, size_y // 2, size_z // 2)
    parent_total = half_x * half_y * half_z
    slot_pos = jnp.arange(slot_total, dtype=jnp.int32) % capacity
    live = slot_pos < jnp.repeat(send_count[0], capacity)
    feats = jnp.where(live[None, :], parent_feat[0], jnp.zeros_like(parent_feat[0]))
    got_feat, got_cell = (
        lax.all_to_all(feats, ("gz", "xy"), split_axis=1, concat_axis=1, tiled=True),
        lax.all_to_all(parent_cell, ("gz", "xy"), split_axis=1, concat_axis=1, tiled=True),
    )
    got_cell = got_cell.reshape(slot_total)
    onehot = (got_cell[:, None] == jnp.arange(parent_total, dtype=jnp.int32)[None, :]).astype(
        jnp.bfloat16
    )
    parent_grid = jnp.dot(got_feat, onehot, preferred_element_type=jnp.float32).astype(jnp.bfloat16)
    up8 = jnp.einsum("ocd,dq->ocq", up_weight, parent_grid, preferred_element_type=jnp.float32)
    up = (
        up8.reshape(2, 2, 2, channels, half_x, half_y, half_z)
        .transpose(3, 4, 0, 5, 1, 6, 2)
        .reshape(shape)
    )
    maskf = child_mask.astype(jnp.float32)
    lifted = (maskf * up).astype(jnp.bfloat16)
    lifted_pad = extend(lifted)
    first_pre = convolve(lifted_pad, conv_one, 1, shape)
    first_act = (maskf * jax.nn.silu(first_pre)).astype(jnp.bfloat16)
    first_pad = extend(first_act)
    second_pre = convolve(first_pad, conv_two, 1, shape)
    decoded = (maskf * jax.nn.silu(second_pre)).astype(jnp.bfloat16)
    delta_two = (cotangent.astype(jnp.float32) * maskf * silu_slope(second_pre)).astype(
        jnp.bfloat16
    )
    term_two = weight_terms(delta_two, first_pad, shape)
    back_one = convolve(extend(delta_two), conv_two, -1, shape)
    delta_one = (back_one * maskf * silu_slope(first_pre)).astype(jnp.bfloat16)
    term_one = weight_terms(delta_one, lifted_pad, shape)
    delta_up = (convolve(extend(delta_one), conv_one, -1, shape) * maskf).astype(jnp.bfloat16)
    du8 = (
        delta_up.reshape(channels, half_x, 2, half_y, 2, half_z, 2)
        .transpose(2, 4, 6, 0, 1, 3, 5)
        .reshape(8, channels, parent_total)
    )
    term_up = jnp.einsum("ocq,dq->ocd", du8, parent_grid, preferred_element_type=jnp.float32)
    delta_parent = jnp.einsum(
        "ocd,ocq->dq", up_weight, du8, preferred_element_type=jnp.float32
    ).astype(jnp.bfloat16)
    slot_grad = lax.dot_general(
        delta_parent, onehot, (((1,), (1,)), ((), ())), preferred_element_type=jnp.float32
    ).astype(jnp.bfloat16)
    returned = lax.all_to_all(slot_grad, ("gz", "xy"), split_axis=1, concat_axis=1, tiled=True)
    grad_parent = jnp.where(live[None, :], returned, jnp.zeros_like(returned))[None]
    sum_one, sum_two, sum_up = lax.psum((term_one, term_two, term_up), ("gz", "xy"))
    scale = 1.0 / math.sqrt(size_x * count_xy * size_y * size_z * count_gz)
    return (decoded, grad_parent, sum_one * scale, sum_two * scale, sum_up * scale)


def solution(mesh):
    placed = (
        P(("gz", "xy"), None, None),
        P(("gz", "xy"), None),
        P(("gz", "xy"), None),
        P(),
        P(),
        P(),
        P("xy", None, "gz"),
        P(None, "xy", None, "gz"),
    )
    return jax.shard_map(
        local,
        mesh=mesh,
        in_specs=placed,
        out_specs=(P(None, "xy", None, "gz"), P(("gz", "xy"), None, None), P(), P(), P()),
        check_vma=False,
    )
```

profile of v0, /device:TPU:1, one launch (start us, length us, event | category | flops | bytes accessed | tf_op | source)
XLA Modules:
  0.0 432.3 jit_solution(10108309760339999828)
XLA Ops:
  9.8 11.5 %all-to-all-start.1 = ((s32[1,128,16]{2,0,1:T(1,128)}), s32[1,128,16]{2,0,1:T(1,128)S(1)}, u32[]{:S(2)}, u32[]{:S(2)}) async-start(s32[1,128,16]{2,0,1:T(1,128)} %bitcast.3), calls=%async_computation.1 | async-start | bytes 131072 | tf_op jit(solution)/shard_map/all_to_all | solution.py:87
  24.6 6.2 %all-to-all-done.1 = s32[1,128,16]{2,0,1:T(1,128)S(1)} async-done(((s32[1,128,16]{2,0,1:T(1,128)}), s32[1,128,16]{2,0,1:T(1,128)S(1)}, u32[]{:S(2)}, u32[]{:S(2)}) %all-to-all-start.1) | async-done | bytes 8224 | tf_op jit(solution)/shard_map/all_to_all | solution.py:87
  30.8 4.5 %all-to-all-start = ((bf16[128,2,512]{2,1,0:T(2,128)(2,1)}), bf16[128,2,512]{2,1,0:T(2,128)(2,1)S(1)}, u32[]{:S(2)}, u32[]{:S(2)}) async-start(bf16[128,2,512]{2,1,0:T(2,128)(2,1)} %reshape.685), calls=%async_computation | async-start | bytes 524288 | tf_op jit(solution)/shard_map/all_to_all | solution.py:86
  36.8 9.8 %all-to-all-done = bf16[128,2,512]{2,1,0:T(2,128)(2,1)S(1)} async-done(((bf16[128,2,512]{2,1,0:T(2,128)(2,1)}), bf16[128,2,512]{2,1,0:T(2,128)(2,1)S(1)}, u32[]{:S(2)}, u32[]{:S(2)}) %all-to-all-start) | async-done | bytes 262176 | tf_op jit(solution)/shard_map/all_to_all | solution.py:86
  53.9 3.6 collective-permute-done.1
  57.8 4.3 collective-permute-start.2
  68.2 4.4 %collective-permute-done.3 = bf16[64,4,8,1]{3,0,2,1:T(8,128)(2,1)S(1)} collective-permute-done((bf16[64,4,8,1]{3,0,2,1:T(8,128)(2,1)S(1)}, bf16[64,4,8,1]{3,0,2,1:T(8,128)(2,1)S(1)}, u32[]{:S(2)}, u32[]{:S(2)}) %collective-permute-start.3) | collective-permute-done | bytes 4128 | tf_op jit(solution)/shard_map/ppermute | solution.py:19
  96.8 3.8 collective-permute-done.5
  102.5 4.1 collective-permute-start.6
  113.1 4.4 %collective-permute-done.7 = bf16[64,4,8,1]{3,0,2,1:T(8,128)(2,1)} collective-permute-done((bf16[64,4,8,1]{3,0,2,1:T(8,128)(2,1)}, bf16[64,4,8,1]{3,0,2,1:T(8,128)(2,1)}, u32[]{:S(2)}, u32[]{:S(2)}) %collective-permute-start.7) | collective-permute-done | bytes 4128 | tf_op jit(solution)/shard_map/ppermute | solution.py:19
  149.3 5.2 %collective-permute-start.8 = (bf16[64,1,8,128]{3,0,2,1:T(8,128)(2,1)S(1)}, bf16[64,1,8,128]{3,0,2,1:T(8,128)(2,1)S(1)}, u32[]{:S(2)}, u32[]{:S(2)}) collective-permute-start(bf16[64,1,8,128]{3,0,2,1:T(8,128)(2,1)S(1)} %get-tuple-element.144), channel_id=1, source_target_pairs={{0,1},{1,2},{2,3},{3,4},{4,5},{5,6},{6,7},{7,8},{8,9},{9,10},{10,1... | collective-permute-start | bytes 393224 | tf_op jit(solution)/shard_map/ppermute | solution.py:18
  156.4 3.8 collective-permute-done.9
  160.6 3.8 collective-permute-start.10
  166.8 3.7 collective-permute-done.10
  170.5 4.4 %collective-permute-done.11 = bf16[64,4,8,1]{3,0,2,1:T(8,128)(2,1)S(1)} collective-permute-done((bf16[64,4,8,1]{3,0,2,1:T(8,128)(2,1)S(1)}, bf16[64,4,8,1]{3,0,2,1:T(8,128)(2,1)S(1)}, u32[]{:S(2)}, u32[]{:S(2)}) %collective-permute-start.11) | collective-permute-done | bytes 4128 | tf_op jit(solution)/shard_map/ppermute | solution.py:19
  203.5 3.5 collective-permute-start.12
  208.9 3.8 collective-permute-done.13
  213.0 4.1 collective-permute-start.14
  219.4 3.9 collective-permute-done.14
  223.3 4.4 %collective-permute-done.15 = bf16[64,4,8,1]{3,0,2,1:T(8,128)(2,1)S(1)} collective-permute-done((bf16[64,4,8,1]{3,0,2,1:T(8,128)(2,1)S(1)}, bf16[64,4,8,1]{3,0,2,1:T(8,128)(2,1)S(1)}, u32[]{:S(2)}, u32[]{:S(2)}) %collective-permute-start.15) | collective-permute-done | bytes 4128 | tf_op jit(solution)/shard_map/ppermute | solution.py:19
  253.7 7.1 %all-to-all-start.2 = ((bf16[128,2,512]{2,1,0:T(2,128)(2,1)}), bf16[128,2,512]{2,1,0:T(2,128)(2,1)S(1)}, u32[]{:S(2)}, u32[]{:S(2)}) async-start(bf16[128,2,512]{2,1,0:T(2,128)(2,1)} %reshape.687), calls=%async_computation.2 | async-start | bytes 524288 | tf_op jit(solution)/shard_map/all_to_all | solution.py:128
  262.7 9.3 %all-to-all-done.2 = bf16[128,2,512]{2,1,0:T(2,128)(2,1)S(1)} async-done(((bf16[128,2,512]{2,1,0:T(2,128)(2,1)}), bf16[128,2,512]{2,1,0:T(2,128)(2,1)S(1)}, u32[]{:S(2)}, u32[]{:S(2)}) %all-to-all-start.2) | async-done | bytes 262176 | tf_op jit(solution)/shard_map/all_to_all | solution.py:128
  273.6 147.1 %all-reduce.7.cloned.1.call-done = (f32[27,64,64]{2,1,0:T(8,128)}, f32[27,64,64]{2,1,0:T(8,128)}, f32[8,64,64]{2,1,0:T(8,128)}) async-done(((f32[27,64,64]{2,1,0:T(8,128)}, f32[27,64,64]{2,1,0:T(8,128)}, f32[8,64,64]{2,1,0:T(8,128)}), (f32[27,64,64]{2,1,0:T(8,128)}, f32[27,64,64]{2,1,0:T(8,128)}, f32[8,64,64]{2,1,0:T(8,128)})) %all-reduce.7.cloned.1.call-update) | async-done | bytes 1015824 | tf_op jit(solution)/shard_map/psum | solution.py:130
  422.4 2.9 broadcast_multiply_fusion
  (429 shorter events, 152.2 us)
Async XLA Ops:
  7.2 40.4 %copy-start = (bf16[8,64,64]{2,1,0:T(8,128)(2,1)S(1)}, bf16[8,64,64]{2,1,0:T(8,128)(2,1)}, u32[]{:S(2)}) copy-start(bf16[8,64,64]{2,1,0:T(8,128)(2,1)} %param.11) | copy-start | bytes 196612
  9.8 21.0 %all-to-all-start.1 = ((s32[1,128,16]{2,0,1:T(1,128)}), s32[1,128,16]{2,0,1:T(1,128)S(1)}, u32[]{:S(2)}, u32[]{:S(2)}) async-start(s32[1,128,16]{2,0,1:T(1,128)} %bitcast.3), calls=%async_computation.1 | async-start | bytes 131072 | tf_op jit(solution)/shard_map/all_to_all | solution.py:87
  23.2 12.0 %copy-start.33 = (s32[2,8,128]{2,1,0:T(8,128)S(1)}, s32[2,8,128]{2,1,0:T(8,128)}, u32[]{:S(2)}) copy-start(s32[2,8,128]{2,1,0:T(8,128)} %param.14) | copy-start | bytes 24580
  30.8 15.7 %all-to-all-start = ((bf16[128,2,512]{2,1,0:T(2,128)(2,1)}), bf16[128,2,512]{2,1,0:T(2,128)(2,1)S(1)}, u32[]{:S(2)}, u32[]{:S(2)}) async-start(bf16[128,2,512]{2,1,0:T(2,128)(2,1)} %reshape.685), calls=%async_computation | async-start | bytes 524288 | tf_op jit(solution)/shard_map/all_to_all | solution.py:86
  49.3 4.6 %collective-permute-start = (bf16[64,1,8,128]{3,0,2,1:T(8,128)(2,1)S(1)}, bf16[64,1,8,128]{3,0,2,1:T(8,128)(2,1)S(1)}, u32[]{:S(2)}, u32[]{:S(2)}) collective-permute-start(bf16[64,1,8,128]{3,0,2,1:T(8,128)(2,1)S(1)} %get-tuple-element.148), channel_id=1, source_target_pairs={{0,1},{1,2},{2,3},{3,4},{4,5},{5,6},{6,7},{7,8},{8,9},{9,10},{10,1... | collective-permute-start | bytes 393224 | tf_op jit(solution)/shard_map/ppermute | solution.py:18
  51.8 5.7 %collective-permute-start.1 = (bf16[64,1,8,128]{3,0,2,1:T(8,128)(2,1)S(1)}, bf16[64,1,8,128]{3,0,2,1:T(8,128)(2,1)S(1)}, u32[]{:S(2)}, u32[]{:S(2)}) collective-permute-start(bf16[64,1,8,128]{3,0,2,1:T(8,128)(2,1)S(1)} %get-tuple-element.149), channel_id=1, source_target_pairs={{1,0},{2,1},{3,2},{4,3},{5,4},{6,5},{7,6},{8,7},{9,8},{10,9},{11,1... | collective-permute-start | bytes 393224 | tf_op jit(solution)/shard_map/ppermute | solution.py:19
  53.9 18.7 %copy-start.17 = (bf16[64,1,8,128]{3,0,2,1:T(8,128)(2,1)}, bf16[64,1,8,128]{3,0,2,1:T(8,128)(2,1)S(1)}, u32[]{:S(2)}) copy-start(bf16[64,1,8,128]{3,0,2,1:T(8,128)(2,1)S(1)} %collective-permute-done) | copy-start | bytes 393220
  57.8 10.4 %collective-permute-start.2 = (bf16[64,4,8,1]{3,0,2,1:T(8,128)(2,1)S(1)}, bf16[64,4,8,1]{3,0,2,1:T(8,128)(2,1)S(1)}, u32[]{:S(2)}, u32[]{:S(2)}) collective-permute-start(bf16[64,4,8,1]{3,0,2,1:T(8,128)(2,1)S(1)} %get-tuple-element.132), channel_id=1, source_target_pairs={{0,16},{16,32},{32,48},{48,64},{64,80},{80,96},{96,112},{1,17},{17... | collective-permute-start | bytes 12296 | tf_op jit(solution)/shard_map/ppermute | solution.py:18
  62.1 10.5 %collective-permute-start.3 = (bf16[64,4,8,1]{3,0,2,1:T(8,128)(2,1)S(1)}, bf16[64,4,8,1]{3,0,2,1:T(8,128)(2,1)S(1)}, u32[]{:S(2)}, u32[]{:S(2)}) collective-permute-start(bf16[64,4,8,1]{3,0,2,1:T(8,128)(2,1)S(1)} %get-tuple-element.133), channel_id=1, source_target_pairs={{16,0},{32,16},{48,32},{64,48},{80,64},{96,80},{112,96},{17,1},{33... | collective-permute-start | bytes 12296 | tf_op jit(solution)/shard_map/ppermute | solution.py:19
  77.2 10.8 %copy-start.5 = (bf16[64,2,8,128]{3,0,2,1:T(8,128)(2,1)}, bf16[64,2,8,128]{3,0,2,1:T(8,128)(2,1)S(1)}, u32[]{:S(2)}) copy-start(bf16[64,2,8,128]{3,0,2,1:T(8,128)(2,1)S(1)} %get-tuple-element.141) | copy-start | bytes 786436
  92.9 3.9 collective-permute-start.4
  94.9 5.7 %collective-permute-start.5 = (bf16[64,1,8,128]{3,0,2,1:T(8,128)(2,1)S(1)}, bf16[64,1,8,128]{3,0,2,1:T(8,128)(2,1)S(1)}, u32[]{:S(2)}, u32[]{:S(2)}) collective-permute-start(bf16[64,1,8,128]{3,0,2,1:T(8,128)(2,1)S(1)} %get-tuple-element.147), channel_id=1, source_target_pairs={{1,0},{2,1},{3,2},{4,3},{5,4},{6,5},{7,6},{8,7},{9,8},{10,9},{11,1... | collective-permute-start | bytes 393224 | tf_op jit(solution)/shard_map/ppermute | solution.py:19
  102.5 10.6 %collective-permute-start.6 = (bf16[64,4,8,1]{3,0,2,1:T(8,128)(2,1)}, bf16[64,4,8,1]{3,0,2,1:T(8,128)(2,1)}, u32[]{:S(2)}, u32[]{:S(2)}) collective-permute-start(bf16[64,4,8,1]{3,0,2,1:T(8,128)(2,1)} %get-tuple-element.130), channel_id=1, source_target_pairs={{0,16},{16,32},{32,48},{48,64},{64,80},{80,96},{96,112},{1,17},{17... | collective-permute-start | bytes 12296 | tf_op jit(solution)/shard_map/ppermute | solution.py:18
  106.7 10.8 %collective-permute-start.7 = (bf16[64,4,8,1]{3,0,2,1:T(8,128)(2,1)}, bf16[64,4,8,1]{3,0,2,1:T(8,128)(2,1)}, u32[]{:S(2)}, u32[]{:S(2)}) collective-permute-start(bf16[64,4,8,1]{3,0,2,1:T(8,128)(2,1)} %get-tuple-element.131), channel_id=1, source_target_pairs={{16,0},{32,16},{48,32},{64,48},{80,64},{96,80},{112,96},{17,1},{33... | collective-permute-start | bytes 12296 | tf_op jit(solution)/shard_map/ppermute | solution.py:19
  149.3 7.2 %collective-permute-start.8 = (bf16[64,1,8,128]{3,0,2,1:T(8,128)(2,1)S(1)}, bf16[64,1,8,128]{3,0,2,1:T(8,128)(2,1)S(1)}, u32[]{:S(2)}, u32[]{:S(2)}) collective-permute-start(bf16[64,1,8,128]{3,0,2,1:T(8,128)(2,1)S(1)} %get-tuple-element.144), channel_id=1, source_target_pairs={{0,1},{1,2},{2,3},{3,4},{4,5},{5,6},{6,7},{7,8},{8,9},{9,10},{10,1... | collective-permute-start | bytes 393224 | tf_op jit(solution)/shard_map/ppermute | solution.py:18
  154.5 5.7 %collective-permute-start.9 = (bf16[64,1,8,128]{3,0,2,1:T(8,128)(2,1)S(1)}, bf16[64,1,8,128]{3,0,2,1:T(8,128)(2,1)S(1)}, u32[]{:S(2)}, u32[]{:S(2)}) collective-permute-start(bf16[64,1,8,128]{3,0,2,1:T(8,128)(2,1)S(1)} %get-tuple-element.145), channel_id=1, source_target_pairs={{1,0},{2,1},{3,2},{4,3},{5,4},{6,5},{7,6},{8,7},{9,8},{10,9},{11,1... | collective-permute-start | bytes 393224 | tf_op jit(solution)/shard_map/ppermute | solution.py:19
  160.6 9.9 %collective-permute-start.10 = (bf16[64,4,8,1]{3,0,2,1:T(8,128)(2,1)S(1)}, bf16[64,4,8,1]{3,0,2,1:T(8,128)(2,1)S(1)}, u32[]{:S(2)}, u32[]{:S(2)}) collective-permute-start(bf16[64,4,8,1]{3,0,2,1:T(8,128)(2,1)S(1)} %get-tuple-element.128), channel_id=1, source_target_pairs={{0,16},{16,32},{32,48},{48,64},{64,80},{80,96},{96,112},{1,17},{17... | collective-permute-start | bytes 12296 | tf_op jit(solution)/shard_map/ppermute | solution.py:18
  164.4 10.5 %collective-permute-start.11 = (bf16[64,4,8,1]{3,0,2,1:T(8,128)(2,1)S(1)}, bf16[64,4,8,1]{3,0,2,1:T(8,128)(2,1)S(1)}, u32[]{:S(2)}, u32[]{:S(2)}) collective-permute-start(bf16[64,4,8,1]{3,0,2,1:T(8,128)(2,1)S(1)} %get-tuple-element.129), channel_id=1, source_target_pairs={{16,0},{32,16},{48,32},{64,48},{80,64},{96,80},{112,96},{17,1},{33... | collective-permute-start | bytes 12296 | tf_op jit(solution)/shard_map/ppermute | solution.py:19
  203.5 5.4 %collective-permute-start.12 = (bf16[64,1,8,128]{3,0,2,1:T(8,128)(2,1)S(1)}, bf16[64,1,8,128]{3,0,2,1:T(8,128)(2,1)S(1)}, u32[]{:S(2)}, u32[]{:S(2)}) collective-permute-start(bf16[64,1,8,128]{3,0,2,1:T(8,128)(2,1)S(1)} %get-tuple-element.142), channel_id=1, source_target_pairs={{0,1},{1,2},{2,3},{3,4},{4,5},{5,6},{6,7},{7,8},{8,9},{9,10},{10,1... | collective-permute-start | bytes 393224 | tf_op jit(solution)/shard_map/ppermute | solution.py:18
  207.0 5.7 %collective-permute-start.13 = (bf16[64,1,8,128]{3,0,2,1:T(8,128)(2,1)S(1)}, bf16[64,1,8,128]{3,0,2,1:T(8,128)(2,1)S(1)}, u32[]{:S(2)}, u32[]{:S(2)}) collective-permute-start(bf16[64,1,8,128]{3,0,2,1:T(8,128)(2,1)S(1)} %get-tuple-element.143), channel_id=1, source_target_pairs={{1,0},{2,1},{3,2},{4,3},{5,4},{6,5},{7,6},{8,7},{9,8},{10,9},{11,1... | collective-permute-start | bytes 393224 | tf_op jit(solution)/shard_map/ppermute | solution.py:19
  213.0 10.2 %collective-permute-start.14 = (bf16[64,4,8,1]{3,0,2,1:T(8,128)(2,1)S(1)}, bf16[64,4,8,1]{3,0,2,1:T(8,128)(2,1)S(1)}, u32[]{:S(2)}, u32[]{:S(2)}) collective-permute-start(bf16[64,4,8,1]{3,0,2,1:T(8,128)(2,1)S(1)} %get-tuple-element.126), channel_id=1, source_target_pairs={{0,16},{16,32},{32,48},{48,64},{64,80},{80,96},{96,112},{1,17},{17... | collective-permute-start | bytes 12296 | tf_op jit(solution)/shard_map/ppermute | solution.py:18
  217.2 10.5 %collective-permute-start.15 = (bf16[64,4,8,1]{3,0,2,1:T(8,128)(2,1)S(1)}, bf16[64,4,8,1]{3,0,2,1:T(8,128)(2,1)S(1)}, u32[]{:S(2)}, u32[]{:S(2)}) collective-permute-start(bf16[64,4,8,1]{3,0,2,1:T(8,128)(2,1)S(1)} %get-tuple-element.127), channel_id=1, source_target_pairs={{16,0},{32,16},{48,32},{64,48},{80,64},{96,80},{112,96},{17,1},{33... | collective-permute-start | bytes 12296 | tf_op jit(solution)/shard_map/ppermute | solution.py:19
  253.7 18.3 %all-to-all-start.2 = ((bf16[128,2,512]{2,1,0:T(2,128)(2,1)}), bf16[128,2,512]{2,1,0:T(2,128)(2,1)S(1)}, u32[]{:S(2)}, u32[]{:S(2)}) async-start(bf16[128,2,512]{2,1,0:T(2,128)(2,1)} %reshape.687), calls=%async_computation.2 | async-start | bytes 524288 | tf_op jit(solution)/shard_map/all_to_all | solution.py:128
  260.8 159.9 %all-reduce.7.cloned.1.call-start = ((), (), s32[]{:S(2)}) async-start(), calls=%async_computation.3 | async-start | bytes 4063232 | tf_op jit(solution)/shard_map/psum | solution.py:130
  (33 other events, 92.0 us)
Sparse Core Ops, SparseCore 0:
  267.6 153.0 all-reduce.6
where the time goes:
time: 441 us; the launch traced here: 432 us
  waiting for transfers between devices  219 us (50%)
  starting transfers between devices  66 us (15%)
  matrix products  65.7 us (15%)
  local copies, waits for them, and re-layouts  41.5 us (9%)
  other arithmetic  23.5 us (5%)
  between operations  16.7 us (4%)
    psum x1, waiting for transfers between devices, local(): lax.psum((term_one, term_two, term_up), ('gz', 'xy'))  147 us
    dot_general x108, matrix products, convolve(): jnp.dot(orient(weights[index], direction), window(padded, offset, directi...  50.1 us
    ppermute x8, waiting for transfers between devices, with_halo(): after = lax.ppermute(first, axis, down)  32.5 us
    ppermute x8, starting transfers between devices, with_halo(): before = lax.ppermute(last, axis, up)  29.5 us
    slice x108, local copies, waits for them, and re-layouts, window(): part = padded[:, 1 + ox:1 + ox + nx, 1 + oy:1 + oy + ny, 1 + oz:1 + oz + nz]  23.1 us
    ppermute x8, waiting for transfers between devices, with_halo(): before = lax.ppermute(last, axis, up)  13.9 us
    ppermute x8, starting transfers between devices, with_halo(): after = lax.ppermute(first, axis, down)  13.4 us
    dot_general x54, matrix products, weight_terms(): lax.dot_general(flat, window(padded, offset, 1, shape), (((1,), (1,)), ((...  13.2 us
  transfers between devices with their start and end apart: 20, of which 20 were waited for; matrix products, arithmetic and copies ran while one was open for 3% of the time, Pallas kernels for 0%

commit v1 on v0

v1 whole, which is shorter than its diff:
```python
import functools
import math

import jax
import jax.numpy as jnp
from jax import lax
from jax.experimental import pallas as pl
from jax.experimental.pallas import tpu as pltpu
from jax.sharding import PartitionSpec as P

BF = jnp.bfloat16
F32 = jnp.float32
XK = (0, 1, 2, -1, -2, 3)
C = 64
Z = 128
Y = 8
K = 64
DEV = 128
NO_CELL = 256.0
STEP = 8


def iota(shape, dim):
    return lax.broadcasted_iota(jnp.int32, shape, dim)


def ones_where(cond):
    return jnp.where(cond, 1.0, 0.0).astype(BF)


def nt(a, b):
    return lax.dot_general(a, b, (((1,), (1,)), ((), ())), preferred_element_type=F32)


def nn(a, b):
    return lax.dot_general(a, b, (((1,), (0,)), ((), ())), preferred_element_type=F32)


def tn(a, b):
    return lax.dot_general(a, b, (((0,), (0,)), ((), ())), preferred_element_type=F32)


def over(total, body, step=STEP):
    full = total // step

    def one(i, carry):
        body(pl.multiple_of(i * step, step), step)
        return carry

    lax.fori_loop(0, full, one, 0)
    if total % step:
        body(full * step, total % step)


def low_lanes(shape):
    return iota(shape, len(shape) - 1) < C


def stack_y(block):
    count, rows, lanes = block.shape
    row = iota(block.shape, 1)
    below = jnp.where(row == 0, 0.0, pltpu.roll(block, 1, 1))
    above = jnp.where(row == rows - 1, 0.0, pltpu.roll(block, rows - 1, 1))
    wide = jnp.concatenate([below, block, above], axis=2)
    return wide.reshape(count * rows, 3 * lanes).astype(BF)


def call(kernel, outs, scratch=(), limit=58 << 20):
    single = isinstance(outs, tuple)
    shapes = [jax.ShapeDtypeStruct(s, d) for s, d in ([outs] if single else outs)]
    vmem = pl.BlockSpec(memory_space=pltpu.VMEM)

    def run(*args):
        got = pl.pallas_call(
            kernel,
            out_shape=shapes,
            in_specs=[vmem] * len(args),
            out_specs=[vmem] * len(shapes),
            scratch_shapes=[pltpu.VMEM(s, d) for s, d in scratch],
            compiler_params=pltpu.CompilerParams(vmem_limit_bytes=limit),
        )(*args)
        return got[0] if single else got

    return run


def weights_kernel(up_ref, one_ref, two_ref, w1_ref, w2_ref, b1_ref, b0_ref, u_ref, ud_ref):
    zero = jnp.zeros((C, C), BF)

    def tap(ref, ox, oy, oz):
        return zero if abs(ox) > 1 else ref[9 * (ox + 1) + 3 * (oy + 1) + oz + 1]

    def join(a, b):
        return jnp.concatenate([a, b], axis=1)

    for oz in (-1, 0, 1):
        for oy in (-1, 0, 1):
            for n, xo in enumerate((0, 1, 2, -1)):
                rows = slice(n * C, n * C + C)
                for p in range(3):
                    at = (oy + 1) * 384 + p * 128
                    pair = [tap(one_ref, XK[2 * p + s] - xo, oy, oz) for s in (0, 1)]
                    w1_ref[oz + 1, rows, at : at + 128] = join(*pair)
            for n, xo in enumerate((0, 1)):
                at_row = (oz + 1) * 128 + n * C
                for p in range(2):
                    at = (oy + 1) * 256 + p * 128
                    pair = [tap(two_ref, XK[2 * p + s] - xo, oy, oz) for s in (0, 1)]
                    w2_ref[at_row : at_row + C, at : at + 128] = join(*pair)
            for kk, xk in enumerate(XK):
                at_row = (oy + 1) * 384 + kk * C
                for p, pair in enumerate(((0, 1), (2, -1))):
                    b1_ref[oz + 1, at_row : at_row + C, p * 128 : p * 128 + 128] = join(
                        *[tap(two_ref, xo - xk, -oy, -oz) for xo in pair]
                    )
            for kk, xk in enumerate(XK[:4]):
                at_row = (oy + 1) * 256 + kk * C
                at = (oz + 1) * 128
                b0_ref[at_row : at_row + C, at : at + 128] = join(
                    *[tap(one_ref, xo - xk, -oy, -oz) for xo in (0, 1)]
                )
    for e in (0, 1):
        for b in (0, 1):
            for a in (0, 1):
                at = (e * 4 + b * 2 + a) * C
                u_ref[at : at + C, :] = join(up_ref[4 * a + 2 * b + e], zero)
        for a in (0, 1):
            at = 512 + (e * 2 + a) * C
            u_ref[at : at + C, :] = ones_where(iota((C, 128), 1) == C + 2 * a + e)
            ud_ref[e, a * C : a * C + C, :] = join(up_ref[4 * a + e], up_ref[4 * a + 2 + e])


def send_kernel(feat_ref, cell_ref, count_ref, out_ref):
    spread = ones_where((iota((DEV, 2048), 1) >> 4) == iota((DEV, 2048), 0))
    count = jnp.broadcast_to(count_ref[...].astype(F32), (8, DEV)).astype(BF)
    counts = nn(count, spread)[0:1]
    slot = (iota((1, 2048), 1) & 15).astype(F32)
    cell = jnp.where(slot < counts, cell_ref[...].astype(F32), NO_CELL)
    for chunk in range(16):
        at = slice(chunk * 128, chunk * 128 + 128)
        feats = feat_ref[0, :, at].astype(F32)
        cells = jnp.broadcast_to(cell[:, at], (C, 128))
        turned = jnp.concatenate([feats, cells], axis=0).T.reshape(8, 2, 8, 128)
        first, second = turned[:, 0], turned[:, 1]
        low = low_lanes(first.shape)
        to = slice(chunk * 8, chunk * 8 + 8)
        out_ref[to, 0:8, :] = jnp.where(low, first, pltpu.roll(second, C, 2)).astype(BF)
        out_ref[to, 8:16, :] = jnp.where(low, pltpu.roll(first, C, 2), second).astype(BF)


def onehots(recv_ref):
    cells = recv_ref[:, 8:16, :].astype(F32).reshape(1024, 128)
    ids = iota((1024, 256), 1).astype(F32)
    return ones_where(cells[:, 0:1] == ids), ones_where(cells[:, C : C + 1] == ids)


def grid_kernel(recv_ref, mask_ref, cot_ref, rec_ref, up_ref, down_ref):
    feats = recv_ref[:, 0:8, :].astype(F32).reshape(1024, 128).astype(BF)
    both = tn(feats, jnp.concatenate(onehots(recv_ref), axis=1))
    grid = both[0:C, 0:256] + both[C:128, 256:512]
    grid = jnp.concatenate([grid, jnp.zeros((C, 256), F32)], axis=0).astype(BF)
    row, col = iota((512, 256), 0), iota((512, 256), 1)
    pick = ones_where(col == ((row & 7) >> 1) * K + (row >> 3))
    rec = nt(pick, grid)
    kk, zz = iota((K, Y, Z), 0), iota((K, Y, Z), 2)
    zrow, lane = iota((Z, 128), 0), iota((Z, 128), 1)
    for a in (0, 1):
        mine = jnp.where((zz >> 1) == kk, mask_ref[a].astype(F32)[None], 0.0)
        place = ones_where(lane == C + 2 * a + (zrow & 1))
        rec = rec + nn(mine.reshape(512, Z).astype(BF), place)
    rec = rec.reshape(K, Y, 128).astype(BF)
    rec_ref[...] = rec
    up_ref[0:2] = rec_ref[K - 2 : K]
    up_ref[2:4] = cot_ref[Z - 2 : Z]
    down_ref[0:2] = rec_ref[0:2]
    down_ref[2:4] = cot_ref[0:2]


def lane_groups(own, left, right):
    low = low_lanes(own.shape)
    return own, jnp.where(low, right, left), jnp.where(low, left, right)


def forward_kernel(
    own_ref, left_ref, right_ref, cot_ref, u_ref, w1_ref, w2_ref,
    act_ref, delta_ref, dec_ref, slope_ref, lifted_ref, keep_ref,
    lift, seen, mask, col1, part1, col2, part2,
):
    kz = own_ref.shape[0]
    odd_row = (iota((kz, Y, 128), 1) & 1) == 1
    for t, ref in enumerate((own_ref, left_ref, right_ref)):
        rec = ref[...].astype(F32).reshape(kz * Y, 128).astype(BF)
        for e in (0, 1):
            both = nt(rec, u_ref[e * 256 : e * 256 + 256, :]).reshape(kz, Y, 256)
            live = nt(rec, u_ref[512 + e * 128 : 640 + e * 128, :]).reshape(kz, Y, 128)
            lift[t, :, e] = live * jnp.where(odd_row, both[:, :, 128:], both[:, :, :128])
            seen[t, :, e] = live

    def columns(k0, n):
        def load(ref):
            return lane_groups(*[ref[t, pl.ds(k0, n)].reshape(2 * n, Y, 128) for t in range(3)])

        own, near, far = load(lift)
        at = pl.ds(2 * k0, 2 * n)
        lifted_ref[at] = jnp.concatenate([own, near], axis=2).astype(BF)
        rows = pl.ds(pl.multiple_of(k0 * 16, 16), 16 * n)
        col1[rows, :] = stack_y(jnp.concatenate([own, near, far], axis=2))
        live_own, live_near, _ = load(seen)
        mask[at] = jnp.concatenate([live_own, live_near], axis=2)

    over(kz, columns, 4)
    for s in range(3):
        part1[s] = nt(col1[...], w1_ref[s]).reshape(2 * kz, Y, 256)

    def first(m, n):
        pre = part1[0, pl.ds(m, n)] + part1[1, pl.ds(m + 1, n)] + part1[2, pl.ds(m + 2, n)]
        live = mask[pl.ds(m + 1, n)]
        sig = jax.nn.sigmoid(pre)
        act = live * (pre * sig)
        slope_ref[pl.ds(m, n)] = live * (sig * (1.0 + pre * (1.0 - sig)))
        act_ref[pl.ds(m, n)] = act.astype(BF)
        col2[pl.ds(pl.multiple_of(m * Y, 16), n * Y), :] = stack_y(act)

    over(2 * kz - 2, first)
    part2[...] = nt(col2[...], w2_ref[...]).reshape(2 * kz - 2, Y, 384)

    def second(q, n):
        pre = (
            part2[pl.ds(q, n), :, 0:128]
            + part2[pl.ds(q + 1, n), :, 128:256]
            + part2[pl.ds(q + 2, n), :, 256:384]
        )
        live = mask[pl.ds(q + 2, n), :, 0:128]
        sig = jax.nn.sigmoid(pre)
        at = pl.ds(q, n)
        dec_ref[at] = (live * (pre * sig)).astype(BF)
        slope = live * (sig * (1.0 + pre * (1.0 - sig)))
        delta_ref[at] = (cot_ref[at].astype(F32) * slope).astype(BF)
        keep_ref[at] = live.astype(BF)

    over(2 * kz - 4, second)


def wgrad(count, field, padded, shifted, col):
    def build(m, n):
        three = [padded[pl.ds(m + s, n)] for s in (2, 1, 0)]
        rows = pl.ds(pl.multiple_of(m * Y, 16), n * Y)
        shifted[rows, :] = jnp.concatenate(three, axis=2).reshape(n * Y, 384).astype(BF)
        col[rows, :] = stack_y(field(m, n))

    over(count, build)
    return tn(shifted[...], col[...])


def packed(block):
    return jnp.concatenate([block[0:32], block[32:64]], axis=1).astype(BF)


def tap_grads(total, put):
    place = {0: 0, 1: 1, 2: 2, -1: 3}
    for ox in (-1, 0, 1):
        for oy in (-1, 0, 1):
            for oz in (-1, 0, 1):
                sums = []
                for x in (0, 1):
                    r = (oz + 1) * 128 + x * C
                    c = (oy + 1) * 256 + place[x + ox] * C
                    sums.append(total[r : r + C, c : c + C])
                put(9 * (ox + 1) + 3 * (oy + 1) + oz + 1, packed(sums[0] + sums[1]))


def second_grad_kernel(act_ref, delta_ref, out_ref, padded, shifted, col, total):
    padded[0:4] = jnp.zeros((4, Y, 128), F32)
    padded[132:136] = jnp.zeros((4, Y, 128), F32)
    padded[4:132] = delta_ref[2:130].astype(F32)
    total[...] = wgrad(134, lambda m, n: act_ref[pl.ds(m, n)].astype(F32), padded, shifted, col)

    def put(t, block):
        out_ref[t] = block

    tap_grads(total, put)


def backward_kernel(
    own_ref, left_ref, right_ref, slope_ref, keep_ref, lifted_ref, rec_ref, recv_ref,
    b1_ref, b0_ref, ud_ref, two_ref, out_ref,
    col3, part3, col4, part4, padded, shifted, col, total, du,
):
    def columns(q, n):
        at = pl.ds(q, n)
        groups = lane_groups(*[r[at].astype(F32) for r in (own_ref, left_ref, right_ref)])
        rows = pl.ds(pl.multiple_of(q * Y, 16), n * Y)
        col3[rows, :] = stack_y(jnp.concatenate(groups, axis=2))

    over(132, columns)
    for s in range(3):
        part3[s] = nn(col3[...], b1_ref[s]).reshape(132, Y, 256)

    def first(r, n):
        back = part3[0, pl.ds(r, n)] + part3[1, pl.ds(r + 1, n)] + part3[2, pl.ds(r + 2, n)]
        delta = back * slope_ref[pl.ds(r + 2, n)]
        padded[pl.ds(r + 2, n)] = delta[:, :, 0:128]
        col4[pl.ds(pl.multiple_of(r * Y, 16), n * Y), :] = stack_y(delta)

    over(130, first)
    padded[0:3] = jnp.zeros((3, Y, 128), F32)
    padded[131:134] = jnp.zeros((3, Y, 128), F32)
    part4[...] = nn(col4[...], b0_ref[...]).reshape(130, Y, 384)

    def upper(z, n):
        back = (
            part4[pl.ds(z, n), :, 0:128]
            + part4[pl.ds(z + 1, n), :, 128:256]
            + part4[pl.ds(z + 2, n), :, 256:384]
        )
        value = keep_ref[pl.ds(z + 2, n)].astype(F32) * back
        du[pl.ds(z >> 1, n // 2)] = value.reshape(n // 2, 2, Y, 128)

    over(Z, upper)

    split = [du[:, e].reshape(K * Y, 128).astype(BF) for e in (0, 1)]
    row, lane = iota((K * Y, 128), 0), iota((K * Y, 128), 1)
    match = ((row & 1) == 0) == (lane < C)
    summed = nn(split[0], ud_ref[0]) + nn(split[1], ud_ref[1])
    summed = jnp.where(match, summed, 0.0).reshape(K, Y, 128)
    summed = summed + pltpu.roll(summed, Y - 1, 1)
    summed = summed + pltpu.roll(summed, C, 2)
    parent = summed.reshape(K * Y, 128).astype(BF)
    cell, src = iota((256, 512), 0), iota((256, 512), 1)
    pick = ones_where(src == (cell & (K - 1)) * Y + 2 * (cell >> 6))
    parent = nn(pick, parent).astype(BF)
    slots = [nn(hot, parent) for hot in onehots(recv_ref)]
    slots = jnp.where(iota((1024, 128), 1) < C, slots[0], slots[1])
    out_ref[:, 0:8, :] = slots.reshape(DEV, 8, 128).astype(BF)

    def put(index, block):
        out_ref[2 * index, 8:24, :] = block[0:16]
        out_ref[2 * index + 1, 8:24, :] = block[16:32]

    rec = rec_ref[...].astype(F32).reshape(K * Y, 128)
    rec = jnp.where(lane < C, rec, pltpu.roll(rec, C, 1))
    rec = jnp.where(match, rec, 0.0).astype(BF)
    for e in (0, 1):
        up_grad = tn(split[e], rec)
        for a in (0, 1):
            for b in (0, 1):
                block = up_grad[a * C : a * C + C, b * C : b * C + C]
                put(54 + 4 * a + 2 * b + e, packed(block))
    total[...] = wgrad(
        132, lambda m, n: lifted_ref[pl.ds(m + 2, n)].astype(F32), padded, shifted, col
    )
    tap_grads(total, lambda t, block: put(27 + t, block))
    for t in range(27):
        put(t, two_ref[t])
    out_ref[124:128, 8:24, :] = jnp.zeros((4, 16, 128), BF)


def sum_kernel(recv_ref, out_ref, *, scale):
    def one(i, total):
        return total + jnp.sum(recv_ref[pl.ds(i * 8, 8), 8:24, :].astype(F32), axis=0)

    total = lax.fori_loop(0, 16, one, jnp.zeros((16, 128), F32))
    out_ref[...] = jnp.broadcast_to((total * scale).astype(BF)[None], out_ref.shape)


def slot_kernel(recv_ref, out_ref):
    for chunk in range(16):
        block = recv_ref[chunk * 8 : chunk * 8 + 8, 0:8, :].astype(F32)
        halves = [block[:, None], pltpu.roll(block, C, 2)[:, None]]
        turned = jnp.concatenate(halves, axis=1).reshape(128, 128).T
        out_ref[0, :, chunk * 128 : chunk * 128 + 128] = turned[0:C].astype(BF)


def unpack_kernel(recv_ref, one_ref, two_ref, up_ref):
    def matrix(index):
        top = recv_ref[2 * index].astype(F32)
        low = recv_ref[2 * index + 1].astype(F32)
        both = jnp.concatenate([top, low], axis=0)
        return jnp.concatenate([both[:, :C], both[:, C:]], axis=0)

    for t in range(27):
        two_ref[t] = matrix(t)
        one_ref[t] = matrix(27 + t)
    for o in range(8):
        up_ref[o] = matrix(54 + o)


def shift(array, axis, step):
    count = lax.axis_size(axis)
    pairs = [(i, i + step) for i in range(count) if 0 <= i + step < count]
    return lax.ppermute(array, axis, pairs)


def exchange(array):
    return lax.all_to_all(array, ("gz", "xy"), 0, 0, tiled=True)


def local(
    parent_feat, parent_cell, send_count, up_weight, conv_one, conv_two, child_mask, cotangent
):
    size_x, size_y, size_z = cotangent.shape[1:]
    voxels = size_x * size_y * size_z * lax.axis_size("xy") * lax.axis_size("gz")
    scale = 1.0 / math.sqrt(voxels)
    kz = K + 4

    sent = call(send_kernel, ((DEV, 16, 128), BF))(parent_feat, parent_cell, send_count)
    recv = exchange(sent)
    cot = cotangent.transpose(3, 2, 1, 0).reshape(Z, Y, 128)
    w1, w2, b1, b0, u, ud = call(
        weights_kernel,
        [
            ((3, 256, 1152), BF), ((384, 768), BF), ((3, 1152, 256), BF), ((768, 384), BF),
            ((768, 128), BF), ((2, 128, 128), BF),
        ],
    )(up_weight, conv_one, conv_two)
    rec, up_edge, down_edge = call(
        grid_kernel, [((K, Y, 128), BF), ((4, Y, 128), BF), ((4, Y, 128), BF)]
    )(recv, child_mask, cot)
    before = shift(up_edge, "gz", 1)
    after = shift(down_edge, "gz", -1)
    rec_ext = jnp.concatenate([before[0:2], rec, after[0:2]], axis=0)
    cot_ext = jnp.concatenate([before[2:4], cot, after[2:4]], axis=0)
    rec_left, rec_right = shift(rec_ext, "xy", 1), shift(rec_ext, "xy", -1)
    act, delta, dec, slope, lifted, keep = call(
        forward_kernel,
        [
            ((134, Y, 256), BF), ((132, Y, 128), BF), ((132, Y, 128), BF),
            ((134, Y, 256), F32), ((136, Y, 256), BF), ((132, Y, 128), BF),
        ],
        [
            ((3, kz, 2, Y, 128), F32), ((3, kz, 2, Y, 128), F32), ((136, Y, 256), F32),
            ((1088, 1152), BF), ((3, 136, Y, 256), F32), ((1072, 768), BF), ((134, Y, 384), F32),
        ],
    )(rec_ext, rec_left, rec_right, cot_ext, u, w1, w2)
    delta_left, delta_right = shift(delta, "xy", 1), shift(delta, "xy", -1)
    two = call(
        second_grad_kernel,
        ((27, 32, 128), BF),
        [((136, Y, 128), F32), ((1072, 384), BF), ((1072, 768), BF), ((384, 768), F32)],
    )(act, delta)
    decoded = dec[2 : 2 + Z].reshape(Z, Y, 2, C).transpose(3, 2, 1, 0)
    message = call(
        backward_kernel,
        ((DEV, 24, 128), BF),
        [
            ((1056, 1152), BF), ((3, 132, Y, 256), F32), ((1040, 768), BF), ((130, Y, 384), F32),
            ((134, Y, 128), F32), ((1056, 384), BF), ((1056, 768), BF), ((384, 768), F32),
            ((K, 2, Y, 128), F32),
        ],
    )(
        delta, delta_left, delta_right, slope, keep, lifted, rec, recv, b1, b0, ud, two
    )
    back = exchange(message)
    total = call(functools.partial(sum_kernel, scale=scale), ((DEV, 16, 128), BF))(back)
    gathered = exchange(total)
    grad_parent = call(slot_kernel, ((1, C, 2048), BF))(back)
    grad_one, grad_two, grad_up = call(
        unpack_kernel, [((27, C, C), F32), ((27, C, C), F32), ((8, C, C), F32)]
    )(gathered)
    return decoded, grad_parent, grad_one, grad_two, grad_up


def solution(mesh):
    placed = (
        P(("gz", "xy"), None, None),
        P(("gz", "xy"), None),
        P(("gz", "xy"), None),
        P(),
        P(),
        P(),
        P("xy", None, "gz"),
        P(None, "xy", None, "gz"),
    )
    return jax.shard_map(
        local,
        mesh=mesh,
        in_specs=placed,
        out_specs=(P(None, "xy", None, "gz"), P(("gz", "xy"), None, None), P(), P(), P()),
        check_vma=False,
    )
```

time: 441 us -> 139 us (0.32); the launches traced: 432 us -> 138 us
  waiting for transfers between devices: 219 us -> 29.1 us
  matrix products: 65.7 us -> 0 us
  Pallas kernels: 0 us -> 43.1 us
  local copies, waits for them, and re-layouts: 41.5 us -> 5.11 us
  starting transfers between devices: 66 us -> 31.4 us
  blocking collectives: 0 us -> 27.1 us
  other arithmetic: 23.5 us -> 1.66 us
  between operations: 16.7 us -> 0.8 us
    psum x1 -> x0, waiting for transfers between devices: 147 us -> none  [local(): lax.psum((term_one, term_two, term_up), ('gz', 'xy'))]
    dot_general x166 -> x0, matrix products: 65.7 us -> none  [the longest x108 50.1 us: convolve(): jnp.dot(orient(weights[index], direction), window(padded, offset, directi...]
    pallas_call x0 -> x9, Pallas kernels: none -> 43.1 us  [run(): pl.pallas_call(kernel, out_shape=shapes, in_specs=[vmem] * len(args), out...]
    ppermute x16 -> x6, waiting for transfers between devices: 46.5 us -> 5.72 us  [shift(): return lax.ppermute(array, axis, pairs)]
    ppermute x16 -> x6, starting transfers between devices: 42.9 us -> 15.6 us  [shift(): return lax.ppermute(array, axis, pairs)]
    all_to_all x0 -> x1, blocking collectives: none -> 27.1 us  [exchange(): return lax.all_to_all(array, ('gz', 'xy'), 0, 0, tiled=True)]
    slice x116 -> x4, local copies, waits for them, and re-layouts: 25.1 us -> 0.25 us  [the longest x2 0.25 us: local(): decoded = dec[2:2 + Z].reshape(Z, Y, 2, C).transpose(3, 2, 1, 0)]
    all_to_all x3 -> x2, starting transfers between devices: 23 us -> 15.8 us  [exchange(): return lax.all_to_all(array, ('gz', 'xy'), 0, 0, tiled=True)]
  transfers between devices with their start and end apart: 20 -> 8, of which waited for: 20 -> 5; matrix products, arithmetic and copies ran while one was open for 3% -> 2% of each run, Pallas kernels for 0% -> 7%
where the time goes in v1:
time: 139 us; the launch traced here: 138 us
  Pallas kernels  43.1 us (31%)
  starting transfers between devices  31.4 us (23%)
  waiting for transfers between devices  29.1 us (21%)
  blocking collectives  27.1 us (19%)
  local copies, waits for them, and re-layouts  5.11 us (4%)
  other arithmetic  1.66 us (1%)
    pallas_call x9, Pallas kernels, run(): pl.pallas_call(kernel, out_shape=shapes, in_specs=[vmem] * len(args), out...  43.1 us
    all_to_all x1, blocking collectives, exchange(): return lax.all_to_all(array, ('gz', 'xy'), 0, 0, tiled=True)  27.1 us
    all_to_all x2, waiting for transfers between devices, exchange(): return lax.all_to_all(array, ('gz', 'xy'), 0, 0, tiled=True)  23.4 us
    all_to_all x2, starting transfers between devices, exchange(): return lax.all_to_all(array, ('gz', 'xy'), 0, 0, tiled=True)  15.8 us
    ppermute x6, starting transfers between devices, shift(): return lax.ppermute(array, axis, pairs)  15.6 us
    ppermute x6, waiting for transfers between devices, shift(): return lax.ppermute(array, axis, pairs)  5.72 us
    unnamed x22, local copies, waits for them, and re-layouts  3.98 us
  transfers between devices with their start and end apart: 8, of which 5 were waited for; matrix products, arithmetic and copies ran while one was open for 2% of the time, Pallas kernels for 7%

profile of v1, /device:TPU:1, one launch (start us, length us, event | category | flops | bytes accessed | tf_op | source)
XLA Modules:
  0.0 138.3 jit_solution(3938813427676489212)
XLA Ops:
  0.6 2.4 %shard_map.119 = bf16[128,16,128]{2,1,0:T(8,128)(2,1)} custom-call(bf16[1,64,2048]{2,1,0:T(8,128)(2,1)} %feat_ref.1, s32[1,2048]{1,0:T(1,128)} %cell_ref.1, s32[1,128]{1,0:T(1,128)} %count_ref.1), custom_call_target="tpu_custom_call" | custom-call | tf_op jit(solution)/shard_map/pallas_call | solution.py:74
  3.0 11.5 %all-to-all-start = ((bf16[128,16,128]{2,1,0:T(8,128)(2,1)}), bf16[128,16,128]{2,1,0:T(8,128)(2,1)S(1)}, u32[]{:S(2)}, u32[]{:S(2)}) async-start(bf16[128,16,128]{2,1,0:T(8,128)(2,1)} %shard_map.119), calls=%async_computation | async-start | bytes 1048576 | tf_op jit(solution)/shard_map/all_to_all | solution.py:395
  14.6 0.9 copy.16.cot_ref
  15.5 12.9 %all-to-all-done.recv_ref = bf16[128,16,128]{2,1,0:T(8,128)(2,1)S(1)} async-done(((bf16[128,16,128]{2,1,0:T(8,128)(2,1)}), bf16[128,16,128]{2,1,0:T(8,128)(2,1)S(1)}, u32[]{:S(2)}, u32[]{:S(2)}) %all-to-all-start) | async-done | bytes 524320 | tf_op jit(solution)/shard_map/all_to_all | solution.py:395
  29.2 2.6 %shard_map.120 = (bf16[64,8,128]{2,1,0:T(8,128)(2,1)}, bf16[4,8,128]{2,1,0:T(8,128)(2,1)}, bf16[4,8,128]{2,1,0:T(8,128)(2,1)}) custom-call(bf16[128,16,128]{2,1,0:T(8,128)(2,1)} %copy-done, s32[2,8,128]{2,1,0:T(8,128)} %mask_ref.1, bf16[128,8,128]{2,1,0:T(8,128)(2,1)} %copy.16.cot_ref), custom_call_target="tpu_custom_call" | custom-call | tf_op jit(solution)/shard_map/pallas_call | solution.py:74
  31.8 2.9 %collective-permute-start = (bf16[4,8,128]{2,1,0:T(8,128)(2,1)}, bf16[4,8,128]{2,1,0:T(8,128)(2,1)S(1)}, u32[]{:S(2)}, u32[]{:S(2)}) collective-permute-start(bf16[4,8,128]{2,1,0:T(8,128)(2,1)} %get-tuple-element.23), channel_id=1, source_target_pairs={{0,16},{16,32},{32,48},{48,64},{64,80},{80,96},{96,112},{1,17},{17... | collective-permute-start | bytes 24584 | tf_op jit(solution)/shard_map/ppermute | solution.py:391
  34.7 1.9 %collective-permute-start.1 = (bf16[4,8,128]{2,1,0:T(8,128)(2,1)}, bf16[4,8,128]{2,1,0:T(8,128)(2,1)S(1)}, u32[]{:S(2)}, u32[]{:S(2)}) collective-permute-start(bf16[4,8,128]{2,1,0:T(8,128)(2,1)} %get-tuple-element.25), channel_id=1, source_target_pairs={{16,0},{32,16},{48,32},{64,48},{80,64},{96,80},{112,96},{17,1},{33... | collective-permute-start | bytes 24584 | tf_op jit(solution)/shard_map/ppermute | solution.py:391
  36.7 3.2 %collective-permute-done.1 = bf16[4,8,128]{2,1,0:T(8,128)(2,1)S(1)} collective-permute-done((bf16[4,8,128]{2,1,0:T(8,128)(2,1)}, bf16[4,8,128]{2,1,0:T(8,128)(2,1)S(1)}, u32[]{:S(2)}, u32[]{:S(2)}) %collective-permute-start.1) | collective-permute-done | bytes 8224 | tf_op jit(solution)/shard_map/ppermute | solution.py:391
  39.9 0.9 pad_maximum_fusion.1.own_ref
  40.9 1.3 collective-permute-start.3
  42.2 4.0 %collective-permute-start.2 = (bf16[68,8,128]{2,1,0:T(8,128)(2,1)S(1)}, bf16[68,8,128]{2,1,0:T(8,128)(2,1)S(1)}, u32[]{:S(2)}, u32[]{:S(2)}) collective-permute-start(bf16[68,8,128]{2,1,0:T(8,128)(2,1)S(1)} %pad_maximum_fusion.1.own_ref), channel_id=1, source_target_pairs={{0,1},{1,2},{2,3},{3,4},{4,5},{5,6},{6,7},{7,8},{8,9},{9,10},{10,1... | collective-permute-start | bytes 417800 | tf_op jit(solution)/shard_map/ppermute | solution.py:391
  46.2 4.2 %shard_map.121 = (bf16[3,256,1152]{2,1,0:T(8,128)(2,1)}, bf16[384,768]{1,0:T(8,128)(2,1)}, bf16[3,1152,256]{2,1,0:T(8,128)(2,1)}, bf16[768,384]{1,0:T(8,128)(2,1...) custom-call(bf16[8,64,64]{2,1,0:T(8,128)(2,1)} %up_ref.1, bf16[27,64,64]{2,1,0:T(8,128)(2,1)} %one_ref.1, ...), custom_call_target="tpu_custom_call" | custom-call | tf_op jit(solution)/shard_map/pallas_call | solution.py:74
  51.8 11.0 %shard_map.122 = (bf16[134,8,256]{2,1,0:T(8,128)(2,1)}, bf16[132,8,128]{2,1,0:T(8,128)(2,1)}, bf16[132,8,128]{2,1,0:T(8,128)(2,1)}, f32[134,8,256]{2,1,0:T(8,128...) custom-call(bf16[68,8,128]{2,1,0:T(8,128)(2,1)} %copy-done.3, bf16[68,8,128]{2,1,0:T(8,128)(2,1)} %copy-done.9, ...), custom_call_target="tpu_custom_call" | custom-call | tf_op jit(solution)/shard_map/pallas_call | solution.py:74
  62.9 1.3 collective-permute-start.5
  64.1 4.2 %collective-permute-start.4 = (bf16[132,8,128]{2,1,0:T(8,128)(2,1)}, bf16[132,8,128]{2,1,0:T(8,128)(2,1)S(1)}, u32[]{:S(2)}, u32[]{:S(2)}) collective-permute-start(bf16[132,8,128]{2,1,0:T(8,128)(2,1)} %get-tuple-element.30.delta_ref.own_ref), channel_id=1, source_target_pairs={{0,1},{1,2},{2,3},{3,4},{4,5},{5,6},{6,7},{7,8},{8,9},{9,10},{10,1... | collective-permute-start | bytes 811016 | tf_op jit(solution)/shard_map/ppermute | solution.py:391
  68.3 3.3 %shard_map.123.two_ref = bf16[27,32,128]{2,1,0:T(8,128)(2,1)} custom-call(bf16[134,8,256]{2,1,0:T(8,128)(2,1)} %get-tuple-element.37.act_ref, bf16[132,8,128]{2,1,0:T(8,128)(2,1)} %get-tuple-element.30.delta_ref.own_ref), custom_call_target="tpu_custom_call" | custom-call | tf_op jit(solution)/shard_map/pallas_call | solution.py:74
  72.3 1.9 %collective-permute-done.4.left_ref = bf16[132,8,128]{2,1,0:T(8,128)(2,1)S(1)} collective-permute-done((bf16[132,8,128]{2,1,0:T(8,128)(2,1)}, bf16[132,8,128]{2,1,0:T(8,128)(2,1)S(1)}, u32[]{:S(2)}, u32[]{:S(2)}) %collective-permute-start.4) | collective-permute-done | bytes 270368 | tf_op jit(solution)/shard_map/ppermute | solution.py:391
  74.9 12.5 %shard_map.124 = bf16[128,24,128]{2,1,0:T(8,128)(2,1)} custom-call(bf16[132,8,128]{2,1,0:T(8,128)(2,1)} %get-tuple-element.30.delta_ref.own_ref, bf16[132,8,128]{2,1,0:T(8,128)(2,1)} %copy-done.5, bf16[132,8,128]{2,1,0:T(8,128)(2,1)} %copy-done.4, f32[134,8,256]{2,1,0:T(8,128)} %get-tuple-element.31.slope_ref, ...), custom_call_target="tpu_custom_call" | custom-call | tf_op jit(solution)/shard_map/pallas_call | solution.py:74
  87.4 27.1 %all_to_all.15.recv_ref = bf16[128,24,128]{2,1,0:T(8,128)(2,1)} all-to-all(bf16[128,24,128]{2,1,0:T(8,128)(2,1)} %shard_map.124), channel_id=1, replica_groups=mesh['gz'=8,'xy'=16] {'gz','xy'}, dimensions={0} | all-to-all | bytes 1572864 | tf_op jit(solution)/shard_map/all_to_all | solution.py:395
  114.5 2.1 %shard_map.126 = bf16[128,16,128]{2,1,0:T(8,128)(2,1)} custom-call(bf16[128,24,128]{2,1,0:T(8,128)(2,1)} %all_to_all.15.recv_ref), custom_call_target="tpu_custom_call" | custom-call | tf_op jit(solution)/shard_map/pallas_call | solution.py:74
  116.6 4.3 %all-to-all-start.2 = ((bf16[128,16,128]{2,1,0:T(8,128)(2,1)}), bf16[128,16,128]{2,1,0:T(8,128)(2,1)S(1)}, u32[]{:S(2)}, u32[]{:S(2)}) async-start(bf16[128,16,128]{2,1,0:T(8,128)(2,1)} %shard_map.126), calls=%async_computation.2 | async-start | bytes 1048576 | tf_op jit(solution)/shard_map/all_to_all | solution.py:395
  122.1 2.3 %shard_map.125 = bf16[1,64,2048]{2,1,0:T(8,128)(2,1)} custom-call(bf16[128,24,128]{2,1,0:T(8,128)(2,1)} %all_to_all.15.recv_ref), custom_call_target="tpu_custom_call" | custom-call | tf_op jit(solution)/shard_map/pallas_call | solution.py:74
  124.4 10.5 %all-to-all-done.2.recv_ref = bf16[128,16,128]{2,1,0:T(8,128)(2,1)S(1)} async-done(((bf16[128,16,128]{2,1,0:T(8,128)(2,1)}), bf16[128,16,128]{2,1,0:T(8,128)(2,1)S(1)}, u32[]{:S(2)}, u32[]{:S(2)}) %all-to-all-start.2) | async-done | bytes 524320 | tf_op jit(solution)/shard_map/all_to_all | solution.py:395
  135.7 2.5 %shard_map.127 = (f32[27,64,64]{2,1,0:T(8,128)}, f32[27,64,64]{2,1,0:T(8,128)}, f32[8,64,64]{2,1,0:T(8,128)}) custom-call(bf16[128,16,128]{2,1,0:T(8,128)(2,1)} %copy-done.2), custom_call_target="tpu_custom_call" | custom-call | tf_op jit(solution)/shard_map/pallas_call | solution.py:74
  (31 shorter events, 5.6 us)
Async XLA Ops:
  0.6 13.9 %copy-start.6 = (bf16[64,2,8,128]{3,2,1,0:T(8,128)(2,1)S(1)}, bf16[64,2,8,128]{3,2,1,0:T(8,128)(2,1)}, u32[]{:S(2)}) copy-start(bf16[64,2,8,128]{3,2,1,0:T(8,128)(2,1)} %param.15) | copy-start | bytes 786436
  3.0 25.3 %all-to-all-start = ((bf16[128,16,128]{2,1,0:T(8,128)(2,1)}), bf16[128,16,128]{2,1,0:T(8,128)(2,1)S(1)}, u32[]{:S(2)}, u32[]{:S(2)}) async-start(bf16[128,16,128]{2,1,0:T(8,128)(2,1)} %shard_map.119), calls=%async_computation | async-start | bytes 1048576 | tf_op jit(solution)/shard_map/all_to_all | solution.py:395
  15.5 34.9 %copy-start.1 = (bf16[128,8,128]{2,1,0:T(8,128)(2,1)S(1)}, bf16[128,8,128]{2,1,0:T(8,128)(2,1)}, u32[]{:S(2)}) copy-start(bf16[128,8,128]{2,1,0:T(8,128)(2,1)} %copy.16.cot_ref) | copy-start | bytes 786436
  28.4 0.8 copy-start
  31.8 4.9 %collective-permute-start = (bf16[4,8,128]{2,1,0:T(8,128)(2,1)}, bf16[4,8,128]{2,1,0:T(8,128)(2,1)S(1)}, u32[]{:S(2)}, u32[]{:S(2)}) collective-permute-start(bf16[4,8,128]{2,1,0:T(8,128)(2,1)} %get-tuple-element.23), channel_id=1, source_target_pairs={{0,16},{16,32},{32,48},{48,64},{64,80},{80,96},{96,112},{1,17},{17... | collective-permute-start | bytes 24584 | tf_op jit(solution)/shard_map/ppermute | solution.py:391
  34.7 5.2 %collective-permute-start.1 = (bf16[4,8,128]{2,1,0:T(8,128)(2,1)}, bf16[4,8,128]{2,1,0:T(8,128)(2,1)S(1)}, u32[]{:S(2)}, u32[]{:S(2)}) collective-permute-start(bf16[4,8,128]{2,1,0:T(8,128)(2,1)} %get-tuple-element.25), channel_id=1, source_target_pairs={{16,0},{32,16},{48,32},{64,48},{80,64},{96,80},{112,96},{17,1},{33... | collective-permute-start | bytes 24584 | tf_op jit(solution)/shard_map/ppermute | solution.py:391
  40.9 10.3 %copy-start.3 = (bf16[68,8,128]{2,1,0:T(8,128)(2,1)}, bf16[68,8,128]{2,1,0:T(8,128)(2,1)S(1)}, u32[]{:S(2)}) copy-start(bf16[68,8,128]{2,1,0:T(8,128)(2,1)S(1)} %pad_maximum_fusion.1.own_ref) | copy-start | bytes 417796
  40.9 10.2 %collective-permute-start.3 = (bf16[68,8,128]{2,1,0:T(8,128)(2,1)S(1)}, bf16[68,8,128]{2,1,0:T(8,128)(2,1)S(1)}, u32[]{:S(2)}, u32[]{:S(2)}) collective-permute-start(bf16[68,8,128]{2,1,0:T(8,128)(2,1)S(1)} %pad_maximum_fusion.1.own_ref), channel_id=1, source_target_pairs={{1,0},{2,1},{3,2},{4,3},{5,4},{6,5},{7,6},{8,7},{9,8},{10,9},{11,1... | collective-permute-start | bytes 417800 | tf_op jit(solution)/shard_map/ppermute | solution.py:391
  42.2 8.9 %collective-permute-start.2 = (bf16[68,8,128]{2,1,0:T(8,128)(2,1)S(1)}, bf16[68,8,128]{2,1,0:T(8,128)(2,1)S(1)}, u32[]{:S(2)}, u32[]{:S(2)}) collective-permute-start(bf16[68,8,128]{2,1,0:T(8,128)(2,1)S(1)} %pad_maximum_fusion.1.own_ref), channel_id=1, source_target_pairs={{0,1},{1,2},{2,3},{3,4},{4,5},{5,6},{6,7},{7,8},{8,9},{9,10},{10,1... | collective-permute-start | bytes 417800 | tf_op jit(solution)/shard_map/ppermute | solution.py:391
  51.1 0.7 copy-start.8
  51.1 0.7 copy-start.9
  62.9 9.4 %collective-permute-start.5 = (bf16[132,8,128]{2,1,0:T(8,128)(2,1)}, bf16[132,8,128]{2,1,0:T(8,128)(2,1)S(1)}, u32[]{:S(2)}, u32[]{:S(2)}) collective-permute-start(bf16[132,8,128]{2,1,0:T(8,128)(2,1)} %get-tuple-element.30.delta_ref.own_ref), channel_id=1, source_target_pairs={{1,0},{2,1},{3,2},{4,3},{5,4},{6,5},{7,6},{8,7},{9,8},{10,9},{11,1... | collective-permute-start | bytes 811016 | tf_op jit(solution)/shard_map/ppermute | solution.py:391
  64.1 10.0 %collective-permute-start.4 = (bf16[132,8,128]{2,1,0:T(8,128)(2,1)}, bf16[132,8,128]{2,1,0:T(8,128)(2,1)S(1)}, u32[]{:S(2)}, u32[]{:S(2)}) collective-permute-start(bf16[132,8,128]{2,1,0:T(8,128)(2,1)} %get-tuple-element.30.delta_ref.own_ref), channel_id=1, source_target_pairs={{0,1},{1,2},{2,3},{3,4},{4,5},{5,6},{6,7},{7,8},{8,9},{9,10},{10,1... | collective-permute-start | bytes 811016 | tf_op jit(solution)/shard_map/ppermute | solution.py:391
  72.3 1.9 %copy-start.4 = (bf16[132,8,128]{2,1,0:T(8,128)(2,1)}, bf16[132,8,128]{2,1,0:T(8,128)(2,1)S(1)}, u32[]{:S(2)}) copy-start(bf16[132,8,128]{2,1,0:T(8,128)(2,1)S(1)} %collective-permute-done.5.right_ref) | copy-start | bytes 811012
  74.1 0.7 copy-start.5
  87.4 33.5 %copy-start.7 = (bf16[132,8,128]{2,1,0:T(8,128)(2,1)S(1)}, bf16[132,8,128]{2,1,0:T(8,128)(2,1)}, u32[]{:S(2)}) copy-start(bf16[132,8,128]{2,1,0:T(8,128)(2,1)} %get-tuple-element.29) | copy-start | bytes 811012
  116.6 18.3 %all-to-all-start.2 = ((bf16[128,16,128]{2,1,0:T(8,128)(2,1)}), bf16[128,16,128]{2,1,0:T(8,128)(2,1)S(1)}, u32[]{:S(2)}, u32[]{:S(2)}) async-start(bf16[128,16,128]{2,1,0:T(8,128)(2,1)} %shard_map.126), calls=%async_computation.2 | async-start | bytes 1048576 | tf_op jit(solution)/shard_map/all_to_all | solution.py:395
  134.9 0.8 copy-start.2

commit v2 on v1

--- a/solution.py
+++ b/solution.py
@@ -15,6 +15,7 @@
 Z = 128
 Y = 8
 K = 64
+KZ = K + 4
 DEV = 128
 NO_CELL = 256.0
 STEP = 8
@@ -65,12 +66,18 @@
     return wide.reshape(count * rows, 3 * lanes).astype(BF)
 
 
-def call(kernel, outs, scratch=(), limit=58 << 20):
+def call(kernel, outs, scratch=(), home=False, raw=False, limit=22 << 20):
     single = isinstance(outs, tuple)
-    shapes = [jax.ShapeDtypeStruct(s, d) for s, d in ([outs] if single else outs)]
+    listed = [outs] if single else outs
+    home = home if isinstance(home, tuple) else (home,) * len(listed)
+    shapes = [
+        jax.ShapeDtypeStruct(s, d) if h else pltpu.VMEM(s, d) for (s, d), h in zip(listed, home)
+    ]
     vmem = pl.BlockSpec(memory_space=pltpu.VMEM)
 
     def run(*args):
+        if not raw:
+            args = [pltpu.with_memory_space_constraint(a, pltpu.VMEM) for a in args]
         got = pl.pallas_call(
             kernel,
             out_shape=shapes,
@@ -84,33 +91,60 @@
     return run
 
 
-def weights_kernel(up_ref, one_ref, two_ref, w1_ref, w2_ref, b1_ref, b0_ref, u_ref, ud_ref):
+def dot_rows(dot, rows_ref, weights, put):
+    total = rows_ref.shape[0]
+    half = (total // 2 + 15) // 16 * 16
+    for start, stop in ((0, half), (half, total)):
+        got = dot(rows_ref[start:stop], weights)
+        put(slice(start // Y, stop // Y), got.reshape((stop - start) // Y, Y, got.shape[1]))
+
+
+def tap(ref, ox, oy, oz):
+    if abs(ox) > 1:
+        return jnp.zeros((C, C), BF)
+    return ref[9 * (ox + 1) + 3 * (oy + 1) + oz + 1]
+
+
+def join(a, b):
+    return jnp.concatenate([a, b], axis=1)
+
+
+def forward_weights(up_ref, one_ref, two_ref, w1o_ref, w1x_ref, w2_ref, u_ref):
     zero = jnp.zeros((C, C), BF)
-
-    def tap(ref, ox, oy, oz):
-        return zero if abs(ox) > 1 else ref[9 * (ox + 1) + 3 * (oy + 1) + oz + 1]
-
-    def join(a, b):
-        return jnp.concatenate([a, b], axis=1)
-
     for oz in (-1, 0, 1):
         for oy in (-1, 0, 1):
             for n, xo in enumerate((0, 1, 2, -1)):
                 rows = slice(n * C, n * C + C)
                 for p in range(3):
-                    at = (oy + 1) * 384 + p * 128
+                    ref, at = w1o_ref, (oy + 1) * 128
+                    if p:
+                        ref, at = w1x_ref, (oy + 1) * 256 + p * 128 - 128
                     pair = [tap(one_ref, XK[2 * p + s] - xo, oy, oz) for s in (0, 1)]
-                    w1_ref[oz + 1, rows, at : at + 128] = join(*pair)
+                    ref[oz + 1, rows, at : at + 128] = join(*pair)
             for n, xo in enumerate((0, 1)):
                 at_row = (oz + 1) * 128 + n * C
                 for p in range(2):
                     at = (oy + 1) * 256 + p * 128
                     pair = [tap(two_ref, XK[2 * p + s] - xo, oy, oz) for s in (0, 1)]
                     w2_ref[at_row : at_row + C, at : at + 128] = join(*pair)
+    for e in (0, 1):
+        for a in (0, 1):
+            for b in (0, 1):
+                at = (e * 4 + b * 2 + a) * C
+                u_ref[at : at + C, :] = join(up_ref[4 * a + 2 * b + e], zero)
+            at = 512 + (e * 2 + a) * C
+            u_ref[at : at + C, :] = ones_where(iota((C, 128), 1) == C + 2 * a + e)
+
+
+def backward_weights(up_ref, one_ref, two_ref, b1o_ref, b1x_ref, b0_ref, ud_ref):
+    for oz in (-1, 0, 1):
+        for oy in (-1, 0, 1):
             for kk, xk in enumerate(XK):
-                at_row = (oy + 1) * 384 + kk * C
+                ref, at_row = b1x_ref, (oy + 1) * 256 + kk * C - 128
+                if kk < 2:
+                    ref, at_row = b1o_ref, (oy + 1) * 128 + kk * C
                 for p, pair in enumerate(((0, 1), (2, -1))):
-                    b1_ref[oz + 1, at_row : at_row + C, p * 128 : p * 128 + 128] = join(
+                    ref[oz + 1, at_row : at_row + C, p * 128 : p * 128 + 128] = join(
                         *[tap(two_ref, xo - xk, -oy, -oz) for xo in pair]
                     )
             for kk, xk in enumerate(XK[:4]):
@@ -120,13 +154,7 @@
                     *[tap(one_ref, xo - xk, -oy, -oz) for xo in (0, 1)]
                 )
     for e in (0, 1):
-        for b in (0, 1):
-            for a in (0, 1):
-                at = (e * 4 + b * 2 + a) * C
-                u_ref[at : at + C, :] = join(up_ref[4 * a + 2 * b + e], zero)
         for a in (0, 1):
-            at = 512 + (e * 2 + a) * C
-            u_ref[at : at + C, :] = ones_where(iota((C, 128), 1) == C + 2 * a + e)
             ud_ref[e, a * C : a * C + C, :] = join(up_ref[4 * a + e], up_ref[4 * a + 2 + e])
 
 
@@ -181,36 +209,69 @@
     return own, jnp.where(low, right, left), jnp.where(low, left, right)
 
 
+def lift_tile(rec_ref, u_ref, lift, seen):
+    kz = rec_ref.shape[0]
+    rec = rec_ref[...].astype(F32).reshape(kz * Y, 128).astype(BF)
+    odd_row = (iota((kz, Y, 128), 1) & 1) == 1
+    for e in (0, 1):
+        both = nt(rec, u_ref[e * 256 : e * 256 + 256, :]).reshape(kz, Y, 256)
+        live = nt(rec, u_ref[512 + e * 128 : 640 + e * 128, :]).reshape(kz, Y, 128)
+        lift[:, e] = live * jnp.where(odd_row, both[:, :, 128:], both[:, :, :128])
+        seen[:, e] = live
+
+
+def own_kernel(
+    rec_ref, up_ref, one_ref, two_ref, lift, seen, part, u_ref, w1x_ref, w2_ref, w1o_ref, col
+):
+    forward_weights(up_ref, one_ref, two_ref, w1o_ref, w1x_ref, w2_ref, u_ref)
+    lift_tile(rec_ref, u_ref, lift, seen)
+
+    def columns(k0, n):
+        own = lift[pl.ds(k0, n)].reshape(2 * n, Y, 128)
+        col[pl.ds(pl.multiple_of(k0 * 16, 16), 16 * n), :] = stack_y(own)
+
+    over(KZ, columns, 4)
+    for s in range(3):
+
+        def keep(at, value, s=s):
+            part[s, at] = value
+
+        dot_rows(nt, col, w1o_ref[s], keep)
+
+
 def forward_kernel(
-    own_ref, left_ref, right_ref, cot_ref, u_ref, w1_ref, w2_ref,
+    left_ref, right_ref, before_ref, after_ref, cot_in_ref,
+    lift_own, seen_own, part_own, u_ref, w1x_ref, w2_ref,
     act_ref, delta_ref, dec_ref, slope_ref, lifted_ref, keep_ref,
-    lift, seen, mask, col1, part1, col2, part2,
+    lift, seen, mask, col1, part1, col2, part2, cot_ref,
 ):
-    kz = own_ref.shape[0]
-    odd_row = (iota((kz, Y, 128), 1) & 1) == 1
-    for t, ref in enumerate((own_ref, left_ref, right_ref)):
-        rec = ref[...].astype(F32).reshape(kz * Y, 128).astype(BF)
-        for e in (0, 1):
-            both = nt(rec, u_ref[e * 256 : e * 256 + 256, :]).reshape(kz, Y, 256)
-            live = nt(rec, u_ref[512 + e * 128 : 640 + e * 128, :]).reshape(kz, Y, 128)
-            lift[t, :, e] = live * jnp.where(odd_row, both[:, :, 128:], both[:, :, :128])
-            seen[t, :, e] = live
+    kz = KZ
+    cot_ref[0:2] = before_ref[2:4]
+    cot_ref[2 : 2 + Z] = cot_in_ref[...]
+    cot_ref[2 + Z : 4 + Z] = after_ref[2:4]
+    for t, ref in enumerate((left_ref, right_ref)):
+        lift_tile(ref, u_ref, lift.at[t], seen.at[t])
 
     def columns(k0, n):
-        def load(ref):
-            return lane_groups(*[ref[t, pl.ds(k0, n)].reshape(2 * n, Y, 128) for t in range(3)])
-
-        own, near, far = load(lift)
+        def load(own_ref, ref):
+            three = [own_ref[pl.ds(k0, n)], ref[0, pl.ds(k0, n)], ref[1, pl.ds(k0, n)]]
+            return lane_groups(*[v.reshape(2 * n, Y, 128) for v in three])
+
+        own, near, far = load(lift_own, lift)
         at = pl.ds(2 * k0, 2 * n)
         lifted_ref[at] = jnp.concatenate([own, near], axis=2).astype(BF)
         rows = pl.ds(pl.multiple_of(k0 * 16, 16), 16 * n)
-        col1[rows, :] = stack_y(jnp.concatenate([own, near, far], axis=2))
-        live_own, live_near, _ = load(seen)
+        col1[rows, :] = stack_y(jnp.concatenate([near, far], axis=2))
+        live_own, live_near, _ = load(seen_own, seen)
         mask[at] = jnp.concatenate([live_own, live_near], axis=2)
 
     over(kz, columns, 4)
     for s in range(3):
-        part1[s] = nt(col1[...], w1_ref[s]).reshape(2 * kz, Y, 256)
+
+        def keep1(at, value, s=s):
+            part1[s, at] = part_own[s, at] + value
+
+        dot_rows(nt, col1, w1x_ref[s], keep1)
 
     def first(m, n):
         pre = part1[0, pl.ds(m, n)] + part1[1, pl.ds(m + 1, n)] + part1[2, pl.ds(m + 2, n)]
@@ -222,7 +283,11 @@
         col2[pl.ds(pl.multiple_of(m * Y, 16), n * Y), :] = stack_y(act)
 
     over(2 * kz - 2, first)
-    part2[...] = nt(col2[...], w2_ref[...]).reshape(2 * kz - 2, Y, 384)
+
+    def keep2(at, value):
+        part2[at] = value
+
+    dot_rows(nt, col2, w2_ref[...], keep2)
 
     def second(q, n):
         pre = (
@@ -241,12 +306,12 @@
     over(2 * kz - 4, second)
 
 
-def wgrad(count, field, padded, shifted, col):
+def wgrad(count, also, padded, shifted, col):
     def build(m, n):
         three = [padded[pl.ds(m + s, n)] for s in (2, 1, 0)]
         rows = pl.ds(pl.multiple_of(m * Y, 16), n * Y)
         shifted[rows, :] = jnp.concatenate(three, axis=2).reshape(n * Y, 384).astype(BF)
-        col[rows, :] = stack_y(field(m, n))
+        also(rows, m, n)
 
     over(count, build)
     return tn(shifted[...], col[...])
@@ -269,11 +334,34 @@
                 put(9 * (ox + 1) + 3 * (oy + 1) + oz + 1, packed(sums[0] + sums[1]))
 
 
-def second_grad_kernel(act_ref, delta_ref, out_ref, padded, shifted, col, total):
+def second_grad_kernel(
+    act_ref, delta_ref, recv_ref, lifted_ref, dec_ref, up_ref, one_ref, two_ref,
+    out_ref, hot_ref, part_ref, lifted_col, dec_out, b1x_ref, b0_ref, ud_ref,
+    b1o_ref, padded, shifted, col, total, col3,
+):
+    hot_ref[...] = jnp.concatenate(onehots(recv_ref), axis=1)
+    dec_out[...] = dec_ref[2 : 2 + Z]
+    backward_weights(up_ref, one_ref, two_ref, b1o_ref, b1x_ref, b0_ref, ud_ref)
+
+    def columns(q, n):
+        rows = pl.ds(pl.multiple_of(q * Y, 16), n * Y)
+        col3[rows, :] = stack_y(delta_ref[pl.ds(q, n)].astype(F32))
+        lifted_col[rows, :] = stack_y(lifted_ref[pl.ds(q + 2, n)].astype(F32))
+
+    over(132, columns)
+    for s in range(3):
+
+        def keep(at, value, s=s):
+            part_ref[s, at] = value
+
+        dot_rows(nn, col3, b1o_ref[s], keep)
     padded[0:4] = jnp.zeros((4, Y, 128), F32)
     padded[132:136] = jnp.zeros((4, Y, 128), F32)
     padded[4:132] = delta_ref[2:130].astype(F32)
-    total[...] = wgrad(134, lambda m, n: act_ref[pl.ds(m, n)].astype(F32), padded, shifted, col)
+    def act_col(rows, m, n):
+        col[rows, :] = stack_y(act_ref[pl.ds(m, n)].astype(F32))
+
+    total[...] = wgrad(134, act_col, padded, shifted, col)
 
     def put(t, block):
         out_ref[t] = block
@@ -282,19 +370,24 @@
 
 
 def backward_kernel(
-    own_ref, left_ref, right_ref, slope_ref, keep_ref, lifted_ref, rec_ref, recv_ref,
-    b1_ref, b0_ref, ud_ref, two_ref, out_ref,
-    col3, part3, col4, part4, padded, shifted, col, total, du,
+    left_ref, right_ref, slope_ref, keep_ref, rec_ref, hot_ref, part_own, lifted_col, two_ref,
+    b1x_ref, b0_ref, ud_ref, out_ref,
+    col3, part3, col4, part4, padded, shifted, total, du,
 ):
     def columns(q, n):
         at = pl.ds(q, n)
-        groups = lane_groups(*[r[at].astype(F32) for r in (own_ref, left_ref, right_ref)])
+        left, right = left_ref[at].astype(F32), right_ref[at].astype(F32)
+        groups = lane_groups(left, left, right)[1:]
         rows = pl.ds(pl.multiple_of(q * Y, 16), n * Y)
         col3[rows, :] = stack_y(jnp.concatenate(groups, axis=2))
 
     over(132, columns)
     for s in range(3):
-        part3[s] = nn(col3[...], b1_ref[s]).reshape(132, Y, 256)
+
+        def keep3(at, value, s=s):
+            part3[s, at] = part_own[s, at] + value
+
+        dot_rows(nn, col3, b1x_ref[s], keep3)
 
     def first(r, n):
         back = part3[0, pl.ds(r, n)] + part3[1, pl.ds(r + 1, n)] + part3[2, pl.ds(r + 2, n)]
@@ -305,7 +398,11 @@
     over(130, first)
     padded[0:3] = jnp.zeros((3, Y, 128), F32)
     padded[131:134] = jnp.zeros((3, Y, 128), F32)
-    part4[...] = nn(col4[...], b0_ref[...]).reshape(130, Y, 384)
+
+    def keep4(at, value):
+        part4[at] = value
+
+    dot_rows(nn, col4, b0_ref[...], keep4)
 
     def upper(z, n):
         back = (
@@ -328,9 +425,10 @@
     parent = summed.reshape(K * Y, 128).astype(BF)
     cell, src = iota((256, 512), 0), iota((256, 512), 1)
     pick = ones_where(src == (cell & (K - 1)) * Y + 2 * (cell >> 6))
-    parent = nn(pick, parent).astype(BF)
-    slots = [nn(hot, parent) for hot in onehots(recv_ref)]
-    slots = jnp.where(iota((1024, 128), 1) < C, slots[0], slots[1])
+    parent = nn(pick, parent)
+    low = low_lanes(parent.shape)
+    sides = [jnp.where(low, parent, 0.0), jnp.where(low, 0.0, parent)]
+    slots = nn(hot_ref[...], jnp.concatenate(sides, axis=0).astype(BF))
     out_ref[:, 0:8, :] = slots.reshape(DEV, 8, 128).astype(BF)
 
     def put(index, block):
@@ -346,9 +444,7 @@
             for b in (0, 1):
                 block = up_grad[a * C : a * C + C, b * C : b * C + C]
                 put(54 + 4 * a + 2 * b + e, packed(block))
-    total[...] = wgrad(
-        132, lambda m, n: lifted_ref[pl.ds(m + 2, n)].astype(F32), padded, shifted, col
-    )
+    total[...] = wgrad(132, lambda *_: None, padded, shifted, lifted_col)
     tap_grads(total, lambda t, block: put(27 + t, block))
     for t in range(27):
         put(t, two_ref[t])
@@ -401,26 +497,26 @@
     size_x, size_y, size_z = cotangent.shape[1:]
     voxels = size_x * size_y * size_z * lax.axis_size("xy") * lax.axis_size("gz")
     scale = 1.0 / math.sqrt(voxels)
-    kz = K + 4
-
-    sent = call(send_kernel, ((DEV, 16, 128), BF))(parent_feat, parent_cell, send_count)
+    sent = call(send_kernel, ((DEV, 16, 128), BF), raw=True, home=True, limit=58 << 20)(
+        parent_feat, parent_cell, send_count
+    )
     recv = exchange(sent)
     cot = cotangent.transpose(3, 2, 1, 0).reshape(Z, Y, 128)
-    w1, w2, b1, b0, u, ud = call(
-        weights_kernel,
-        [
-            ((3, 256, 1152), BF), ((384, 768), BF), ((3, 1152, 256), BF), ((768, 384), BF),
-            ((768, 128), BF), ((2, 128, 128), BF),
-        ],
-    )(up_weight, conv_one, conv_two)
     rec, up_edge, down_edge = call(
         grid_kernel, [((K, Y, 128), BF), ((4, Y, 128), BF), ((4, Y, 128), BF)]
     )(recv, child_mask, cot)
-    before = shift(up_edge, "gz", 1)
-    after = shift(down_edge, "gz", -1)
+    before, after = shift(up_edge, "gz", 1), shift(down_edge, "gz", -1)
     rec_ext = jnp.concatenate([before[0:2], rec, after[0:2]], axis=0)
-    cot_ext = jnp.concatenate([before[2:4], cot, after[2:4]], axis=0)
-    rec_left, rec_right = shift(rec_ext, "xy", 1), shift(rec_ext, "xy", -1)
+    left, right = shift(rec_ext, "xy", 1), shift(rec_ext, "xy", -1)
+    weights = up_weight, conv_one, conv_two
+    lift_own, seen_own, part_own, u, w1x, w2 = call(
+        own_kernel,
+        [
+            ((KZ, 2, Y, 128), F32), ((KZ, 2, Y, 128), F32), ((3, 136, Y, 256), F32),
+            ((768, 128), BF), ((3, 256, 768), BF), ((384, 768), BF),
+        ],
+        [((3, 256, 384), BF), ((1088, 384), BF)],
+    )(rec_ext, *weights)
     act, delta, dec, slope, lifted, keep = call(
         forward_kernel,
         [
@@ -428,34 +524,41 @@
             ((134, Y, 256), F32), ((136, Y, 256), BF), ((132, Y, 128), BF),
         ],
         [
-            ((3, kz, 2, Y, 128), F32), ((3, kz, 2, Y, 128), F32), ((136, Y, 256), F32),
-            ((1088, 1152), BF), ((3, 136, Y, 256), F32), ((1072, 768), BF), ((134, Y, 384), F32),
+            ((2, KZ, 2, Y, 128), F32), ((2, KZ, 2, Y, 128), F32), ((136, Y, 256), F32),
+            ((1088, 768), BF), ((3, 136, Y, 256), F32), ((1072, 768), BF), ((134, Y, 384), F32),
+            ((132, Y, 128), BF),
         ],
-    )(rec_ext, rec_left, rec_right, cot_ext, u, w1, w2)
+    )(left, right, before, after, cot, lift_own, seen_own, part_own, u, w1x, w2)
     delta_left, delta_right = shift(delta, "xy", 1), shift(delta, "xy", -1)
-    two = call(
+    two, hot, part_back, lifted_col, dec, b1x, b0, ud = call(
         second_grad_kernel,
-        ((27, 32, 128), BF),
-        [((136, Y, 128), F32), ((1072, 384), BF), ((1072, 768), BF), ((384, 768), F32)],
-    )(act, delta)
-    decoded = dec[2 : 2 + Z].reshape(Z, Y, 2, C).transpose(3, 2, 1, 0)
+        [
+            ((27, 32, 128), BF), ((1024, 512), BF), ((3, 132, Y, 256), F32), ((1056, 768), BF),
+            ((Z, Y, 128), BF), ((3, 768, 256), BF), ((768, 384), BF), ((2, 128, 128), BF),
+        ],
+        [
+            ((3, 384, 256), BF), ((136, Y, 128), F32), ((1072, 384), BF), ((1072, 768), BF), ((384, 768), F32),
+            ((1056, 384), BF),
+        ],
+        home=(False, False, False, False, True, False, False, False),
+    )(act, delta, recv, lifted, dec, *weights)
+    decoded = dec.reshape(Z, Y, 2, C).transpose(3, 2, 1, 0)
     message = call(
         backward_kernel,
         ((DEV, 24, 128), BF),
         [
-            ((1056, 1152), BF), ((3, 132, Y, 256), F32), ((1040, 768), BF), ((130, Y, 384), F32),
-            ((134, Y, 128), F32), ((1056, 384), BF), ((1056, 768), BF), ((384, 768), F32),
-            ((K, 2, Y, 128), F32),
+            ((1056, 768), BF), ((3, 132, Y, 256), F32), ((1040, 768), BF), ((130, Y, 384), F32),
+            ((134, Y, 128), F32), ((1056, 384), BF), ((384, 768), F32), ((K, 2, Y, 128), F32),
         ],
     )(
-        delta, delta_left, delta_right, slope, keep, lifted, rec, recv, b1, b0, ud, two
+        delta_left, delta_right, slope, keep, rec, hot, part_back, lifted_col, two, b1x, b0, ud
     )
     back = exchange(message)
     total = call(functools.partial(sum_kernel, scale=scale), ((DEV, 16, 128), BF))(back)
     gathered = exchange(total)
-    grad_parent = call(slot_kernel, ((1, C, 2048), BF))(back)
+    grad_parent = call(slot_kernel, ((1, C, 2048), BF), home=True)(back)
     grad_one, grad_two, grad_up = call(
-        unpack_kernel, [((27, C, C), F32), ((27, C, C), F32), ((8, C, C), F32)]
+        unpack_kernel, [((27, C, C), F32), ((27, C, C), F32), ((8, C, C), F32)], home=True
     )(gathered)
     return decoded, grad_parent, grad_one, grad_two, grad_up
 

time: 139 us -> 117 us (0.84)
  Pallas kernels: 43.1 us -> 23.5 us
  waiting for transfers between devices: 29.1 us -> 36.1 us
  starting transfers between devices: 31.4 us -> 27.5 us
  local copies, waits for them, and re-layouts: 5.11 us -> 1.39 us
  other arithmetic: 1.66 us -> 0.02 us
    pallas_call x9, Pallas kernels: 43.1 us -> 23.5 us  [run(): pl.pallas_call(kernel, out_shape=shapes, in_specs=[vmem] * len(args), out...]
    ppermute x6, waiting for transfers between devices: 5.72 us -> 10.8 us  [shift(): return lax.ppermute(array, axis, pairs)]
    ppermute x6, starting transfers between devices: 15.6 us -> 11.7 us  [shift(): return lax.ppermute(array, axis, pairs)]
    unnamed x22 -> x12, local copies, waits for them, and re-layouts: 3.98 us -> 0.97 us
    all_to_all x2, waiting for transfers between devices: 23.4 us -> 25.3 us  [exchange(): return lax.all_to_all(array, ('gz', 'xy'), 0, 0, tiled=True)]
  transfers between devices with their start and end apart: 8 -> 8, of which waited for: 5 -> 6; matrix products, arithmetic and copies ran while one was open for 2% -> 1% of each run, Pallas kernels for 7% -> 6%
where the time goes in v2:
time: 117 us
  waiting for transfers between devices  36.1 us (31%)
  starting transfers between devices  27.5 us (24%)
  blocking collectives  27.5 us (24%)
  Pallas kernels  23.5 us (20%)
  local copies, waits for them, and re-layouts  1.39 us (1%)
    all_to_all x1, blocking collectives, exchange(): return lax.all_to_all(array, ('gz', 'xy'), 0, 0, tiled=True)  27.5 us
    all_to_all x2, waiting for transfers between devices, exchange(): return lax.all_to_all(array, ('gz', 'xy'), 0, 0, tiled=True)  25.3 us
    pallas_call x9, Pallas kernels, run(): pl.pallas_call(kernel, out_shape=shapes, in_specs=[vmem] * len(args), out...  23.5 us
    all_to_all x2, starting transfers between devices, exchange(): return lax.all_to_all(array, ('gz', 'xy'), 0, 0, tiled=True)  15.8 us
    ppermute x6, starting transfers between devices, shift(): return lax.ppermute(array, axis, pairs)  11.7 us
    ppermute x6, waiting for transfers between devices, shift(): return lax.ppermute(array, axis, pairs)  10.8 us
  transfers between devices with their start and end apart: 8, of which 6 were waited for; matrix products, arithmetic and copies ran while one was open for 1% of the time, Pallas kernels for 6%

profile of v2, /device:TPU:1, one launch (start us, length us, event | category | flops | bytes accessed | tf_op | source)
XLA Modules:
  0.0 116.8 jit_solution(3780047298150179231)
XLA Ops:
  0.7 2.4 %shard_map.119 = bf16[128,16,128]{2,1,0:T(8,128)(2,1)} custom-call(bf16[1,64,2048]{2,1,0:T(8,128)(2,1)} %feat_ref.1, s32[1,2048]{1,0:T(1,128)} %cell_ref.1, s32[1,128]{1,0:T(1,128)} %count_ref.1), custom_call_target="tpu_custom_call" | custom-call | tf_op jit(solution)/shard_map/pallas_call | solution.py:81
  3.1 11.5 %all-to-all-start = ((bf16[128,16,128]{2,1,0:T(8,128)(2,1)}), bf16[128,16,128]{2,1,0:T(8,128)(2,1)S(1)}, u32[]{:S(2)}, u32[]{:S(2)}) async-start(bf16[128,16,128]{2,1,0:T(8,128)(2,1)} %shard_map.119), calls=%async_computation | async-start | bytes 1048576 | tf_op jit(solution)/shard_map/all_to_all | solution.py:491
  14.8 13.6 %all-to-all-done.recv_ref = bf16[128,16,128]{2,1,0:T(8,128)(2,1)S(1)} async-done(((bf16[128,16,128]{2,1,0:T(8,128)(2,1)}), bf16[128,16,128]{2,1,0:T(8,128)(2,1)S(1)}, u32[]{:S(2)}, u32[]{:S(2)}) %all-to-all-start) | async-done | bytes 524320 | tf_op jit(solution)/shard_map/all_to_all | solution.py:491
  28.4 0.9 shard_map.120
  29.3 2.9 %collective-permute-start = (bf16[4,8,128]{2,1,0:T(8,128)(2,1)S(1)}, bf16[4,8,128]{2,1,0:T(8,128)(2,1)S(1)}, u32[]{:S(2)}, u32[]{:S(2)}) collective-permute-start(bf16[4,8,128]{2,1,0:T(8,128)(2,1)S(1)} %get-tuple-element.31), channel_id=1, source_target_pairs={{0,16},{16,32},{32,48},{48,64},{64,80},{80,96},{96,112},{1,17},{17... | collective-permute-start | bytes 24584 | tf_op jit(solution)/shard_map/ppermute | solution.py:487
  32.2 1.9 %collective-permute-start.1 = (bf16[4,8,128]{2,1,0:T(8,128)(2,1)S(1)}, bf16[4,8,128]{2,1,0:T(8,128)(2,1)S(1)}, u32[]{:S(2)}, u32[]{:S(2)}) collective-permute-start(bf16[4,8,128]{2,1,0:T(8,128)(2,1)S(1)} %get-tuple-element.33), channel_id=1, source_target_pairs={{16,0},{32,16},{48,32},{64,48},{80,64},{96,80},{112,96},{17,1},{33... | collective-permute-start | bytes 24584 | tf_op jit(solution)/shard_map/ppermute | solution.py:487
  34.1 3.0 %collective-permute-done.1.after_ref = bf16[4,8,128]{2,1,0:T(8,128)(2,1)S(1)} collective-permute-done((bf16[4,8,128]{2,1,0:T(8,128)(2,1)S(1)}, bf16[4,8,128]{2,1,0:T(8,128)(2,1)S(1)}, u32[]{:S(2)}, u32[]{:S(2)}) %collective-permute-start.1) | collective-permute-done | bytes 8224 | tf_op jit(solution)/shard_map/ppermute | solution.py:487
  37.2 2.5 %collective-permute-start.2 = (bf16[68,8,128]{2,1,0:T(8,128)(2,1)S(1)}, bf16[68,8,128]{2,1,0:T(8,128)(2,1)S(1)}, u32[]{:S(2)}, u32[]{:S(2)}) collective-permute-start(bf16[68,8,128]{2,1,0:T(8,128)(2,1)S(1)} %pad_maximum_fusion.rec_ref), channel_id=1, source_target_pairs={{0,1},{1,2},{2,3},{3,4},{4,5},{5,6},{6,7},{7,8},{8,9},{9,10},{10,1... | collective-permute-start | bytes 417800 | tf_op jit(solution)/shard_map/ppermute | solution.py:487
  39.7 1.3 %collective-permute-start.3 = (bf16[68,8,128]{2,1,0:T(8,128)(2,1)S(1)}, bf16[68,8,128]{2,1,0:T(8,128)(2,1)S(1)}, u32[]{:S(2)}, u32[]{:S(2)}) collective-permute-start(bf16[68,8,128]{2,1,0:T(8,128)(2,1)S(1)} %pad_maximum_fusion.rec_ref), channel_id=1, source_target_pairs={{1,0},{2,1},{3,2},{4,3},{5,4},{6,5},{7,6},{8,7},{9,8},{10,9},{11,1... | collective-permute-start | bytes 417800 | tf_op jit(solution)/shard_map/ppermute | solution.py:487
  41.0 1.8 %shard_map.121 = (f32[68,2,8,128]{3,2,1,0:T(8,128)S(1)}, f32[68,2,8,128]{3,2,1,0:T(8,128)S(1)}, f32[3,136,8,256]{3,2,1,0:T(8,128)S(1)}, bf16[768,128]{1,0:T(8,12...) custom-call(bf16[68,8,128]{2,1,0:T(8,128)(2,1)S(1)} %pad_maximum_fusion.rec_ref, ...), custom_call_target="tpu_custom_call" | custom-call | tf_op jit(solution)/shard_map/pallas_call | solution.py:81
  42.8 3.0 %collective-permute-done.3.right_ref = bf16[68,8,128]{2,1,0:T(8,128)(2,1)S(1)} collective-permute-done((bf16[68,8,128]{2,1,0:T(8,128)(2,1)S(1)}, bf16[68,8,128]{2,1,0:T(8,128)(2,1)S(1)}, u32[]{:S(2)}, u32[]{:S(2)}) %collective-permute-start.3) | collective-permute-done | bytes 139296 | tf_op jit(solution)/shard_map/ppermute | solution.py:487
  45.8 4.7 %shard_map.122 = (bf16[134,8,256]{2,1,0:T(8,128)(2,1)S(1)}, bf16[132,8,128]{2,1,0:T(8,128)(2,1)S(1)}, bf16[132,8,128]{2,1,0:T(8,128)(2,1)S(1)}, f32[134,8,256]{2...) custom-call(bf16[68,8,128]{2,1,0:T(8,128)(2,1)S(1)} %collective-permute-done.2.left_ref, ...), custom_call_target="tpu_custom_call" | custom-call | tf_op jit(solution)/shard_map/pallas_call | solution.py:81
  50.5 1.6 %collective-permute-start.4 = (bf16[132,8,128]{2,1,0:T(8,128)(2,1)S(1)}, bf16[132,8,128]{2,1,0:T(8,128)(2,1)S(1)}, u32[]{:S(2)}, u32[]{:S(2)}) collective-permute-start(bf16[132,8,128]{2,1,0:T(8,128)(2,1)S(1)} %get-tuple-element.41.delta_ref), channel_id=1, source_target_pairs={{0,1},{1,2},{2,3},{3,4},{4,5},{5,6},{6,7},{7,8},{8,9},{9,10},{10,1... | collective-permute-start | bytes 811016 | tf_op jit(solution)/shard_map/ppermute | solution.py:487
  52.2 1.5 %collective-permute-start.5 = (bf16[132,8,128]{2,1,0:T(8,128)(2,1)S(1)}, bf16[132,8,128]{2,1,0:T(8,128)(2,1)S(1)}, u32[]{:S(2)}, u32[]{:S(2)}) collective-permute-start(bf16[132,8,128]{2,1,0:T(8,128)(2,1)S(1)} %get-tuple-element.41.delta_ref), channel_id=1, source_target_pairs={{1,0},{2,1},{3,2},{4,3},{5,4},{6,5},{7,6},{8,7},{9,8},{10,9},{11,1... | collective-permute-start | bytes 811016 | tf_op jit(solution)/shard_map/ppermute | solution.py:487
  53.6 4.0 %shard_map.123 = (bf16[27,32,128]{2,1,0:T(8,128)(2,1)S(1)}, bf16[1024,512]{1,0:T(8,128)(2,1)S(1)}, f32[3,132,8,256]{3,2,1,0:T(8,128)S(1)}, bf16[1056,768]{1,0:T(...) custom-call(bf16[134,8,256]{2,1,0:T(8,128)(2,1)S(1)} %get-tuple-elem, ...), custom_call_target="tpu_custom_call" | custom-call | tf_op jit(solution)/shard_map/pallas_call | solution.py:81
  58.1 4.3 %collective-permute-done.5.right_ref = bf16[132,8,128]{2,1,0:T(8,128)(2,1)S(1)} collective-permute-done((bf16[132,8,128]{2,1,0:T(8,128)(2,1)S(1)}, bf16[132,8,128]{2,1,0:T(8,128)(2,1)S(1)}, u32[]{:S(2)}, u32[]{:S(2)}) %collective-permute-start.5) | collective-permute-done | bytes 270368 | tf_op jit(solution)/shard_map/ppermute | solution.py:487
  62.4 6.1 %shard_map.124 = bf16[128,24,128]{2,1,0:T(8,128)(2,1)S(1)} custom-call(bf16[132,8,128]{2,1,0:T(8,128)(2,1)S(1)} %collective-permute-done.4.left_ref, bf16[132,8,128]{2,1,0:T(8,128)(2,1)S(1)} %collective-permute-done.5.right_ref, f32[134,8,256]{2,1,0:T(8,128)S(1)} %get-tuple-element.45.slope_ref, bf16[132,8,128]{2,1,0:T(8,128)(2,1)S(1)} %get-tuple-element.46.keep_ref, ...), custom_call_target="tpu_custom_call" | custom-call | tf_op jit(solution)/shard_map/pallas_call | solution.py:81
  68.5 27.5 %all_to_all.15.recv_ref = bf16[128,24,128]{2,1,0:T(8,128)(2,1)S(1)} all-to-all(bf16[128,24,128]{2,1,0:T(8,128)(2,1)S(1)} %shard_map.124), channel_id=1, replica_groups=mesh['gz'=8,'xy'=16] {'gz','xy'}, dimensions={0} | all-to-all | bytes 1572864 | tf_op jit(solution)/shard_map/all_to_all | solution.py:491
  96.0 1.0 shard_map.126
  97.0 4.3 %all-to-all-start.2 = ((bf16[128,16,128]{2,1,0:T(8,128)(2,1)}), bf16[128,16,128]{2,1,0:T(8,128)(2,1)S(1)}, u32[]{:S(2)}, u32[]{:S(2)}) async-start(bf16[128,16,128]{2,1,0:T(8,128)(2,1)} %shard_map.126), calls=%async_computation.2 | async-start | bytes 1048576 | tf_op jit(solution)/shard_map/all_to_all | solution.py:491
  101.6 0.9 copy.19
  102.4 1.2 shard_map.125
  103.6 11.7 %all-to-all-done.2.recv_ref = bf16[128,16,128]{2,1,0:T(8,128)(2,1)S(1)} async-done(((bf16[128,16,128]{2,1,0:T(8,128)(2,1)}), bf16[128,16,128]{2,1,0:T(8,128)(2,1)S(1)}, u32[]{:S(2)}, u32[]{:S(2)}) %all-to-all-start.2) | async-done | bytes 524320 | tf_op jit(solution)/shard_map/all_to_all | solution.py:491
  115.3 1.5 %shard_map.127 = (f32[27,64,64]{2,1,0:T(8,128)}, f32[27,64,64]{2,1,0:T(8,128)}, f32[8,64,64]{2,1,0:T(8,128)}) custom-call(bf16[128,16,128]{2,1,0:T(8,128)(2,1)S(1)} %all-to-all-done.2.recv_ref), custom_call_target="tpu_custom_call" | custom-call | tf_op jit(solution)/shard_map/pallas_call | solution.py:81
  (19 shorter events, 1.0 us)
Async XLA Ops:
  0.6 13.9 %copy-start.4 = (bf16[64,2,8,128]{3,2,1,0:T(8,128)(2,1)S(1)}, bf16[64,2,8,128]{3,2,1,0:T(8,128)(2,1)}, u32[]{:S(2)}) copy-start(bf16[64,2,8,128]{3,2,1,0:T(8,128)(2,1)} %param.15) | copy-start | bytes 786436
  0.6 27.8 %copy-start.3 = (s32[2,8,128]{2,1,0:T(8,128)S(1)}, s32[2,8,128]{2,1,0:T(8,128)}, u32[]{:S(2)}) copy-start(s32[2,8,128]{2,1,0:T(8,128)} %mask_ref.1) | copy-start | bytes 24580
  3.0 37.9 %copy-start = (bf16[27,64,64]{2,1,0:T(8,128)(2,1)S(1)}, bf16[27,64,64]{2,1,0:T(8,128)(2,1)}, u32[]{:S(2)}) copy-start(bf16[27,64,64]{2,1,0:T(8,128)(2,1)} %one_ref.3) | copy-start | bytes 663556
  3.1 37.9 %copy-start.1 = (bf16[27,64,64]{2,1,0:T(8,128)(2,1)S(1)}, bf16[27,64,64]{2,1,0:T(8,128)(2,1)}, u32[]{:S(2)}) copy-start(bf16[27,64,64]{2,1,0:T(8,128)(2,1)} %two_ref.3) | copy-start | bytes 663556
  3.1 37.9 %copy-start.2 = (bf16[8,64,64]{2,1,0:T(8,128)(2,1)S(1)}, bf16[8,64,64]{2,1,0:T(8,128)(2,1)}, u32[]{:S(2)}) copy-start(bf16[8,64,64]{2,1,0:T(8,128)(2,1)} %up_ref.3) | copy-start | bytes 196612
  3.1 25.3 %all-to-all-start = ((bf16[128,16,128]{2,1,0:T(8,128)(2,1)}), bf16[128,16,128]{2,1,0:T(8,128)(2,1)S(1)}, u32[]{:S(2)}, u32[]{:S(2)}) async-start(bf16[128,16,128]{2,1,0:T(8,128)(2,1)} %shard_map.119), calls=%async_computation | async-start | bytes 1048576 | tf_op jit(solution)/shard_map/all_to_all | solution.py:491
  29.3 4.9 %collective-permute-start = (bf16[4,8,128]{2,1,0:T(8,128)(2,1)S(1)}, bf16[4,8,128]{2,1,0:T(8,128)(2,1)S(1)}, u32[]{:S(2)}, u32[]{:S(2)}) collective-permute-start(bf16[4,8,128]{2,1,0:T(8,128)(2,1)S(1)} %get-tuple-element.31), channel_id=1, source_target_pairs={{0,16},{16,32},{32,48},{48,64},{64,80},{80,96},{96,112},{1,17},{17... | collective-permute-start | bytes 24584 | tf_op jit(solution)/shard_map/ppermute | solution.py:487
  32.2 5.0 %collective-permute-start.1 = (bf16[4,8,128]{2,1,0:T(8,128)(2,1)S(1)}, bf16[4,8,128]{2,1,0:T(8,128)(2,1)S(1)}, u32[]{:S(2)}, u32[]{:S(2)}) collective-permute-start(bf16[4,8,128]{2,1,0:T(8,128)(2,1)S(1)} %get-tuple-element.33), channel_id=1, source_target_pairs={{16,0},{32,16},{48,32},{64,48},{80,64},{96,80},{112,96},{17,1},{33... | collective-permute-start | bytes 24584 | tf_op jit(solution)/shard_map/ppermute | solution.py:487
  37.2 5.6 %collective-permute-start.2 = (bf16[68,8,128]{2,1,0:T(8,128)(2,1)S(1)}, bf16[68,8,128]{2,1,0:T(8,128)(2,1)S(1)}, u32[]{:S(2)}, u32[]{:S(2)}) collective-permute-start(bf16[68,8,128]{2,1,0:T(8,128)(2,1)S(1)} %pad_maximum_fusion.rec_ref), channel_id=1, source_target_pairs={{0,1},{1,2},{2,3},{3,4},{4,5},{5,6},{6,7},{7,8},{8,9},{9,10},{10,1... | collective-permute-start | bytes 417800 | tf_op jit(solution)/shard_map/ppermute | solution.py:487
  39.7 6.1 %collective-permute-start.3 = (bf16[68,8,128]{2,1,0:T(8,128)(2,1)S(1)}, bf16[68,8,128]{2,1,0:T(8,128)(2,1)S(1)}, u32[]{:S(2)}, u32[]{:S(2)}) collective-permute-start(bf16[68,8,128]{2,1,0:T(8,128)(2,1)S(1)} %pad_maximum_fusion.rec_ref), channel_id=1, source_target_pairs={{1,0},{2,1},{3,2},{4,3},{5,4},{6,5},{7,6},{8,7},{9,8},{10,9},{11,1... | collective-permute-start | bytes 417800 | tf_op jit(solution)/shard_map/ppermute | solution.py:487
  50.5 7.6 %collective-permute-start.4 = (bf16[132,8,128]{2,1,0:T(8,128)(2,1)S(1)}, bf16[132,8,128]{2,1,0:T(8,128)(2,1)S(1)}, u32[]{:S(2)}, u32[]{:S(2)}) collective-permute-start(bf16[132,8,128]{2,1,0:T(8,128)(2,1)S(1)} %get-tuple-element.41.delta_ref), channel_id=1, source_target_pairs={{0,1},{1,2},{2,3},{3,4},{4,5},{5,6},{6,7},{7,8},{8,9},{9,10},{10,1... | collective-permute-start | bytes 811016 | tf_op jit(solution)/shard_map/ppermute | solution.py:487
  52.2 10.3 %collective-permute-start.5 = (bf16[132,8,128]{2,1,0:T(8,128)(2,1)S(1)}, bf16[132,8,128]{2,1,0:T(8,128)(2,1)S(1)}, u32[]{:S(2)}, u32[]{:S(2)}) collective-permute-start(bf16[132,8,128]{2,1,0:T(8,128)(2,1)S(1)} %get-tuple-element.41.delta_ref), channel_id=1, source_target_pairs={{1,0},{2,1},{3,2},{4,3},{5,4},{6,5},{7,6},{8,7},{9,8},{10,9},{11,1... | collective-permute-start | bytes 811016 | tf_op jit(solution)/shard_map/ppermute | solution.py:487
  97.0 18.3 %all-to-all-start.2 = ((bf16[128,16,128]{2,1,0:T(8,128)(2,1)}), bf16[128,16,128]{2,1,0:T(8,128)(2,1)S(1)}, u32[]{:S(2)}, u32[]{:S(2)}) async-start(bf16[128,16,128]{2,1,0:T(8,128)(2,1)} %shard_map.126), calls=%async_computation.2 | async-start | bytes 1048576 | tf_op jit(solution)/shard_map/all_to_all | solution.py:491

commit v3 on v2

--- a/solution.py
+++ b/solution.py
@@ -18,6 +18,7 @@
 KZ = K + 4
 DEV = 128
 NO_CELL = 256.0
+ROWS = 10
 STEP = 8
 
 
@@ -158,38 +159,58 @@
             ud_ref[e, a * C : a * C + C, :] = join(up_ref[4 * a + e], up_ref[4 * a + 2 + e])
 
 
-def send_kernel(feat_ref, cell_ref, count_ref, out_ref):
-    spread = ones_where((iota((DEV, 2048), 1) >> 4) == iota((DEV, 2048), 0))
-    count = jnp.broadcast_to(count_ref[...].astype(F32), (8, DEV)).astype(BF)
-    counts = nn(count, spread)[0:1]
-    slot = (iota((1, 2048), 1) & 15).astype(F32)
-    cell = jnp.where(slot < counts, cell_ref[...].astype(F32), NO_CELL)
+def send_kernel(feat_ref, cell_ref, count_ref, out_ref, rows_ref):
+    counts = jnp.broadcast_to(count_ref[...].astype(F32), (DEV, DEV)).T
+    lane = iota((8, 128), 1)
     for chunk in range(16):
         at = slice(chunk * 128, chunk * 128 + 128)
         feats = feat_ref[0, :, at].astype(F32)
-        cells = jnp.broadcast_to(cell[:, at], (C, 128))
-        turned = jnp.concatenate([feats, cells], axis=0).T.reshape(8, 2, 8, 128)
-        first, second = turned[:, 0], turned[:, 1]
-        low = low_lanes(first.shape)
-        to = slice(chunk * 8, chunk * 8 + 8)
-        out_ref[to, 0:8, :] = jnp.where(low, first, pltpu.roll(second, C, 2)).astype(BF)
-        out_ref[to, 8:16, :] = jnp.where(low, pltpu.roll(first, C, 2), second).astype(BF)
-
-
-def onehots(recv_ref):
-    cells = recv_ref[:, 8:16, :].astype(F32).reshape(1024, 128)
-    ids = iota((1024, 256), 1).astype(F32)
-    return ones_where(cells[:, 0:1] == ids), ones_where(cells[:, C : C + 1] == ids)
-
-
-def grid_kernel(recv_ref, mask_ref, cot_ref, rec_ref, up_ref, down_ref):
-    feats = recv_ref[:, 0:8, :].astype(F32).reshape(1024, 128).astype(BF)
-    both = tn(feats, jnp.concatenate(onehots(recv_ref), axis=1))
-    grid = both[0:C, 0:256] + both[C:128, 256:512]
-    grid = jnp.concatenate([grid, jnp.zeros((C, 256), F32)], axis=0).astype(BF)
+        turned = jnp.concatenate([feats, feats], axis=0).T.reshape(8, 2, 8, 128)
+        slots = jnp.where(low_lanes((8, 8, 128)), turned[:, 0], turned[:, 1])
+        cells = jnp.broadcast_to(cell_ref[0:1, at].astype(F32), (8, 128))
+        cells = pltpu.roll(cells, 0, 1, stride=16, stride_axis=0)
+        cells = jnp.concatenate([cells[-d % 8 : -d % 8 + 1] for d in range(8)], axis=0)
+        live = lane.astype(F32) < counts[chunk * 8 : chunk * 8 + 8]
+        cells = jnp.where(live, cells, NO_CELL)
+        for d in range(8):
+            row = (chunk * 8 + d) * ROWS
+            rows_ref[row : row + 8, :] = slots[d]
+            rows_ref[row + 8 : row + 9, :] = cells[d : d + 1]
+            rows_ref[row + 9 : row + 10, :] = cells[d : d + 1]
+    out_ref[...] = rows_ref[...].astype(BF)
+
+
+def equal(a, b):
+    return jnp.where(a == b, jnp.ones((), BF), jnp.zeros((), BF))
+
+
+def onehots(recv_ref, rows, wide_ref):
+    count = DEV * rows
+    lane = iota((1, count), 1)
+    sender = lane // rows
+    r = lane - sender * rows
+    wide_ref[...] = recv_ref[...].astype(F32)
+    cells = wide_ref[pl.ds(8, DEV, stride=ROWS), :].astype(BF)
+    down = iota((DEV, count), 0)
+    here = down == sender
+    down = down.astype(F32).astype(BF)
+    ids = iota((256, count), 0).astype(F32).astype(BF)
+    hot = []
+    for h in (0, 1):
+        spot = jnp.where(r < 8, r + h * 8, 255).astype(F32).astype(BF)
+        values = nn(cells, equal(down, spot))
+        cell = jnp.sum(jnp.where(here, values, 0.0), axis=0, keepdims=True)
+        cell = jnp.where(r < 8, cell, NO_CELL)
+        hot.append(equal(ids, cell.astype(BF)))
+    return hot
+
+
+def grid_kernel(recv_ref, mask_ref, cot_ref, rec_ref, up_ref, down_ref, wide):
+    first, second = [nn(hot, recv_ref[...]) for hot in onehots(recv_ref, ROWS, wide)]
+    grid = jnp.where(low_lanes(first.shape), first + pltpu.roll(second, C, 1), 0.0).astype(BF)
     row, col = iota((512, 256), 0), iota((512, 256), 1)
     pick = ones_where(col == ((row & 7) >> 1) * K + (row >> 3))
-    rec = nt(pick, grid)
+    rec = nn(pick, grid)
     kk, zz = iota((K, Y, Z), 0), iota((K, Y, Z), 2)
     zrow, lane = iota((Z, 128), 0), iota((Z, 128), 1)
     for a in (0, 1):
@@ -306,15 +327,13 @@
     over(2 * kz - 4, second)
 
 
-def wgrad(count, also, padded, shifted, col):
-    def build(m, n):
-        three = [padded[pl.ds(m + s, n)] for s in (2, 1, 0)]
-        rows = pl.ds(pl.multiple_of(m * Y, 16), n * Y)
-        shifted[rows, :] = jnp.concatenate(three, axis=2).reshape(n * Y, 384).astype(BF)
-        also(rows, m, n)
-
-    over(count, build)
-    return tn(shifted[...], col[...])
+def wgrad(count, padded, shifted, col, total):
+    flat = padded[...].reshape((count + 2) * Y, 128).astype(BF).T
+    width = count * Y
+    for i, s in enumerate((2, 1, 0)):
+        shifted[i * 128 : i * 128 + 128, :] = flat[:, s * Y : s * Y + width]
+    for start in (0, 192):
+        total[start : start + 192, :] = nn(shifted[start : start + 192, :], col[...])
 
 
 def packed(block):
@@ -335,11 +354,18 @@
 
 
 def second_grad_kernel(
-    act_ref, delta_ref, recv_ref, lifted_ref, dec_ref, up_ref, one_ref, two_ref,
-    out_ref, hot_ref, part_ref, lifted_col, dec_out, b1x_ref, b0_ref, ud_ref,
-    b1o_ref, padded, shifted, col, total, col3,
+    act_ref, delta_ref, recv_ref, lifted_ref, dec_ref, rec_ref, up_ref, one_ref, two_ref,
+    out_ref, hot_ref, part_ref, lifted_col, dec_out, b1x_ref, b0_ref, ud_ref, pick_ref, parent_ref,
+    b1o_ref, padded, shifted, col, total, col3, wide,
 ):
-    hot_ref[...] = jnp.concatenate(onehots(recv_ref), axis=1)
+    for h, hot in enumerate(onehots(recv_ref, 8, wide)):
+        hot_ref[:, h * 256 : h * 256 + 256] = hot.T
+    cell, src = iota((256, 512), 0), iota((256, 512), 1)
+    pick_ref[...] = ones_where(src == (cell & (K - 1)) * Y + 2 * (cell >> 6))
+    rec = rec_ref[...].astype(F32).reshape(K * Y, 128)
+    row, lane = iota((K * Y, 128), 0), iota((K * Y, 128), 1)
+    rec = jnp.where(lane < C, rec, pltpu.roll(rec, C, 1))
+    parent_ref[...] = jnp.where(((row & 1) == 0) == (lane < C), rec, 0.0).astype(BF)
     dec_out[...] = dec_ref[2 : 2 + Z]
     backward_weights(up_ref, one_ref, two_ref, b1o_ref, b1x_ref, b0_ref, ud_ref)
 
@@ -358,10 +384,12 @@
     padded[0:4] = jnp.zeros((4, Y, 128), F32)
     padded[132:136] = jnp.zeros((4, Y, 128), F32)
     padded[4:132] = delta_ref[2:130].astype(F32)
-    def act_col(rows, m, n):
+    def act_col(m, n):
+        rows = pl.ds(pl.multiple_of(m * Y, 16), n * Y)
         col[rows, :] = stack_y(act_ref[pl.ds(m, n)].astype(F32))
 
-    total[...] = wgrad(134, act_col, padded, shifted, col)
+    over(134, act_col)
+    wgrad(134, padded, shifted, col, total)
 
     def put(t, block):
         out_ref[t] = block
@@ -370,8 +398,8 @@
 
 
 def backward_kernel(
-    left_ref, right_ref, slope_ref, keep_ref, rec_ref, hot_ref, part_own, lifted_col, two_ref,
-    b1x_ref, b0_ref, ud_ref, out_ref,
+    left_ref, right_ref, slope_ref, keep_ref, hot_ref, part_own, lifted_col, two_ref,
+    b1x_ref, b0_ref, ud_ref, pick_ref, parent_ref, out_ref,
     col3, part3, col4, part4, padded, shifted, total, du,
 ):
     def columns(q, n):
@@ -423,9 +451,7 @@
     summed = summed + pltpu.roll(summed, Y - 1, 1)
     summed = summed + pltpu.roll(summed, C, 2)
     parent = summed.reshape(K * Y, 128).astype(BF)
-    cell, src = iota((256, 512), 0), iota((256, 512), 1)
-    pick = ones_where(src == (cell & (K - 1)) * Y + 2 * (cell >> 6))
-    parent = nn(pick, parent)
+    parent = nn(pick_ref[...], parent)
     low = low_lanes(parent.shape)
     sides = [jnp.where(low, parent, 0.0), jnp.where(low, 0.0, parent)]
     slots = nn(hot_ref[...], jnp.concatenate(sides, axis=0).astype(BF))
@@ -435,16 +461,13 @@
         out_ref[2 * index, 8:24, :] = block[0:16]
         out_ref[2 * index + 1, 8:24, :] = block[16:32]
 
-    rec = rec_ref[...].astype(F32).reshape(K * Y, 128)
-    rec = jnp.where(lane < C, rec, pltpu.roll(rec, C, 1))
-    rec = jnp.where(match, rec, 0.0).astype(BF)
     for e in (0, 1):
-        up_grad = tn(split[e], rec)
+        up_grad = tn(split[e], parent_ref[...])
         for a in (0, 1):
             for b in (0, 1):
                 block = up_grad[a * C : a * C + C, b * C : b * C + C]
                 put(54 + 4 * a + 2 * b + e, packed(block))
-    total[...] = wgrad(132, lambda *_: None, padded, shifted, lifted_col)
+    wgrad(132, padded, shifted, lifted_col, total)
     tap_grads(total, lambda t, block: put(27 + t, block))
     for t in range(27):
         put(t, two_ref[t])
@@ -497,13 +520,15 @@
     size_x, size_y, size_z = cotangent.shape[1:]
     voxels = size_x * size_y * size_z * lax.axis_size("xy") * lax.axis_size("gz")
     scale = 1.0 / math.sqrt(voxels)
-    sent = call(send_kernel, ((DEV, 16, 128), BF), raw=True, home=True, limit=58 << 20)(
+    sent = call(send_kernel, ((DEV * ROWS, 128), BF), [((DEV * ROWS, 128), F32)], raw=True, limit=58 << 20)(
         parent_feat, parent_cell, send_count
     )
-    recv = exchange(sent)
+    recv = exchange(sent.reshape(DEV, ROWS // 2, 2, 128)).reshape(DEV * ROWS, 128)
     cot = cotangent.transpose(3, 2, 1, 0).reshape(Z, Y, 128)
     rec, up_edge, down_edge = call(
-        grid_kernel, [((K, Y, 128), BF), ((4, Y, 128), BF), ((4, Y, 128), BF)]
+        grid_kernel,
+        [((K, Y, 128), BF), ((4, Y, 128), BF), ((4, Y, 128), BF)],
+        [((DEV * ROWS, 128), F32)],
     )(recv, child_mask, cot)
     before, after = shift(up_edge, "gz", 1), shift(down_edge, "gz", -1)
     rec_ext = jnp.concatenate([before[0:2], rec, after[0:2]], axis=0)
@@ -530,28 +555,29 @@
         ],
     )(left, right, before, after, cot, lift_own, seen_own, part_own, u, w1x, w2)
     delta_left, delta_right = shift(delta, "xy", 1), shift(delta, "xy", -1)
-    two, hot, part_back, lifted_col, dec, b1x, b0, ud = call(
+    two, hot, part_back, lifted_col, dec, b1x, b0, ud, pick, parent = call(
         second_grad_kernel,
         [
             ((27, 32, 128), BF), ((1024, 512), BF), ((3, 132, Y, 256), F32), ((1056, 768), BF),
             ((Z, Y, 128), BF), ((3, 768, 256), BF), ((768, 384), BF), ((2, 128, 128), BF),
+            ((256, 512), BF), ((512, 128), BF),
         ],
         [
-            ((3, 384, 256), BF), ((136, Y, 128), F32), ((1072, 384), BF), ((1072, 768), BF), ((384, 768), F32),
-            ((1056, 384), BF),
+            ((3, 384, 256), BF), ((136, Y, 128), F32), ((384, 1072), BF), ((1072, 768), BF), ((384, 768), F32),
+            ((1056, 384), BF), ((DEV * ROWS, 128), F32),
         ],
-        home=(False, False, False, False, True, False, False, False),
-    )(act, delta, recv, lifted, dec, *weights)
+        home=(False, False, False, False, True, *[False] * 5),
+    )(act, delta, recv, lifted, dec, rec, *weights)
     decoded = dec.reshape(Z, Y, 2, C).transpose(3, 2, 1, 0)
     message = call(
         backward_kernel,
         ((DEV, 24, 128), BF),
         [
             ((1056, 768), BF), ((3, 132, Y, 256), F32), ((1040, 768), BF), ((130, Y, 384), F32),
-            ((134, Y, 128), F32), ((1056, 384), BF), ((384, 768), F32), ((K, 2, Y, 128), F32),
+            ((134, Y, 128), F32), ((384, 1056), BF), ((384, 768), F32), ((K, 2, Y, 128), F32),
         ],
     )(
-        delta_left, delta_right, slope, keep, rec, hot, part_back, lifted_col, two, b1x, b0, ud
+        delta_left, delta_right, slope, keep, hot, part_back, lifted_col, two, b1x, b0, ud, pick, parent
     )
     back = exchange(message)
     total = call(functools.partial(sum_kernel, scale=scale), ((DEV, 16, 128), BF))(back)

time: 117 us -> 115 us (0.983)
  waiting for transfers between devices: 36.1 us -> 33 us
    all_to_all x2, waiting for transfers between devices: 25.3 us -> 22.4 us  [exchange(): return lax.all_to_all(array, ('gz', 'xy'), 0, 0, tiled=True)]
  transfers between devices with their start and end apart: 8 -> 8, of which waited for: 6 -> 6; matrix products, arithmetic and copies ran while one was open for 1% -> 2% of each run, Pallas kernels for 6% -> 6%
where the time goes in v3:
time: 115 us
  waiting for transfers between devices  33 us (29%)
  blocking collectives  28.2 us (25%)
  starting transfers between devices  27.4 us (24%)
  Pallas kernels  22.7 us (20%)
  local copies, waits for them, and re-layouts  2.34 us (2%)
    all_to_all x1, blocking collectives, exchange(): return lax.all_to_all(array, ('gz', 'xy'), 0, 0, tiled=True)  28.2 us
    pallas_call x9, Pallas kernels, run(): pl.pallas_call(kernel, out_shape=shapes, in_specs=[vmem] * len(args), out...  22.7 us
    all_to_all x2, waiting for transfers between devices, exchange(): return lax.all_to_all(array, ('gz', 'xy'), 0, 0, tiled=True)  22.4 us
    all_to_all x2, starting transfers between devices, exchange(): return lax.all_to_all(array, ('gz', 'xy'), 0, 0, tiled=True)  15.8 us
    ppermute x6, starting transfers between devices, shift(): return lax.ppermute(array, axis, pairs)  11.7 us
    ppermute x6, waiting for transfers between devices, shift(): return lax.ppermute(array, axis, pairs)  10.6 us
  transfers between devices with their start and end apart: 8, of which 6 were waited for; matrix products, arithmetic and copies ran while one was open for 2% of the time, Pallas kernels for 6%

profile of v3, /device:TPU:1, one launch (start us, length us, event | category | flops | bytes accessed | tf_op | source)
XLA Modules:
  0.0 114.5 jit_solution(5886910574899538655)
XLA Ops:
  0.7 2.1 %shard_map.119 = bf16[1280,128]{1,0:T(8,128)(2,1)} custom-call(bf16[1,64,2048]{2,1,0:T(8,128)(2,1)} %feat_ref.1, s32[1,2048]{1,0:T(1,128)} %cell_ref.1, s32[1,128]{1,0:T(1,128)} %count_ref.1), custom_call_target="tpu_custom_call" | custom-call | tf_op jit(solution)/shard_map/pallas_call | solution.py:82
  2.8 11.5 %all-to-all-start = ((bf16[128,5,2,128]{3,2,1,0:T(2,128)(2,1)}), bf16[128,5,2,128]{3,2,1,0:T(2,128)(2,1)S(1)}, u32[]{:S(2)}, u32[]{:S(2)}) async-start(bf16[128,5,2,128]{3,2,1,0:T(2,128)(2,1)} %bitcast), calls=%async_computation | async-start | bytes 655360 | tf_op jit(solution)/shard_map/all_to_all | solution.py:514
  14.3 1.0 copy.15
  15.5 10.7 %all-to-all-done = bf16[128,5,2,128]{3,2,1,0:T(2,128)(2,1)S(1)} async-done(((bf16[128,5,2,128]{3,2,1,0:T(2,128)(2,1)}), bf16[128,5,2,128]{3,2,1,0:T(2,128)(2,1)S(1)}, u32[]{:S(2)}, u32[]{:S(2)}) %all-to-all-start) | async-done | bytes 327712 | tf_op jit(solution)/shard_map/all_to_all | solution.py:514
  26.1 1.1 shard_map.120
  27.2 2.8 %collective-permute-start = (bf16[4,8,128]{2,1,0:T(8,128)(2,1)S(1)}, bf16[4,8,128]{2,1,0:T(8,128)(2,1)S(1)}, u32[]{:S(2)}, u32[]{:S(2)}) collective-permute-start(bf16[4,8,128]{2,1,0:T(8,128)(2,1)S(1)} %get-tuple-element.33), channel_id=1, source_target_pairs={{0,16},{16,32},{32,48},{48,64},{64,80},{80,96},{96,112},{1,17},{17... | collective-permute-start | bytes 24584 | tf_op jit(solution)/shard_map/ppermute | solution.py:510
  30.1 1.9 %collective-permute-start.1 = (bf16[4,8,128]{2,1,0:T(8,128)(2,1)S(1)}, bf16[4,8,128]{2,1,0:T(8,128)(2,1)S(1)}, u32[]{:S(2)}, u32[]{:S(2)}) collective-permute-start(bf16[4,8,128]{2,1,0:T(8,128)(2,1)S(1)} %get-tuple-element.35), channel_id=1, source_target_pairs={{16,0},{32,16},{48,32},{64,48},{80,64},{96,80},{112,96},{17,1},{33... | collective-permute-start | bytes 24584 | tf_op jit(solution)/shard_map/ppermute | solution.py:510
  32.0 3.0 %collective-permute-done.1.after_ref = bf16[4,8,128]{2,1,0:T(8,128)(2,1)S(1)} collective-permute-done((bf16[4,8,128]{2,1,0:T(8,128)(2,1)S(1)}, bf16[4,8,128]{2,1,0:T(8,128)(2,1)S(1)}, u32[]{:S(2)}, u32[]{:S(2)}) %collective-permute-start.1) | collective-permute-done | bytes 8224 | tf_op jit(solution)/shard_map/ppermute | solution.py:510
  35.1 2.5 %collective-permute-start.2 = (bf16[68,8,128]{2,1,0:T(8,128)(2,1)S(1)}, bf16[68,8,128]{2,1,0:T(8,128)(2,1)S(1)}, u32[]{:S(2)}, u32[]{:S(2)}) collective-permute-start(bf16[68,8,128]{2,1,0:T(8,128)(2,1)S(1)} %pad_maximum_fusion.rec_ref), channel_id=1, source_target_pairs={{0,1},{1,2},{2,3},{3,4},{4,5},{5,6},{6,7},{7,8},{8,9},{9,10},{10,1... | collective-permute-start | bytes 417800 | tf_op jit(solution)/shard_map/ppermute | solution.py:510
  37.5 1.3 %collective-permute-start.3 = (bf16[68,8,128]{2,1,0:T(8,128)(2,1)S(1)}, bf16[68,8,128]{2,1,0:T(8,128)(2,1)S(1)}, u32[]{:S(2)}, u32[]{:S(2)}) collective-permute-start(bf16[68,8,128]{2,1,0:T(8,128)(2,1)S(1)} %pad_maximum_fusion.rec_ref), channel_id=1, source_target_pairs={{1,0},{2,1},{3,2},{4,3},{5,4},{6,5},{7,6},{8,7},{9,8},{10,9},{11,1... | collective-permute-start | bytes 417800 | tf_op jit(solution)/shard_map/ppermute | solution.py:510
  38.9 1.8 %shard_map.121 = (f32[68,2,8,128]{3,2,1,0:T(8,128)S(1)}, f32[68,2,8,128]{3,2,1,0:T(8,128)S(1)}, f32[3,136,8,256]{3,2,1,0:T(8,128)S(1)}, bf16[768,128]{1,0:T(8,12...) custom-call(bf16[68,8,128]{2,1,0:T(8,128)(2,1)S(1)} %pad_maximum_fusion.rec_ref, ...), custom_call_target="tpu_custom_call" | custom-call | tf_op jit(solution)/shard_map/pallas_call | solution.py:82
  40.7 3.0 %collective-permute-done.3.right_ref = bf16[68,8,128]{2,1,0:T(8,128)(2,1)S(1)} collective-permute-done((bf16[68,8,128]{2,1,0:T(8,128)(2,1)S(1)}, bf16[68,8,128]{2,1,0:T(8,128)(2,1)S(1)}, u32[]{:S(2)}, u32[]{:S(2)}) %collective-permute-start.3) | collective-permute-done | bytes 139296 | tf_op jit(solution)/shard_map/ppermute | solution.py:510
  43.7 4.6 %shard_map.122 = (bf16[134,8,256]{2,1,0:T(8,128)(2,1)S(1)}, bf16[132,8,128]{2,1,0:T(8,128)(2,1)S(1)}, bf16[132,8,128]{2,1,0:T(8,128)(2,1)S(1)}, f32[134,8,256]{2...) custom-call(bf16[68,8,128]{2,1,0:T(8,128)(2,1)S(1)} %collective-permute-done.2.left_ref, ...), custom_call_target="tpu_custom_call" | custom-call | tf_op jit(solution)/shard_map/pallas_call | solution.py:82
  48.3 1.7 %collective-permute-start.4 = (bf16[132,8,128]{2,1,0:T(8,128)(2,1)S(1)}, bf16[132,8,128]{2,1,0:T(8,128)(2,1)S(1)}, u32[]{:S(2)}, u32[]{:S(2)}) collective-permute-start(bf16[132,8,128]{2,1,0:T(8,128)(2,1)S(1)} %get-tuple-element.43.delta_ref), channel_id=1, source_target_pairs={{0,1},{1,2},{2,3},{3,4},{4,5},{5,6},{6,7},{7,8},{8,9},{9,10},{10,1... | collective-permute-start | bytes 811016 | tf_op jit(solution)/shard_map/ppermute | solution.py:510
  50.0 1.5 %collective-permute-start.5 = (bf16[132,8,128]{2,1,0:T(8,128)(2,1)S(1)}, bf16[132,8,128]{2,1,0:T(8,128)(2,1)S(1)}, u32[]{:S(2)}, u32[]{:S(2)}) collective-permute-start(bf16[132,8,128]{2,1,0:T(8,128)(2,1)S(1)} %get-tuple-element.43.delta_ref), channel_id=1, source_target_pairs={{1,0},{2,1},{3,2},{4,3},{5,4},{6,5},{7,6},{8,7},{9,8},{10,9},{11,1... | collective-permute-start | bytes 811016 | tf_op jit(solution)/shard_map/ppermute | solution.py:510
  51.5 4.2 %shard_map.123 = (bf16[27,32,128]{2,1,0:T(8,128)(2,1)S(1)}, bf16[1024,512]{1,0:T(8,128)(2,1)S(1)}, f32[3,132,8,256]{3,2,1,0:T(8,128)S(1)}, bf16[1056,768]{1,0:T(...) custom-call(bf16[134,8,256]{2,1,0:T(8,128)(2,1)S(1)} %get-tuple-elem, ...), custom_call_target="tpu_custom_call" | custom-call | tf_op jit(solution)/shard_map/pallas_call | solution.py:82
  56.0 4.3 %collective-permute-done.5.right_ref = bf16[132,8,128]{2,1,0:T(8,128)(2,1)S(1)} collective-permute-done((bf16[132,8,128]{2,1,0:T(8,128)(2,1)S(1)}, bf16[132,8,128]{2,1,0:T(8,128)(2,1)S(1)}, u32[]{:S(2)}, u32[]{:S(2)}) %collective-permute-start.5) | collective-permute-done | bytes 270368 | tf_op jit(solution)/shard_map/ppermute | solution.py:510
  60.3 5.3 %shard_map.124 = bf16[128,24,128]{2,1,0:T(8,128)(2,1)S(1)} custom-call(bf16[132,8,128]{2,1,0:T(8,128)(2,1)S(1)} %collective-permute-done.4.left_ref, bf16[132,8,128]{2,1,0:T(8,128)(2,1)S(1)} %collective-permute-done.5.right_ref, f32[134,8,256]{2,1,0:T(8,128)S(1)} %get-tuple-element.47.slope_ref, bf16[132,8,128]{2,1,0:T(8,128)(2,1)S(1)} %get-tuple-element.48.keep_ref, ...), custom_call_target="tpu_custom_call" | custom-call | tf_op jit(solution)/shard_map/pallas_call | solution.py:82
  65.6 28.2 %all_to_all.15.recv_ref = bf16[128,24,128]{2,1,0:T(8,128)(2,1)S(1)} all-to-all(bf16[128,24,128]{2,1,0:T(8,128)(2,1)S(1)} %shard_map.124), channel_id=1, replica_groups=mesh['gz'=8,'xy'=16] {'gz','xy'}, dimensions={0} | all-to-all | bytes 1572864 | tf_op jit(solution)/shard_map/all_to_all | solution.py:514
  93.8 1.0 shard_map.126
  94.8 4.3 %all-to-all-start.2 = ((bf16[128,16,128]{2,1,0:T(8,128)(2,1)}), bf16[128,16,128]{2,1,0:T(8,128)(2,1)S(1)}, u32[]{:S(2)}, u32[]{:S(2)}) async-start(bf16[128,16,128]{2,1,0:T(8,128)(2,1)} %shard_map.126), calls=%async_computation.2 | async-start | bytes 1048576 | tf_op jit(solution)/shard_map/all_to_all | solution.py:514
  100.2 1.2 %shard_map.125 = bf16[1,64,2048]{2,1,0:T(8,128)(2,1)} custom-call(bf16[128,24,128]{2,1,0:T(8,128)(2,1)S(1)} %all_to_all.15.recv_ref), custom_call_target="tpu_custom_call" | custom-call | tf_op jit(solution)/shard_map/pallas_call | solution.py:82
  101.3 11.7 %all-to-all-done.2.recv_ref = bf16[128,16,128]{2,1,0:T(8,128)(2,1)S(1)} async-done(((bf16[128,16,128]{2,1,0:T(8,128)(2,1)}), bf16[128,16,128]{2,1,0:T(8,128)(2,1)S(1)}, u32[]{:S(2)}, u32[]{:S(2)}) %all-to-all-start.2) | async-done | bytes 524320 | tf_op jit(solution)/shard_map/all_to_all | solution.py:514
  113.1 1.5 %shard_map.127 = (f32[27,64,64]{2,1,0:T(8,128)}, f32[27,64,64]{2,1,0:T(8,128)}, f32[8,64,64]{2,1,0:T(8,128)}) custom-call(bf16[128,16,128]{2,1,0:T(8,128)(2,1)S(1)} %all-to-all-done.2.recv_ref), custom_call_target="tpu_custom_call" | custom-call | tf_op jit(solution)/shard_map/pallas_call | solution.py:82
  (17 shorter events, 1.6 us)
Async XLA Ops:
  0.6 25.5 %copy-start.3 = (s32[2,8,128]{2,1,0:T(8,128)S(1)}, s32[2,8,128]{2,1,0:T(8,128)}, u32[]{:S(2)}) copy-start(s32[2,8,128]{2,1,0:T(8,128)} %mask_ref.1) | copy-start | bytes 24580
  0.6 38.2 %copy-start.2 = (bf16[8,64,64]{2,1,0:T(8,128)(2,1)S(1)}, bf16[8,64,64]{2,1,0:T(8,128)(2,1)}, u32[]{:S(2)}) copy-start(bf16[8,64,64]{2,1,0:T(8,128)(2,1)} %up_ref.3) | copy-start | bytes 196612
  0.7 38.2 %copy-start = (bf16[27,64,64]{2,1,0:T(8,128)(2,1)S(1)}, bf16[27,64,64]{2,1,0:T(8,128)(2,1)}, u32[]{:S(2)}) copy-start(bf16[27,64,64]{2,1,0:T(8,128)(2,1)} %one_ref.3) | copy-start | bytes 663556
  0.7 38.2 %copy-start.1 = (bf16[27,64,64]{2,1,0:T(8,128)(2,1)S(1)}, bf16[27,64,64]{2,1,0:T(8,128)(2,1)}, u32[]{:S(2)}) copy-start(bf16[27,64,64]{2,1,0:T(8,128)(2,1)} %two_ref.3) | copy-start | bytes 663556
  2.8 23.4 %all-to-all-start = ((bf16[128,5,2,128]{3,2,1,0:T(2,128)(2,1)}), bf16[128,5,2,128]{3,2,1,0:T(2,128)(2,1)S(1)}, u32[]{:S(2)}, u32[]{:S(2)}) async-start(bf16[128,5,2,128]{3,2,1,0:T(2,128)(2,1)} %bitcast), calls=%async_computation | async-start | bytes 655360 | tf_op jit(solution)/shard_map/all_to_all | solution.py:514
  27.2 4.8 %collective-permute-start = (bf16[4,8,128]{2,1,0:T(8,128)(2,1)S(1)}, bf16[4,8,128]{2,1,0:T(8,128)(2,1)S(1)}, u32[]{:S(2)}, u32[]{:S(2)}) collective-permute-start(bf16[4,8,128]{2,1,0:T(8,128)(2,1)S(1)} %get-tuple-element.33), channel_id=1, source_target_pairs={{0,16},{16,32},{32,48},{48,64},{64,80},{80,96},{96,112},{1,17},{17... | collective-permute-start | bytes 24584 | tf_op jit(solution)/shard_map/ppermute | solution.py:510
  30.1 5.0 %collective-permute-start.1 = (bf16[4,8,128]{2,1,0:T(8,128)(2,1)S(1)}, bf16[4,8,128]{2,1,0:T(8,128)(2,1)S(1)}, u32[]{:S(2)}, u32[]{:S(2)}) collective-permute-start(bf16[4,8,128]{2,1,0:T(8,128)(2,1)S(1)} %get-tuple-element.35), channel_id=1, source_target_pairs={{16,0},{32,16},{48,32},{64,48},{80,64},{96,80},{112,96},{17,1},{33... | collective-permute-start | bytes 24584 | tf_op jit(solution)/shard_map/ppermute | solution.py:510
  35.1 5.6 %collective-permute-start.2 = (bf16[68,8,128]{2,1,0:T(8,128)(2,1)S(1)}, bf16[68,8,128]{2,1,0:T(8,128)(2,1)S(1)}, u32[]{:S(2)}, u32[]{:S(2)}) collective-permute-start(bf16[68,8,128]{2,1,0:T(8,128)(2,1)S(1)} %pad_maximum_fusion.rec_ref), channel_id=1, source_target_pairs={{0,1},{1,2},{2,3},{3,4},{4,5},{5,6},{6,7},{7,8},{8,9},{9,10},{10,1... | collective-permute-start | bytes 417800 | tf_op jit(solution)/shard_map/ppermute | solution.py:510
  37.5 6.1 %collective-permute-start.3 = (bf16[68,8,128]{2,1,0:T(8,128)(2,1)S(1)}, bf16[68,8,128]{2,1,0:T(8,128)(2,1)S(1)}, u32[]{:S(2)}, u32[]{:S(2)}) collective-permute-start(bf16[68,8,128]{2,1,0:T(8,128)(2,1)S(1)} %pad_maximum_fusion.rec_ref), channel_id=1, source_target_pairs={{1,0},{2,1},{3,2},{4,3},{5,4},{6,5},{7,6},{8,7},{9,8},{10,9},{11,1... | collective-permute-start | bytes 417800 | tf_op jit(solution)/shard_map/ppermute | solution.py:510
  48.3 7.6 %collective-permute-start.4 = (bf16[132,8,128]{2,1,0:T(8,128)(2,1)S(1)}, bf16[132,8,128]{2,1,0:T(8,128)(2,1)S(1)}, u32[]{:S(2)}, u32[]{:S(2)}) collective-permute-start(bf16[132,8,128]{2,1,0:T(8,128)(2,1)S(1)} %get-tuple-element.43.delta_ref), channel_id=1, source_target_pairs={{0,1},{1,2},{2,3},{3,4},{4,5},{5,6},{6,7},{7,8},{8,9},{9,10},{10,1... | collective-permute-start | bytes 811016 | tf_op jit(solution)/shard_map/ppermute | solution.py:510
  50.0 10.3 %collective-permute-start.5 = (bf16[132,8,128]{2,1,0:T(8,128)(2,1)S(1)}, bf16[132,8,128]{2,1,0:T(8,128)(2,1)S(1)}, u32[]{:S(2)}, u32[]{:S(2)}) collective-permute-start(bf16[132,8,128]{2,1,0:T(8,128)(2,1)S(1)} %get-tuple-element.43.delta_ref), channel_id=1, source_target_pairs={{1,0},{2,1},{3,2},{4,3},{5,4},{6,5},{7,6},{8,7},{9,8},{10,9},{11,1... | collective-permute-start | bytes 811016 | tf_op jit(solution)/shard_map/ppermute | solution.py:510
  94.8 18.3 %all-to-all-start.2 = ((bf16[128,16,128]{2,1,0:T(8,128)(2,1)}), bf16[128,16,128]{2,1,0:T(8,128)(2,1)S(1)}, u32[]{:S(2)}, u32[]{:S(2)}) async-start(bf16[128,16,128]{2,1,0:T(8,128)(2,1)} %shard_map.126), calls=%async_computation.2 | async-start | bytes 1048576 | tf_op jit(solution)/shard_map/all_to_all | solution.py:514

commit v4 on v3

--- a/solution.py
+++ b/solution.py
@@ -225,9 +225,9 @@
     down_ref[2:4] = cot_ref[0:2]
 
 
-def lane_groups(own, left, right):
-    low = low_lanes(own.shape)
-    return own, jnp.where(low, right, left), jnp.where(low, left, right)
+def side_groups(side, far_pair, near_pair):
+    low = jnp.broadcast_to(side[None], near_pair.shape)
+    return jnp.where(low, near_pair, far_pair), jnp.where(low, far_pair, near_pair)
 
 
 def lift_tile(rec_ref, u_ref, lift, seen):
@@ -261,22 +261,21 @@
 
 
 def forward_kernel(
-    left_ref, right_ref, before_ref, after_ref, cot_in_ref,
+    far_ref, near_ref, side_ref, cot_ref,
     lift_own, seen_own, part_own, u_ref, w1x_ref, w2_ref,
     act_ref, delta_ref, dec_ref, slope_ref, lifted_ref, keep_ref,
-    lift, seen, mask, col1, part1, col2, part2, cot_ref,
+    lift, seen, mask, col1, part1, col2, part2,
 ):
     kz = KZ
-    cot_ref[0:2] = before_ref[2:4]
-    cot_ref[2 : 2 + Z] = cot_in_ref[...]
-    cot_ref[2 + Z : 4 + Z] = after_ref[2:4]
-    for t, ref in enumerate((left_ref, right_ref)):
+    side = side_ref[...] != 0
+    for t, ref in enumerate((far_ref, near_ref)):
         lift_tile(ref, u_ref, lift.at[t], seen.at[t])
 
     def columns(k0, n):
         def load(own_ref, ref):
             three = [own_ref[pl.ds(k0, n)], ref[0, pl.ds(k0, n)], ref[1, pl.ds(k0, n)]]
-            return lane_groups(*[v.reshape(2 * n, Y, 128) for v in three])
+            three = [v.reshape(2 * n, Y, 128) for v in three]
+            return three[0], *side_groups(side, *three[1:])
 
         own, near, far = load(lift_own, lift)
         at = pl.ds(2 * k0, 2 * n)
@@ -398,14 +397,15 @@
 
 
 def backward_kernel(
-    left_ref, right_ref, slope_ref, keep_ref, hot_ref, part_own, lifted_col, two_ref,
+    far_ref, near_ref, side_ref, slope_ref, keep_ref, hot_ref, part_own, lifted_col, two_ref,
     b1x_ref, b0_ref, ud_ref, pick_ref, parent_ref, out_ref,
     col3, part3, col4, part4, padded, shifted, total, du,
 ):
+    side = side_ref[...] != 0
+
     def columns(q, n):
         at = pl.ds(q, n)
-        left, right = left_ref[at].astype(F32), right_ref[at].astype(F32)
-        groups = lane_groups(left, left, right)[1:]
+        groups = side_groups(side, far_ref[at].astype(F32), near_ref[at].astype(F32))
         rows = pl.ds(pl.multiple_of(q * Y, 16), n * Y)
         col3[rows, :] = stack_y(jnp.concatenate(groups, axis=2))
 
@@ -504,10 +504,14 @@
         up_ref[o] = matrix(54 + o)
 
 
-def shift(array, axis, step):
+def swap(array, axis, first):
     count = lax.axis_size(axis)
-    pairs = [(i, i + step) for i in range(count) if 0 <= i + step < count]
-    return lax.ppermute(array, axis, pairs)
+    pairs = [(i, i + 1) for i in range(first, count - 1, 2)]
+    return lax.ppermute(array, axis, pairs + [(j, i) for i, j in pairs])
+
+
+def swaps(far, near, axis):
+    return swap(far, axis, 1), swap(near, axis, 0)
 
 
 def exchange(array):
@@ -530,9 +534,16 @@
         [((K, Y, 128), BF), ((4, Y, 128), BF), ((4, Y, 128), BF)],
         [((DEV * ROWS, 128), F32)],
     )(recv, child_mask, cot)
-    before, after = shift(up_edge, "gz", 1), shift(down_edge, "gz", -1)
+    odd_z = lax.axis_index("gz") % 2 == 1
+    far, near = swaps(
+        jnp.where(odd_z, up_edge, down_edge), jnp.where(odd_z, down_edge, up_edge), "gz"
+    )
+    before, after = jnp.where(odd_z, near, far), jnp.where(odd_z, far, near)
     rec_ext = jnp.concatenate([before[0:2], rec, after[0:2]], axis=0)
-    left, right = shift(rec_ext, "xy", 1), shift(rec_ext, "xy", -1)
+    cot_ext = jnp.concatenate([before[2:4], cot, after[2:4]], axis=0)
+    even_x = lax.axis_index("xy") % 2 == 0
+    side = (low_lanes((8, 128)) == even_x).astype(jnp.int32)
+    rec_far, rec_near = swaps(rec_ext, rec_ext, "xy")
     weights = up_weight, conv_one, conv_two
     lift_own, seen_own, part_own, u, w1x, w2 = call(
         own_kernel,
@@ -551,10 +562,9 @@
         [
             ((2, KZ, 2, Y, 128), F32), ((2, KZ, 2, Y, 128), F32), ((136, Y, 256), F32),
             ((1088, 768), BF), ((3, 136, Y, 256), F32), ((1072, 768), BF), ((134, Y, 384), F32),
-            ((132, Y, 128), BF),
         ],
-    )(left, right, before, after, cot, lift_own, seen_own, part_own, u, w1x, w2)
-    delta_left, delta_right = shift(delta, "xy", 1), shift(delta, "xy", -1)
+    )(rec_far, rec_near, side, cot_ext, lift_own, seen_own, part_own, u, w1x, w2)
+    delta_far, delta_near = swaps(delta, delta, "xy")
     two, hot, part_back, lifted_col, dec, b1x, b0, ud, pick, parent = call(
         second_grad_kernel,
         [
@@ -577,7 +587,7 @@
             ((134, Y, 128), F32), ((384, 1056), BF), ((384, 768), F32), ((K, 2, Y, 128), F32),
         ],
     )(
-        delta_left, delta_right, slope, keep, hot, part_back, lifted_col, two, b1x, b0, ud, pick, parent
+        delta_far, delta_near, side, slope, keep, hot, part_back, lifted_col, two, b1x, b0, ud, pick, parent
     )
     back = exchange(message)
     total = call(functools.partial(sum_kernel, scale=scale), ((DEV, 16, 128), BF))(back)

time: 115 us -> 106 us (0.922)
  waiting for transfers between devices: 33 us -> 26.5 us
  blocking collectives: 28.2 us -> 26.9 us
  starting transfers between devices: 27.4 us -> 26.2 us
    ppermute x6, waiting for transfers between devices: 10.6 us -> 4.18 us  [swap(): return lax.ppermute(array, axis, pairs + [(j, i) for i, j in pairs])]
    all_to_all x1, blocking collectives: 28.2 us -> 26.9 us  [exchange(): return lax.all_to_all(array, ('gz', 'xy'), 0, 0, tiled=True)]
    ppermute x6, starting transfers between devices: 11.7 us -> 10.4 us  [swap(): return lax.ppermute(array, axis, pairs + [(j, i) for i, j in pairs])]
  transfers between devices with their start and end apart: 8 -> 8, of which waited for: 6 -> 5; matrix products, arithmetic and copies ran while one was open for 2% -> 2% of each run, Pallas kernels for 6% -> 7%
where the time goes in v4:
time: 106 us
  blocking collectives  26.9 us (25%)
  waiting for transfers between devices  26.5 us (25%)
  starting transfers between devices  26.2 us (25%)
  Pallas kernels  22.8 us (22%)
  local copies, waits for them, and re-layouts  2.34 us (2%)
    all_to_all x1, blocking collectives, exchange(): return lax.all_to_all(array, ('gz', 'xy'), 0, 0, tiled=True)  26.9 us
    pallas_call x9, Pallas kernels, run(): pl.pallas_call(kernel, out_shape=shapes, in_specs=[vmem] * len(args), out...  22.8 us
    all_to_all x2, waiting for transfers between devices, exchange(): return lax.all_to_all(array, ('gz', 'xy'), 0, 0, tiled=True)  22.4 us
    all_to_all x2, starting transfers between devices, exchange(): return lax.all_to_all(array, ('gz', 'xy'), 0, 0, tiled=True)  15.8 us
    ppermute x6, starting transfers between devices, swap(): return lax.ppermute(array, axis, pairs + [(j, i) for i, j in pairs])  10.4 us
    ppermute x6, waiting for transfers between devices, swap(): return lax.ppermute(array, axis, pairs + [(j, i) for i, j in pairs])  4.18 us
  transfers between devices with their start and end apart: 8, of which 5 were waited for; matrix products, arithmetic and copies ran while one was open for 2% of the time, Pallas kernels for 7%

profile of v4, /device:TPU:1, one launch (start us, length us, event | category | flops | bytes accessed | tf_op | source)
XLA Modules:
  0.0 105.6 jit_solution(14295964918975586797)
XLA Ops:
  0.7 2.1 %shard_map.119 = bf16[1280,128]{1,0:T(8,128)(2,1)} custom-call(bf16[1,64,2048]{2,1,0:T(8,128)(2,1)} %feat_ref.1, s32[1,2048]{1,0:T(1,128)} %cell_ref.1, s32[1,128]{1,0:T(1,128)} %count_ref.1), custom_call_target="tpu_custom_call" | custom-call | tf_op jit(solution)/shard_map/pallas_call | solution.py:82
  2.8 11.5 %all-to-all-start = ((bf16[128,5,2,128]{3,2,1,0:T(2,128)(2,1)}), bf16[128,5,2,128]{3,2,1,0:T(2,128)(2,1)S(1)}, u32[]{:S(2)}, u32[]{:S(2)}) async-start(bf16[128,5,2,128]{3,2,1,0:T(2,128)(2,1)} %bitcast), calls=%async_computation | async-start | bytes 655360 | tf_op jit(solution)/shard_map/all_to_all | solution.py:518
  14.3 1.0 copy.15
  15.5 10.6 %all-to-all-done = bf16[128,5,2,128]{3,2,1,0:T(2,128)(2,1)S(1)} async-done(((bf16[128,5,2,128]{3,2,1,0:T(2,128)(2,1)}), bf16[128,5,2,128]{3,2,1,0:T(2,128)(2,1)S(1)}, u32[]{:S(2)}, u32[]{:S(2)}) %all-to-all-start) | async-done | bytes 327712 | tf_op jit(solution)/shard_map/all_to_all | solution.py:518
  26.1 1.1 %shard_map.120 = (bf16[64,8,128]{2,1,0:T(8,128)(2,1)S(1)}, bf16[4,8,128]{2,1,0:T(8,128)(2,1)S(1)}, bf16[4,8,128]{2,1,0:T(8,128)(2,1)S(1)}) custom-call(bf16[1280,128]{1,0:T(8,128)(2,1)S(1)} %bitcast.8, s32[2,8,128]{2,1,0:T(8,128)S(1)} %copy-done.3, bf16[128,8,128]{2,1,0:T(8,128)(2,1)S(1)} %copy.16.cot_ref), custom_call_target="tpu_custom_call" | custom-call | tf_op jit(solution)/shard_map/pallas_call | solution.py:82
  27.2 0.8 collective-permute-start
  28.0 2.1 %collective-permute-start.1 = (bf16[4,8,128]{2,1,0:T(8,128)(2,1)S(1)}, bf16[4,8,128]{2,1,0:T(8,128)(2,1)S(1)}, u32[]{:S(2)}, u32[]{:S(2)}) collective-permute-start(bf16[4,8,128]{2,1,0:T(8,128)(2,1)S(1)} %get-tuple-element.69), channel_id=1, source_target_pairs={{16,32},{48,64},{80,96},{32,16},{64,48},{96,80},{17,33},{49,65},{8... | collective-permute-start | bytes 24584 | tf_op jit(solution)/shard_map/ppermute | solution.py:510
  30.2 3.1 %collective-permute-done.1 = bf16[4,8,128]{2,1,0:T(8,128)(2,1)S(1)} collective-permute-done((bf16[4,8,128]{2,1,0:T(8,128)(2,1)S(1)}, bf16[4,8,128]{2,1,0:T(8,128)(2,1)S(1)}, u32[]{:S(2)}, u32[]{:S(2)}) %collective-permute-start.1) | collective-permute-done | bytes 8224 | tf_op jit(solution)/shard_map/ppermute | solution.py:510
  33.3 0.7 collective-permute-start.2
  34.0 1.6 %collective-permute-start.3 = (bf16[68,8,128]{2,1,0:T(8,128)(2,1)S(1)}, bf16[68,8,128]{2,1,0:T(8,128)(2,1)S(1)}, u32[]{:S(2)}, u32[]{:S(2)}) collective-permute-start(bf16[68,8,128]{2,1,0:T(8,128)(2,1)S(1)} %pad_maximum_fusion.1.rec_ref), channel_id=1, source_target_pairs={{0,1},{2,3},{4,5},{6,7},{8,9},{10,11},{12,13},{14,15},{1,0},{3,2},... | collective-permute-start | bytes 417800 | tf_op jit(solution)/shard_map/ppermute | solution.py:510
  35.6 1.8 %shard_map.121 = (f32[68,2,8,128]{3,2,1,0:T(8,128)S(1)}, f32[68,2,8,128]{3,2,1,0:T(8,128)S(1)}, f32[3,136,8,256]{3,2,1,0:T(8,128)S(1)}, bf16[768,128]{1,0:T(8,12...) custom-call(bf16[68,8,128]{2,1,0:T(8,128)(2,1)S(1)} %pad_maximum_fusion.1.rec_ref, ...), custom_call_target="tpu_custom_call" | custom-call | tf_op jit(solution)/shard_map/pallas_call | solution.py:82
  37.5 0.6 collective-permute-done.3.near_ref
  38.1 4.7 %shard_map.122 = (bf16[134,8,256]{2,1,0:T(8,128)(2,1)S(1)}, bf16[132,8,128]{2,1,0:T(8,128)(2,1)S(1)}, bf16[132,8,128]{2,1,0:T(8,128)(2,1)S(1)}, f32[134,8,256]{2...) custom-call(bf16[68,8,128]{2,1,0:T(8,128)(2,1)S(1)} %collective-permute-done.2.far_ref, ...), custom_call_target="tpu_custom_call" | custom-call | tf_op jit(solution)/shard_map/pallas_call | solution.py:82
  42.7 0.7 collective-permute-start.4
  43.4 4.5 %collective-permute-start.5 = (bf16[132,8,128]{2,1,0:T(8,128)(2,1)S(1)}, bf16[132,8,128]{2,1,0:T(8,128)(2,1)S(1)}, u32[]{:S(2)}, u32[]{:S(2)}) collective-permute-start(bf16[132,8,128]{2,1,0:T(8,128)(2,1)S(1)} %get-tuple-element.43.delta_ref), channel_id=1, source_target_pairs={{0,1},{2,3},{4,5},{6,7},{8,9},{10,11},{12,13},{14,15},{1,0},{3,2},... | collective-permute-start | bytes 811016 | tf_op jit(solution)/shard_map/ppermute | solution.py:510
  48.0 4.2 %shard_map.123 = (bf16[27,32,128]{2,1,0:T(8,128)(2,1)S(1)}, bf16[1024,512]{1,0:T(8,128)(2,1)S(1)}, f32[3,132,8,256]{3,2,1,0:T(8,128)S(1)}, bf16[1056,768]{1,0:T(...) custom-call(bf16[134,8,256]{2,1,0:T(8,128)(2,1)S(1)} %get-tuple-elem, ...), custom_call_target="tpu_custom_call" | custom-call | tf_op jit(solution)/shard_map/pallas_call | solution.py:82
  52.7 5.3 %shard_map.124 = bf16[128,24,128]{2,1,0:T(8,128)(2,1)S(1)} custom-call(bf16[132,8,128]{2,1,0:T(8,128)(2,1)S(1)} %collective-permute-done.4.far_ref, bf16[132,8,128]{2,1,0:T(8,128)(2,1)S(1)} %collective-permute-done.5.near_ref, s32[8,128]{1,0:T(8,128)S(1)} %iota.7.side_ref, f32[134,8,256]{2,1,0:T(8,128)S(1)} %get-tuple-element.47.slope_ref, ...), custom_call_target="tpu_custom_call" | custom-call | tf_op jit(solution)/shard_map/pallas_call | solution.py:82
  58.0 26.9 %all_to_all.15.recv_ref = bf16[128,24,128]{2,1,0:T(8,128)(2,1)S(1)} all-to-all(bf16[128,24,128]{2,1,0:T(8,128)(2,1)S(1)} %shard_map.124), channel_id=1, replica_groups=mesh['gz'=8,'xy'=16] {'gz','xy'}, dimensions={0} | all-to-all | bytes 1572864 | tf_op jit(solution)/shard_map/all_to_all | solution.py:518
  84.8 1.0 shard_map.126
  85.8 4.3 %all-to-all-start.2 = ((bf16[128,16,128]{2,1,0:T(8,128)(2,1)}), bf16[128,16,128]{2,1,0:T(8,128)(2,1)S(1)}, u32[]{:S(2)}, u32[]{:S(2)}) async-start(bf16[128,16,128]{2,1,0:T(8,128)(2,1)} %shard_map.126), calls=%async_computation.2 | async-start | bytes 1048576 | tf_op jit(solution)/shard_map/all_to_all | solution.py:518
  90.4 0.9 copy.19
  91.2 1.2 %shard_map.125 = bf16[1,64,2048]{2,1,0:T(8,128)(2,1)} custom-call(bf16[128,24,128]{2,1,0:T(8,128)(2,1)S(1)} %all_to_all.15.recv_ref), custom_call_target="tpu_custom_call" | custom-call | tf_op jit(solution)/shard_map/pallas_call | solution.py:82
  92.4 11.7 %all-to-all-done.2.recv_ref = bf16[128,16,128]{2,1,0:T(8,128)(2,1)S(1)} async-done(((bf16[128,16,128]{2,1,0:T(8,128)(2,1)}), bf16[128,16,128]{2,1,0:T(8,128)(2,1)S(1)}, u32[]{:S(2)}, u32[]{:S(2)}) %all-to-all-start.2) | async-done | bytes 524320 | tf_op jit(solution)/shard_map/all_to_all | solution.py:518
  104.1 1.5 %shard_map.127 = (f32[27,64,64]{2,1,0:T(8,128)}, f32[27,64,64]{2,1,0:T(8,128)}, f32[8,64,64]{2,1,0:T(8,128)}) custom-call(bf16[128,16,128]{2,1,0:T(8,128)(2,1)S(1)} %all-to-all-done.2.recv_ref), custom_call_target="tpu_custom_call" | custom-call | tf_op jit(solution)/shard_map/pallas_call | solution.py:82
  (21 shorter events, 1.1 us)
Async XLA Ops:
  0.6 25.5 %copy-start.3 = (s32[2,8,128]{2,1,0:T(8,128)S(1)}, s32[2,8,128]{2,1,0:T(8,128)}, u32[]{:S(2)}) copy-start(s32[2,8,128]{2,1,0:T(8,128)} %mask_ref.1) | copy-start | bytes 24580
  0.6 35.0 %copy-start.2 = (bf16[8,64,64]{2,1,0:T(8,128)(2,1)S(1)}, bf16[8,64,64]{2,1,0:T(8,128)(2,1)}, u32[]{:S(2)}) copy-start(bf16[8,64,64]{2,1,0:T(8,128)(2,1)} %up_ref.3) | copy-start | bytes 196612
  0.7 35.0 %copy-start = (bf16[27,64,64]{2,1,0:T(8,128)(2,1)S(1)}, bf16[27,64,64]{2,1,0:T(8,128)(2,1)}, u32[]{:S(2)}) copy-start(bf16[27,64,64]{2,1,0:T(8,128)(2,1)} %one_ref.3) | copy-start | bytes 663556
  0.7 35.0 %copy-start.1 = (bf16[27,64,64]{2,1,0:T(8,128)(2,1)S(1)}, bf16[27,64,64]{2,1,0:T(8,128)(2,1)}, u32[]{:S(2)}) copy-start(bf16[27,64,64]{2,1,0:T(8,128)(2,1)} %two_ref.3) | copy-start | bytes 663556
  2.8 23.4 %all-to-all-start = ((bf16[128,5,2,128]{3,2,1,0:T(2,128)(2,1)}), bf16[128,5,2,128]{3,2,1,0:T(2,128)(2,1)S(1)}, u32[]{:S(2)}, u32[]{:S(2)}) async-start(bf16[128,5,2,128]{3,2,1,0:T(2,128)(2,1)} %bitcast), calls=%async_computation | async-start | bytes 655360 | tf_op jit(solution)/shard_map/all_to_all | solution.py:518
  27.2 3.0 %collective-permute-start = (bf16[4,8,128]{2,1,0:T(8,128)(2,1)S(1)}, bf16[4,8,128]{2,1,0:T(8,128)(2,1)S(1)}, u32[]{:S(2)}, u32[]{:S(2)}) collective-permute-start(bf16[4,8,128]{2,1,0:T(8,128)(2,1)S(1)} %get-tuple-element.68), channel_id=1, source_target_pairs={{0,16},{32,48},{64,80},{96,112},{16,0},{48,32},{80,64},{112,96},{1... | collective-permute-start | bytes 24584 | tf_op jit(solution)/shard_map/ppermute | solution.py:510
  28.0 5.3 %collective-permute-start.1 = (bf16[4,8,128]{2,1,0:T(8,128)(2,1)S(1)}, bf16[4,8,128]{2,1,0:T(8,128)(2,1)S(1)}, u32[]{:S(2)}, u32[]{:S(2)}) collective-permute-start(bf16[4,8,128]{2,1,0:T(8,128)(2,1)S(1)} %get-tuple-element.69), channel_id=1, source_target_pairs={{16,32},{48,64},{80,96},{32,16},{64,48},{96,80},{17,33},{49,65},{8... | collective-permute-start | bytes 24584 | tf_op jit(solution)/shard_map/ppermute | solution.py:510
  33.3 4.1 %collective-permute-start.2 = (bf16[68,8,128]{2,1,0:T(8,128)(2,1)S(1)}, bf16[68,8,128]{2,1,0:T(8,128)(2,1)S(1)}, u32[]{:S(2)}, u32[]{:S(2)}) collective-permute-start(bf16[68,8,128]{2,1,0:T(8,128)(2,1)S(1)} %pad_maximum_fusion.1.rec_ref), channel_id=1, source_target_pairs={{1,2},{3,4},{5,6},{7,8},{9,10},{11,12},{13,14},{2,1},{4,3},{6,5},{... | collective-permute-start | bytes 417800 | tf_op jit(solution)/shard_map/ppermute | solution.py:510
  34.0 4.0 %collective-permute-start.3 = (bf16[68,8,128]{2,1,0:T(8,128)(2,1)S(1)}, bf16[68,8,128]{2,1,0:T(8,128)(2,1)S(1)}, u32[]{:S(2)}, u32[]{:S(2)}) collective-permute-start(bf16[68,8,128]{2,1,0:T(8,128)(2,1)S(1)} %pad_maximum_fusion.1.rec_ref), channel_id=1, source_target_pairs={{0,1},{2,3},{4,5},{6,7},{8,9},{10,11},{12,13},{14,15},{1,0},{3,2},... | collective-permute-start | bytes 417800 | tf_op jit(solution)/shard_map/ppermute | solution.py:510
  42.7 9.4 %collective-permute-start.4 = (bf16[132,8,128]{2,1,0:T(8,128)(2,1)S(1)}, bf16[132,8,128]{2,1,0:T(8,128)(2,1)S(1)}, u32[]{:S(2)}, u32[]{:S(2)}) collective-permute-start(bf16[132,8,128]{2,1,0:T(8,128)(2,1)S(1)} %get-tuple-element.43.delta_ref), channel_id=1, source_target_pairs={{1,2},{3,4},{5,6},{7,8},{9,10},{11,12},{13,14},{2,1},{4,3},{6,5},{... | collective-permute-start | bytes 811016 | tf_op jit(solution)/shard_map/ppermute | solution.py:510
  43.4 9.3 %collective-permute-start.5 = (bf16[132,8,128]{2,1,0:T(8,128)(2,1)S(1)}, bf16[132,8,128]{2,1,0:T(8,128)(2,1)S(1)}, u32[]{:S(2)}, u32[]{:S(2)}) collective-permute-start(bf16[132,8,128]{2,1,0:T(8,128)(2,1)S(1)} %get-tuple-element.43.delta_ref), channel_id=1, source_target_pairs={{0,1},{2,3},{4,5},{6,7},{8,9},{10,11},{12,13},{14,15},{1,0},{3,2},... | collective-permute-start | bytes 811016 | tf_op jit(solution)/shard_map/ppermute | solution.py:510
  85.8 18.3 %all-to-all-start.2 = ((bf16[128,16,128]{2,1,0:T(8,128)(2,1)}), bf16[128,16,128]{2,1,0:T(8,128)(2,1)S(1)}, u32[]{:S(2)}, u32[]{:S(2)}) async-start(bf16[128,16,128]{2,1,0:T(8,128)(2,1)} %shard_map.126), calls=%async_computation.2 | async-start | bytes 1048576 | tf_op jit(solution)/shard_map/all_to_all | solution.py:518

commit v5 on v4

--- a/solution.py
+++ b/solution.py
@@ -134,7 +134,8 @@
                 at = (e * 4 + b * 2 + a) * C
                 u_ref[at : at + C, :] = join(up_ref[4 * a + 2 * b + e], zero)
             at = 512 + (e * 2 + a) * C
-            u_ref[at : at + C, :] = ones_where(iota((C, 128), 1) == C + 2 * a + e)
+            lane = iota((C, 128), 1)
+            u_ref[at : at + C, :] = ones_where((lane & ~4) == C + 2 * a + e)
 
 
 def backward_weights(up_ref, one_ref, two_ref, b1o_ref, b1x_ref, b0_ref, ud_ref):
@@ -208,21 +209,24 @@
 def grid_kernel(recv_ref, mask_ref, cot_ref, rec_ref, up_ref, down_ref, wide):
     first, second = [nn(hot, recv_ref[...]) for hot in onehots(recv_ref, ROWS, wide)]
     grid = jnp.where(low_lanes(first.shape), first + pltpu.roll(second, C, 1), 0.0).astype(BF)
-    row, col = iota((512, 256), 0), iota((512, 256), 1)
-    pick = ones_where(col == ((row & 7) >> 1) * K + (row >> 3))
-    rec = nn(pick, grid)
+    row, col = iota((256, 256), 0), iota((256, 256), 1)
+    rec = nn(ones_where(col == (row & 3) * K + (row >> 2)), grid)
     kk, zz = iota((K, Y, Z), 0), iota((K, Y, Z), 2)
     zrow, lane = iota((Z, 128), 0), iota((Z, 128), 1)
+    marks = jnp.zeros((512, 128), F32)
     for a in (0, 1):
         mine = jnp.where((zz >> 1) == kk, mask_ref[a].astype(F32)[None], 0.0)
         place = ones_where(lane == C + 2 * a + (zrow & 1))
-        rec = rec + nn(mine.reshape(512, Z).astype(BF), place)
-    rec = rec.reshape(K, Y, 128).astype(BF)
+        marks = marks + nn(mine.reshape(512, Z).astype(BF), place)
+    odd_y = (iota((512, 128), 0) & 1) == 1
+    marks = jnp.where(odd_y, pltpu.roll(marks, 4, 1), marks).astype(BF)
+    fold = ones_where((iota((256, 512), 1) >> 1) == iota((256, 512), 0))
+    rec = (rec + nn(fold, marks)).reshape(K // 2, Y, 128).astype(BF)
     rec_ref[...] = rec
-    up_ref[0:2] = rec_ref[K - 2 : K]
-    up_ref[2:4] = cot_ref[Z - 2 : Z]
-    down_ref[0:2] = rec_ref[0:2]
-    down_ref[2:4] = cot_ref[0:2]
+    up_ref[0:1] = rec_ref[K // 2 - 1 : K // 2]
+    up_ref[1:3] = cot_ref[Z - 2 : Z]
+    down_ref[0:1] = rec_ref[0:1]
+    down_ref[1:3] = cot_ref[0:2]
 
 
 def side_groups(side, far_pair, near_pair):
@@ -230,9 +234,16 @@
     return jnp.where(low, near_pair, far_pair), jnp.where(low, far_pair, near_pair)
 
 
-def lift_tile(rec_ref, u_ref, lift, seen):
-    kz = rec_ref.shape[0]
-    rec = rec_ref[...].astype(F32).reshape(kz * Y, 128).astype(BF)
+def rows_of(rec_ref):
+    tiles = rec_ref.shape[0]
+    return rec_ref[...].astype(F32).reshape(tiles * Y, 128).astype(BF)
+
+
+def lift_tile(rec_ref, spread_ref, u_ref, lift, seen):
+    kz = 2 * rec_ref.shape[0]
+    rec = nn(spread_ref[...], rows_of(rec_ref))
+    row, lane = iota(rec.shape, 0), iota(rec.shape, 1)
+    rec = jnp.where((lane < C) | ((lane - C) >> 2 == (row & 1)), rec, 0.0).astype(BF)
     odd_row = (iota((kz, Y, 128), 1) & 1) == 1
     for e in (0, 1):
         both = nt(rec, u_ref[e * 256 : e * 256 + 256, :]).reshape(kz, Y, 256)
@@ -242,10 +253,12 @@
 
 
 def own_kernel(
-    rec_ref, up_ref, one_ref, two_ref, lift, seen, part, u_ref, w1x_ref, w2_ref, w1o_ref, col
+    rec_ref, up_ref, one_ref, two_ref,
+    lift, seen, part, u_ref, w1x_ref, w2_ref, spread_ref, w1o_ref, col,
 ):
+    spread_ref[...] = ones_where((iota((544, 272), 0) >> 1) == iota((544, 272), 1))
     forward_weights(up_ref, one_ref, two_ref, w1o_ref, w1x_ref, w2_ref, u_ref)
-    lift_tile(rec_ref, u_ref, lift, seen)
+    lift_tile(rec_ref, spread_ref, u_ref, lift, seen)
 
     def columns(k0, n):
         own = lift[pl.ds(k0, n)].reshape(2 * n, Y, 128)
@@ -262,14 +275,13 @@
 
 def forward_kernel(
     far_ref, near_ref, side_ref, cot_ref,
-    lift_own, seen_own, part_own, u_ref, w1x_ref, w2_ref,
+    lift_own, seen_own, part_own, u_ref, w1x_ref, w2_ref, spread_ref,
     act_ref, delta_ref, dec_ref, slope_ref, lifted_ref, keep_ref,
     lift, seen, mask, col1, part1, col2, part2,
 ):
-    kz = KZ
     side = side_ref[...] != 0
     for t, ref in enumerate((far_ref, near_ref)):
-        lift_tile(ref, u_ref, lift.at[t], seen.at[t])
+        lift_tile(ref, spread_ref, u_ref, lift.at[t], seen.at[t])
 
     def columns(k0, n):
         def load(own_ref, ref):
@@ -285,7 +297,7 @@
         live_own, live_near, _ = load(seen_own, seen)
         mask[at] = jnp.concatenate([live_own, live_near], axis=2)
 
-    over(kz, columns, 4)
+    over(KZ, columns, 4)
     for s in range(3):
 
         def keep1(at, value, s=s):
@@ -302,7 +314,7 @@
         act_ref[pl.ds(m, n)] = act.astype(BF)
         col2[pl.ds(pl.multiple_of(m * Y, 16), n * Y), :] = stack_y(act)
 
-    over(2 * kz - 2, first)
+    over(2 * KZ - 2, first)
 
     def keep2(at, value):
         part2[at] = value
@@ -323,7 +335,7 @@
         delta_ref[at] = (cot_ref[at].astype(F32) * slope).astype(BF)
         keep_ref[at] = live.astype(BF)
 
-    over(2 * kz - 4, second)
+    over(2 * KZ - 4, second)
 
 
 def wgrad(count, padded, shifted, col, total):
@@ -361,8 +373,8 @@
         hot_ref[:, h * 256 : h * 256 + 256] = hot.T
     cell, src = iota((256, 512), 0), iota((256, 512), 1)
     pick_ref[...] = ones_where(src == (cell & (K - 1)) * Y + 2 * (cell >> 6))
-    rec = rec_ref[...].astype(F32).reshape(K * Y, 128)
     row, lane = iota((K * Y, 128), 0), iota((K * Y, 128), 1)
+    rec = nn(ones_where((iota((512, 256), 0) >> 1) == iota((512, 256), 1)), rows_of(rec_ref))
     rec = jnp.where(lane < C, rec, pltpu.roll(rec, C, 1))
     parent_ref[...] = jnp.where(((row & 1) == 0) == (lane < C), rec, 0.0).astype(BF)
     dec_out[...] = dec_ref[2 : 2 + Z]
@@ -531,7 +543,7 @@
     cot = cotangent.transpose(3, 2, 1, 0).reshape(Z, Y, 128)
     rec, up_edge, down_edge = call(
         grid_kernel,
-        [((K, Y, 128), BF), ((4, Y, 128), BF), ((4, Y, 128), BF)],
+        [((K // 2, Y, 128), BF), ((3, Y, 128), BF), ((3, Y, 128), BF)],
         [((DEV * ROWS, 128), F32)],
     )(recv, child_mask, cot)
     odd_z = lax.axis_index("gz") % 2 == 1
@@ -539,17 +551,17 @@
         jnp.where(odd_z, up_edge, down_edge), jnp.where(odd_z, down_edge, up_edge), "gz"
     )
     before, after = jnp.where(odd_z, near, far), jnp.where(odd_z, far, near)
-    rec_ext = jnp.concatenate([before[0:2], rec, after[0:2]], axis=0)
-    cot_ext = jnp.concatenate([before[2:4], cot, after[2:4]], axis=0)
+    rec_ext = jnp.concatenate([before[0:1], rec, after[0:1]], axis=0)
+    cot_ext = jnp.concatenate([before[1:3], cot, after[1:3]], axis=0)
     even_x = lax.axis_index("xy") % 2 == 0
     side = (low_lanes((8, 128)) == even_x).astype(jnp.int32)
     rec_far, rec_near = swaps(rec_ext, rec_ext, "xy")
     weights = up_weight, conv_one, conv_two
-    lift_own, seen_own, part_own, u, w1x, w2 = call(
+    lift_own, seen_own, part_own, u, w1x, w2, spread = call(
         own_kernel,
         [
             ((KZ, 2, Y, 128), F32), ((KZ, 2, Y, 128), F32), ((3, 136, Y, 256), F32),
-            ((768, 128), BF), ((3, 256, 768), BF), ((384, 768), BF),
+            ((768, 128), BF), ((3, 256, 768), BF), ((384, 768), BF), ((544, 272), BF),
         ],
         [((3, 256, 384), BF), ((1088, 384), BF)],
     )(rec_ext, *weights)
@@ -563,7 +575,7 @@
             ((2, KZ, 2, Y, 128), F32), ((2, KZ, 2, Y, 128), F32), ((136, Y, 256), F32),
             ((1088, 768), BF), ((3, 136, Y, 256), F32), ((1072, 768), BF), ((134, Y, 384), F32),
         ],
-    )(rec_far, rec_near, side, cot_ext, lift_own, seen_own, part_own, u, w1x, w2)
+    )(rec_far, rec_near, side, cot_ext, lift_own, seen_own, part_own, u, w1x, w2, spread)
     delta_far, delta_near = swaps(delta, delta, "xy")
     two, hot, part_back, lifted_col, dec, b1x, b0, ud, pick, parent = call(
         second_grad_kernel,

time: 106 us -> 105 us (level)
  waiting for transfers between devices: 26.5 us -> 25.1 us
  blocking collectives: 26.9 us -> 25.8 us
    ppermute x6, waiting for transfers between devices: 4.18 us -> 2.79 us  [swap(): return lax.ppermute(array, axis, pairs + [(j, i) for i, j in pairs])]
  transfers between devices with their start and end apart: 8 -> 8, of which waited for: 5 -> 3; matrix products, arithmetic and copies ran while one was open for 2% -> 2% of each run, Pallas kernels for 7% -> 7%
where the time goes in v5:
time: 105 us; the launch traced here: 104 us
  starting transfers between devices  26.5 us (25%)
  blocking collectives  25.8 us (25%)
  waiting for transfers between devices  25.1 us (24%)
  Pallas kernels  23.7 us (23%)
  local copies, waits for them, and re-layouts  2.35 us (2%)
    all_to_all x1, blocking collectives, exchange(): return lax.all_to_all(array, ('gz', 'xy'), 0, 0, tiled=True)  25.8 us
    pallas_call x9, Pallas kernels, run(): pl.pallas_call(kernel, out_shape=shapes, in_specs=[vmem] * len(args), out...  23.7 us
    all_to_all x2, waiting for transfers between devices, exchange(): return lax.all_to_all(array, ('gz', 'xy'), 0, 0, tiled=True)  22.3 us
    all_to_all x2, starting transfers between devices, exchange(): return lax.all_to_all(array, ('gz', 'xy'), 0, 0, tiled=True)  15.8 us
    ppermute x6, starting transfers between devices, swap(): return lax.ppermute(array, axis, pairs + [(j, i) for i, j in pairs])  10.7 us
    ppermute x6, waiting for transfers between devices, swap(): return lax.ppermute(array, axis, pairs + [(j, i) for i, j in pairs])  2.79 us
  transfers between devices with their start and end apart: 8, of which 3 were waited for; matrix products, arithmetic and copies ran while one was open for 2% of the time, Pallas kernels for 7%

profile of v5, /device:TPU:1, one launch (start us, length us, event | category | flops | bytes accessed | tf_op | source)
XLA Modules:
  0.0 104.5 jit_solution(13230826716511389224)
XLA Ops:
  0.7 2.1 %shard_map.119 = bf16[1280,128]{1,0:T(8,128)(2,1)} custom-call(bf16[1,64,2048]{2,1,0:T(8,128)(2,1)} %feat_ref.1, s32[1,2048]{1,0:T(1,128)} %cell_ref.1, s32[1,128]{1,0:T(1,128)} %count_ref.1), custom_call_target="tpu_custom_call" | custom-call | tf_op jit(solution)/shard_map/pallas_call | solution.py:82
  2.8 11.5 %all-to-all-start = ((bf16[128,5,2,128]{3,2,1,0:T(2,128)(2,1)}), bf16[128,5,2,128]{3,2,1,0:T(2,128)(2,1)S(1)}, u32[]{:S(2)}, u32[]{:S(2)}) async-start(bf16[128,5,2,128]{3,2,1,0:T(2,128)(2,1)} %bitcast), calls=%async_computation | async-start | bytes 655360 | tf_op jit(solution)/shard_map/all_to_all | solution.py:530
  14.3 1.0 copy.15
  15.5 10.6 %all-to-all-done = bf16[128,5,2,128]{3,2,1,0:T(2,128)(2,1)S(1)} async-done(((bf16[128,5,2,128]{3,2,1,0:T(2,128)(2,1)}), bf16[128,5,2,128]{3,2,1,0:T(2,128)(2,1)S(1)}, u32[]{:S(2)}, u32[]{:S(2)}) %all-to-all-start) | async-done | bytes 327712 | tf_op jit(solution)/shard_map/all_to_all | solution.py:530
  26.1 1.3 %shard_map.120 = (bf16[32,8,128]{2,1,0:T(8,128)(2,1)S(1)}, bf16[3,8,128]{2,1,0:T(8,128)(2,1)S(1)}, bf16[3,8,128]{2,1,0:T(8,128)(2,1)S(1)}) custom-call(bf16[1280,128]{1,0:T(8,128)(2,1)S(1)} %bitcast.8, s32[2,8,128]{2,1,0:T(8,128)S(1)} %copy-done.3, bf16[128,8,128]{2,1,0:T(8,128)(2,1)S(1)} %copy.16.cot_ref), custom_call_target="tpu_custom_call" | custom-call | tf_op jit(solution)/shard_map/pallas_call | solution.py:82
  27.4 0.8 collective-permute-start
  28.2 2.1 %collective-permute-start.1 = (bf16[3,8,128]{2,1,0:T(8,128)(2,1)S(1)}, bf16[3,8,128]{2,1,0:T(8,128)(2,1)S(1)}, u32[]{:S(2)}, u32[]{:S(2)}) collective-permute-start(bf16[3,8,128]{2,1,0:T(8,128)(2,1)S(1)} %get-tuple-element.71), channel_id=1, source_target_pairs={{16,32},{48,64},{80,96},{32,16},{64,48},{96,80},{17,33},{49,65},{8... | collective-permute-start | bytes 18440 | tf_op jit(solution)/shard_map/ppermute | solution.py:522
  30.4 2.8 %collective-permute-done.1 = bf16[3,8,128]{2,1,0:T(8,128)(2,1)S(1)} collective-permute-done((bf16[3,8,128]{2,1,0:T(8,128)(2,1)S(1)}, bf16[3,8,128]{2,1,0:T(8,128)(2,1)S(1)}, u32[]{:S(2)}, u32[]{:S(2)}) %collective-permute-start.1) | collective-permute-done | bytes 6176 | tf_op jit(solution)/shard_map/ppermute | solution.py:522
  33.2 0.7 collective-permute-start.2
  33.9 1.9 %collective-permute-start.3 = (bf16[34,8,128]{2,1,0:T(8,128)(2,1)S(1)}, bf16[34,8,128]{2,1,0:T(8,128)(2,1)S(1)}, u32[]{:S(2)}, u32[]{:S(2)}) collective-permute-start(bf16[34,8,128]{2,1,0:T(8,128)(2,1)S(1)} %pad_maximum_fusion.1.rec_ref), channel_id=1, source_target_pairs={{0,1},{2,3},{4,5},{6,7},{8,9},{10,11},{12,13},{14,15},{1,0},{3,2},... | collective-permute-start | bytes 208904 | tf_op jit(solution)/shard_map/ppermute | solution.py:522
  35.8 2.1 %shard_map.121 = (f32[68,2,8,128]{3,2,1,0:T(8,128)S(1)}, f32[68,2,8,128]{3,2,1,0:T(8,128)S(1)}, f32[3,136,8,256]{3,2,1,0:T(8,128)S(1)}, bf16[768,128]{1,0:T(8,12...) custom-call(bf16[34,8,128]{2,1,0:T(8,128)(2,1)S(1)} %pad_maximum_fusion.1., ...), custom_call_target="tpu_custom_call" | custom-call | tf_op jit(solution)/shard_map/pallas_call | solution.py:82
  38.0 5.0 %shard_map.122 = (bf16[134,8,256]{2,1,0:T(8,128)(2,1)S(1)}, bf16[132,8,128]{2,1,0:T(8,128)(2,1)S(1)}, bf16[132,8,128]{2,1,0:T(8,128)(2,1)S(1)}, f32[134,8,256]{2...) custom-call(bf16[34,8,128]{2,1,0:T(8,128)(2,1)S(1)} %collective-permute-done.2.far_ref, ...), custom_call_target="tpu_custom_call" | custom-call | tf_op jit(solution)/shard_map/pallas_call | solution.py:82
  43.0 0.7 collective-permute-start.4
  43.7 4.5 %collective-permute-start.5 = (bf16[132,8,128]{2,1,0:T(8,128)(2,1)S(1)}, bf16[132,8,128]{2,1,0:T(8,128)(2,1)S(1)}, u32[]{:S(2)}, u32[]{:S(2)}) collective-permute-start(bf16[132,8,128]{2,1,0:T(8,128)(2,1)S(1)} %get-tuple-element.45.delta_ref), channel_id=1, source_target_pairs={{0,1},{2,3},{4,5},{6,7},{8,9},{10,11},{12,13},{14,15},{1,0},{3,2},... | collective-permute-start | bytes 811016 | tf_op jit(solution)/shard_map/ppermute | solution.py:522
  48.3 4.3 %shard_map.123 = (bf16[27,32,128]{2,1,0:T(8,128)(2,1)S(1)}, bf16[1024,512]{1,0:T(8,128)(2,1)S(1)}, f32[3,132,8,256]{3,2,1,0:T(8,128)S(1)}, bf16[1056,768]{1,0:T(...) custom-call(bf16[134,8,256]{2,1,0:T(8,128)(2,1)S(1)} %get-tuple-elem, ...), custom_call_target="tpu_custom_call" | custom-call | tf_op jit(solution)/shard_map/pallas_call | solution.py:82
  52.6 5.3 %shard_map.124 = bf16[128,24,128]{2,1,0:T(8,128)(2,1)S(1)} custom-call(bf16[132,8,128]{2,1,0:T(8,128)(2,1)S(1)} %collective-permute-done.4.far_ref, bf16[132,8,128]{2,1,0:T(8,128)(2,1)S(1)} %collective-permute-done.5.near_ref, s32[8,128]{1,0:T(8,128)S(1)} %iota.7.side_ref, f32[134,8,256]{2,1,0:T(8,128)S(1)} %get-tuple-element.49.slope_ref, ...), custom_call_target="tpu_custom_call" | custom-call | tf_op jit(solution)/shard_map/pallas_call | solution.py:82
  57.9 25.8 %all_to_all.15.recv_ref = bf16[128,24,128]{2,1,0:T(8,128)(2,1)S(1)} all-to-all(bf16[128,24,128]{2,1,0:T(8,128)(2,1)S(1)} %shard_map.124), channel_id=1, replica_groups=mesh['gz'=8,'xy'=16] {'gz','xy'}, dimensions={0} | all-to-all | bytes 1572864 | tf_op jit(solution)/shard_map/all_to_all | solution.py:530
  83.7 1.0 shard_map.126
  84.7 4.3 %all-to-all-start.2 = ((bf16[128,16,128]{2,1,0:T(8,128)(2,1)}), bf16[128,16,128]{2,1,0:T(8,128)(2,1)S(1)}, u32[]{:S(2)}, u32[]{:S(2)}) async-start(bf16[128,16,128]{2,1,0:T(8,128)(2,1)} %shard_map.126), calls=%async_computation.2 | async-start | bytes 1048576 | tf_op jit(solution)/shard_map/all_to_all | solution.py:530
  89.0 0.2 copy.18
  89.2 0.9 copy.19
  90.1 1.2 %shard_map.125 = bf16[1,64,2048]{2,1,0:T(8,128)(2,1)} custom-call(bf16[128,24,128]{2,1,0:T(8,128)(2,1)S(1)} %all_to_all.15.recv_ref), custom_call_target="tpu_custom_call" | custom-call | tf_op jit(solution)/shard_map/pallas_call | solution.py:82
  91.3 11.7 %all-to-all-done.2.recv_ref = bf16[128,16,128]{2,1,0:T(8,128)(2,1)S(1)} async-done(((bf16[128,16,128]{2,1,0:T(8,128)(2,1)}), bf16[128,16,128]{2,1,0:T(8,128)(2,1)S(1)}, u32[]{:S(2)}, u32[]{:S(2)}) %all-to-all-start.2) | async-done | bytes 524320 | tf_op jit(solution)/shard_map/all_to_all | solution.py:530
  103.0 1.5 %shard_map.127 = (f32[27,64,64]{2,1,0:T(8,128)}, f32[27,64,64]{2,1,0:T(8,128)}, f32[8,64,64]{2,1,0:T(8,128)}) custom-call(bf16[128,16,128]{2,1,0:T(8,128)(2,1)S(1)} %all-to-all-done.2.recv_ref), custom_call_target="tpu_custom_call" | custom-call | tf_op jit(solution)/shard_map/pallas_call | solution.py:82
  (24 shorter events, 0.3 us)
Async XLA Ops:
  0.6 25.5 %copy-start.3 = (s32[2,8,128]{2,1,0:T(8,128)S(1)}, s32[2,8,128]{2,1,0:T(8,128)}, u32[]{:S(2)}) copy-start(s32[2,8,128]{2,1,0:T(8,128)} %mask_ref.1) | copy-start | bytes 24580
  0.6 35.2 %copy-start.2 = (bf16[8,64,64]{2,1,0:T(8,128)(2,1)S(1)}, bf16[8,64,64]{2,1,0:T(8,128)(2,1)}, u32[]{:S(2)}) copy-start(bf16[8,64,64]{2,1,0:T(8,128)(2,1)} %up_ref.3) | copy-start | bytes 196612
  0.7 35.1 %copy-start = (bf16[27,64,64]{2,1,0:T(8,128)(2,1)S(1)}, bf16[27,64,64]{2,1,0:T(8,128)(2,1)}, u32[]{:S(2)}) copy-start(bf16[27,64,64]{2,1,0:T(8,128)(2,1)} %one_ref.3) | copy-start | bytes 663556
  0.7 35.1 %copy-start.1 = (bf16[27,64,64]{2,1,0:T(8,128)(2,1)S(1)}, bf16[27,64,64]{2,1,0:T(8,128)(2,1)}, u32[]{:S(2)}) copy-start(bf16[27,64,64]{2,1,0:T(8,128)(2,1)} %two_ref.3) | copy-start | bytes 663556
  2.8 23.4 %all-to-all-start = ((bf16[128,5,2,128]{3,2,1,0:T(2,128)(2,1)}), bf16[128,5,2,128]{3,2,1,0:T(2,128)(2,1)S(1)}, u32[]{:S(2)}, u32[]{:S(2)}) async-start(bf16[128,5,2,128]{3,2,1,0:T(2,128)(2,1)} %bitcast), calls=%async_computation | async-start | bytes 655360 | tf_op jit(solution)/shard_map/all_to_all | solution.py:530
  27.4 3.0 %collective-permute-start = (bf16[3,8,128]{2,1,0:T(8,128)(2,1)S(1)}, bf16[3,8,128]{2,1,0:T(8,128)(2,1)S(1)}, u32[]{:S(2)}, u32[]{:S(2)}) collective-permute-start(bf16[3,8,128]{2,1,0:T(8,128)(2,1)S(1)} %get-tuple-element.70), channel_id=1, source_target_pairs={{0,16},{32,48},{64,80},{96,112},{16,0},{48,32},{80,64},{112,96},{1... | collective-permute-start | bytes 18440 | tf_op jit(solution)/shard_map/ppermute | solution.py:522
  28.2 4.9 %collective-permute-start.1 = (bf16[3,8,128]{2,1,0:T(8,128)(2,1)S(1)}, bf16[3,8,128]{2,1,0:T(8,128)(2,1)S(1)}, u32[]{:S(2)}, u32[]{:S(2)}) collective-permute-start(bf16[3,8,128]{2,1,0:T(8,128)(2,1)S(1)} %get-tuple-element.71), channel_id=1, source_target_pairs={{16,32},{48,64},{80,96},{32,16},{64,48},{96,80},{17,33},{49,65},{8... | collective-permute-start | bytes 18440 | tf_op jit(solution)/shard_map/ppermute | solution.py:522
  33.2 4.7 %collective-permute-start.2 = (bf16[34,8,128]{2,1,0:T(8,128)(2,1)S(1)}, bf16[34,8,128]{2,1,0:T(8,128)(2,1)S(1)}, u32[]{:S(2)}, u32[]{:S(2)}) collective-permute-start(bf16[34,8,128]{2,1,0:T(8,128)(2,1)S(1)} %pad_maximum_fusion.1.rec_ref), channel_id=1, source_target_pairs={{1,2},{3,4},{5,6},{7,8},{9,10},{11,12},{13,14},{2,1},{4,3},{6,5},{... | collective-permute-start | bytes 208904 | tf_op jit(solution)/shard_map/ppermute | solution.py:522
  33.9 4.1 %collective-permute-start.3 = (bf16[34,8,128]{2,1,0:T(8,128)(2,1)S(1)}, bf16[34,8,128]{2,1,0:T(8,128)(2,1)S(1)}, u32[]{:S(2)}, u32[]{:S(2)}) collective-permute-start(bf16[34,8,128]{2,1,0:T(8,128)(2,1)S(1)} %pad_maximum_fusion.1.rec_ref), channel_id=1, source_target_pairs={{0,1},{2,3},{4,5},{6,7},{8,9},{10,11},{12,13},{14,15},{1,0},{3,2},... | collective-permute-start | bytes 208904 | tf_op jit(solution)/shard_map/ppermute | solution.py:522
  43.0 9.5 %collective-permute-start.4 = (bf16[132,8,128]{2,1,0:T(8,128)(2,1)S(1)}, bf16[132,8,128]{2,1,0:T(8,128)(2,1)S(1)}, u32[]{:S(2)}, u32[]{:S(2)}) collective-permute-start(bf16[132,8,128]{2,1,0:T(8,128)(2,1)S(1)} %get-tuple-element.45.delta_ref), channel_id=1, source_target_pairs={{1,2},{3,4},{5,6},{7,8},{9,10},{11,12},{13,14},{2,1},{4,3},{6,5},{... | collective-permute-start | bytes 811016 | tf_op jit(solution)/shard_map/ppermute | solution.py:522
  43.7 8.8 %collective-permute-start.5 = (bf16[132,8,128]{2,1,0:T(8,128)(2,1)S(1)}, bf16[132,8,128]{2,1,0:T(8,128)(2,1)S(1)}, u32[]{:S(2)}, u32[]{:S(2)}) collective-permute-start(bf16[132,8,128]{2,1,0:T(8,128)(2,1)S(1)} %get-tuple-element.45.delta_ref), channel_id=1, source_target_pairs={{0,1},{2,3},{4,5},{6,7},{8,9},{10,11},{12,13},{14,15},{1,0},{3,2},... | collective-permute-start | bytes 811016 | tf_op jit(solution)/shard_map/ppermute | solution.py:522
  84.7 18.3 %all-to-all-start.2 = ((bf16[128,16,128]{2,1,0:T(8,128)(2,1)}), bf16[128,16,128]{2,1,0:T(8,128)(2,1)S(1)}, u32[]{:S(2)}, u32[]{:S(2)}) async-start(bf16[128,16,128]{2,1,0:T(8,128)(2,1)} %shard_map.126), calls=%async_computation.2 | async-start | bytes 1048576 | tf_op jit(solution)/shard_map/all_to_all | solution.py:530

commit v6 on v5

--- a/solution.py
+++ b/solution.py
@@ -110,24 +110,34 @@
     return jnp.concatenate([a, b], axis=1)
 
 
-def forward_weights(up_ref, one_ref, two_ref, w1o_ref, w1x_ref, w2_ref, u_ref):
-    zero = jnp.zeros((C, C), BF)
+def first_weights(one_ref, own_ref, outer_ref):
     for oz in (-1, 0, 1):
         for oy in (-1, 0, 1):
             for n, xo in enumerate((0, 1, 2, -1)):
                 rows = slice(n * C, n * C + C)
                 for p in range(3):
-                    ref, at = w1o_ref, (oy + 1) * 128
+                    ref, at = own_ref, (oy + 1) * 128
                     if p:
-                        ref, at = w1x_ref, (oy + 1) * 256 + p * 128 - 128
+                        ref, at = outer_ref, (oy + 1) * 256 + p * 128 - 128
+                    if ref is None:
+                        continue
                     pair = [tap(one_ref, XK[2 * p + s] - xo, oy, oz) for s in (0, 1)]
                     ref[oz + 1, rows, at : at + 128] = join(*pair)
+
+
+def second_weights(two_ref, w2_ref):
+    for oz in (-1, 0, 1):
+        for oy in (-1, 0, 1):
             for n, xo in enumerate((0, 1)):
                 at_row = (oz + 1) * 128 + n * C
                 for p in range(2):
                     at = (oy + 1) * 256 + p * 128
                     pair = [tap(two_ref, XK[2 * p + s] - xo, oy, oz) for s in (0, 1)]
                     w2_ref[at_row : at_row + C, at : at + 128] = join(*pair)
+
+
+def lift_weights(up_ref, u_ref):
+    zero = jnp.zeros((C, C), BF)
     for e in (0, 1):
         for a in (0, 1):
             for b in (0, 1):
@@ -206,11 +216,9 @@
     return hot
 
 
-def grid_kernel(recv_ref, mask_ref, cot_ref, rec_ref, up_ref, down_ref, wide):
-    first, second = [nn(hot, recv_ref[...]) for hot in onehots(recv_ref, ROWS, wide)]
-    grid = jnp.where(low_lanes(first.shape), first + pltpu.roll(second, C, 1), 0.0).astype(BF)
-    row, col = iota((256, 256), 0), iota((256, 256), 1)
-    rec = nn(ones_where(col == (row & 3) * K + (row >> 2)), grid)
+def prepare_kernel(
+    mask_ref, up_ref, one_ref, marks_ref, spread_ref, w1x_ref, u_ref
+):
     kk, zz = iota((K, Y, Z), 0), iota((K, Y, Z), 2)
     zrow, lane = iota((Z, 128), 0), iota((Z, 128), 1)
     marks = jnp.zeros((512, 128), F32)
@@ -221,7 +229,18 @@
     odd_y = (iota((512, 128), 0) & 1) == 1
     marks = jnp.where(odd_y, pltpu.roll(marks, 4, 1), marks).astype(BF)
     fold = ones_where((iota((256, 512), 1) >> 1) == iota((256, 512), 0))
-    rec = (rec + nn(fold, marks)).reshape(K // 2, Y, 128).astype(BF)
+    marks_ref[...] = nn(fold, marks)
+    spread_ref[...] = ones_where((iota((544, 272), 0) >> 1) == iota((544, 272), 1))
+    first_weights(one_ref, None, w1x_ref)
+    lift_weights(up_ref, u_ref)
+
+
+def grid_kernel(recv_ref, marks_ref, cot_ref, rec_ref, up_ref, down_ref, wide):
+    first, second = [nn(hot, recv_ref[...]) for hot in onehots(recv_ref, ROWS, wide)]
+    grid = jnp.where(low_lanes(first.shape), first + pltpu.roll(second, C, 1), 0.0).astype(BF)
+    row, col = iota((256, 256), 0), iota((256, 256), 1)
+    pick = ones_where(col == (row & 3) * K + (row >> 2))
+    rec = (nn(pick, grid) + marks_ref[...]).reshape(K // 2, Y, 128).astype(BF)
     rec_ref[...] = rec
     up_ref[0:1] = rec_ref[K // 2 - 1 : K // 2]
     up_ref[1:3] = cot_ref[Z - 2 : Z]
@@ -253,11 +272,10 @@
 
 
 def own_kernel(
-    rec_ref, up_ref, one_ref, two_ref,
-    lift, seen, part, u_ref, w1x_ref, w2_ref, spread_ref, w1o_ref, col,
+    rec_ref, spread_ref, u_ref, one_ref, two_ref, lift, seen, part, w2_ref, w1o_ref, col
 ):
-    spread_ref[...] = ones_where((iota((544, 272), 0) >> 1) == iota((544, 272), 1))
-    forward_weights(up_ref, one_ref, two_ref, w1o_ref, w1x_ref, w2_ref, u_ref)
+    first_weights(one_ref, w1o_ref, None)
+    second_weights(two_ref, w2_ref)
     lift_tile(rec_ref, spread_ref, u_ref, lift, seen)
 
     def columns(k0, n):
@@ -276,8 +294,8 @@
 def forward_kernel(
     far_ref, near_ref, side_ref, cot_ref,
     lift_own, seen_own, part_own, u_ref, w1x_ref, w2_ref, spread_ref,
-    act_ref, delta_ref, dec_ref, slope_ref, lifted_ref, keep_ref,
-    lift, seen, mask, col1, part1, col2, part2,
+    act_ref, delta_ref, dec_ref, pre_ref, lifted_ref, keep_ref, mask,
+    lift, seen, col1, part1, col2, part2,
 ):
     side = side_ref[...] != 0
     for t, ref in enumerate((far_ref, near_ref)):
@@ -310,7 +328,7 @@
         live = mask[pl.ds(m + 1, n)]
         sig = jax.nn.sigmoid(pre)
         act = live * (pre * sig)
-        slope_ref[pl.ds(m, n)] = live * (sig * (1.0 + pre * (1.0 - sig)))
+        pre_ref[pl.ds(m, n)] = pre
         act_ref[pl.ds(m, n)] = act.astype(BF)
         col2[pl.ds(pl.multiple_of(m * Y, 16), n * Y), :] = stack_y(act)
 
@@ -365,8 +383,10 @@
 
 
 def second_grad_kernel(
-    act_ref, delta_ref, recv_ref, lifted_ref, dec_ref, rec_ref, up_ref, one_ref, two_ref,
+    act_ref, delta_ref, recv_ref, lifted_ref, dec_ref, rec_ref, pre_ref, mask_ref,
+    up_ref, one_ref, two_ref,
     out_ref, hot_ref, part_ref, lifted_col, dec_out, b1x_ref, b0_ref, ud_ref, pick_ref, parent_ref,
+    slope_ref,
     b1o_ref, padded, shifted, col, total, col3, wide,
 ):
     for h, hot in enumerate(onehots(recv_ref, 8, wide)):
@@ -396,6 +416,9 @@
     padded[132:136] = jnp.zeros((4, Y, 128), F32)
     padded[4:132] = delta_ref[2:130].astype(F32)
     def act_col(m, n):
+        pre = pre_ref[pl.ds(m, n)]
+        sig = jax.nn.sigmoid(pre)
+        slope_ref[pl.ds(m, n)] = mask_ref[pl.ds(m + 1, n)] * (sig * (1.0 + pre * (1.0 - sig)))
         rows = pl.ds(pl.multiple_of(m * Y, 16), n * Y)
         col[rows, :] = stack_y(act_ref[pl.ds(m, n)].astype(F32))
 
@@ -539,13 +562,21 @@
     sent = call(send_kernel, ((DEV * ROWS, 128), BF), [((DEV * ROWS, 128), F32)], raw=True, limit=58 << 20)(
         parent_feat, parent_cell, send_count
     )
+    sent, child_mask = lax.optimization_barrier((sent, child_mask))
     recv = exchange(sent.reshape(DEV, ROWS // 2, 2, 128)).reshape(DEV * ROWS, 128)
     cot = cotangent.transpose(3, 2, 1, 0).reshape(Z, Y, 128)
+    weights = up_weight, conv_one, conv_two
+    marks, spread, w1x, u = call(
+        prepare_kernel,
+        [
+            ((256, 128), F32), ((544, 272), BF), ((3, 256, 768), BF), ((768, 128), BF),
+        ],
+    )(child_mask, up_weight, conv_one)
     rec, up_edge, down_edge = call(
         grid_kernel,
         [((K // 2, Y, 128), BF), ((3, Y, 128), BF), ((3, Y, 128), BF)],
         [((DEV * ROWS, 128), F32)],
-    )(recv, child_mask, cot)
+    )(recv, marks, cot)
     odd_z = lax.axis_index("gz") % 2 == 1
     far, near = swaps(
         jnp.where(odd_z, up_edge, down_edge), jnp.where(odd_z, down_edge, up_edge), "gz"
@@ -556,40 +587,37 @@
     even_x = lax.axis_index("xy") % 2 == 0
     side = (low_lanes((8, 128)) == even_x).astype(jnp.int32)
     rec_far, rec_near = swaps(rec_ext, rec_ext, "xy")
-    weights = up_weight, conv_one, conv_two
-    lift_own, seen_own, part_own, u, w1x, w2, spread = call(
+    lift_own, seen_own, part_own, w2 = call(
         own_kernel,
-        [
-            ((KZ, 2, Y, 128), F32), ((KZ, 2, Y, 128), F32), ((3, 136, Y, 256), F32),
-            ((768, 128), BF), ((3, 256, 768), BF), ((384, 768), BF), ((544, 272), BF),
-        ],
+        [((KZ, 2, Y, 128), F32), ((KZ, 2, Y, 128), F32), ((3, 136, Y, 256), F32), ((384, 768), BF)],
         [((3, 256, 384), BF), ((1088, 384), BF)],
-    )(rec_ext, *weights)
-    act, delta, dec, slope, lifted, keep = call(
+    )(rec_ext, spread, u, conv_one, conv_two)
+    act, delta, dec, pre, lifted, keep, mask = call(
         forward_kernel,
         [
             ((134, Y, 256), BF), ((132, Y, 128), BF), ((132, Y, 128), BF),
             ((134, Y, 256), F32), ((136, Y, 256), BF), ((132, Y, 128), BF),
+            ((136, Y, 256), F32),
         ],
         [
-            ((2, KZ, 2, Y, 128), F32), ((2, KZ, 2, Y, 128), F32), ((136, Y, 256), F32),
+            ((2, KZ, 2, Y, 128), F32), ((2, KZ, 2, Y, 128), F32),
             ((1088, 768), BF), ((3, 136, Y, 256), F32), ((1072, 768), BF), ((134, Y, 384), F32),
         ],
     )(rec_far, rec_near, side, cot_ext, lift_own, seen_own, part_own, u, w1x, w2, spread)
     delta_far, delta_near = swaps(delta, delta, "xy")
-    two, hot, part_back, lifted_col, dec, b1x, b0, ud, pick, parent = call(
+    two, hot, part_back, lifted_col, dec, b1x, b0, ud, pick, parent, slope = call(
         second_grad_kernel,
         [
             ((27, 32, 128), BF), ((1024, 512), BF), ((3, 132, Y, 256), F32), ((1056, 768), BF),
             ((Z, Y, 128), BF), ((3, 768, 256), BF), ((768, 384), BF), ((2, 128, 128), BF),
-            ((256, 512), BF), ((512, 128), BF),
+            ((256, 512), BF), ((512, 128), BF), ((134, Y, 256), F32),
         ],
         [
             ((3, 384, 256), BF), ((136, Y, 128), F32), ((384, 1072), BF), ((1072, 768), BF), ((384, 768), F32),
             ((1056, 384), BF), ((DEV * ROWS, 128), F32),
         ],
-        home=(False, False, False, False, True, *[False] * 5),
-    )(act, delta, recv, lifted, dec, rec, *weights)
+        home=(False, False, False, False, True, *[False] * 6),
+    )(act, delta, recv, lifted, dec, rec, pre, mask, *weights)
     decoded = dec.reshape(Z, Y, 2, C).transpose(3, 2, 1, 0)
     message = call(
         backward_kernel,

time: 105 us -> 104 us (level)
    pallas_call x9 -> x10, Pallas kernels: 23.7 us -> 24 us  [run(): pl.pallas_call(kernel, out_shape=shapes, in_specs=[vmem] * len(args), out...]
  transfers between devices with their start and end apart: 8 -> 8, of which waited for: 3 -> 3; matrix products, arithmetic and copies ran while one was open for 2% -> 1% of each run, Pallas kernels for 7% -> 8%
where the time goes in v6:
time: 104 us
  starting transfers between devices  26.5 us (25%)
  blocking collectives  25.7 us (25%)
  waiting for transfers between devices  25.4 us (24%)
  Pallas kernels  24 us (23%)
  local copies, waits for them, and re-layouts  1.4 us (1%)
    all_to_all x1, blocking collectives, exchange(): return lax.all_to_all(array, ('gz', 'xy'), 0, 0, tiled=True)  25.7 us
    pallas_call x10, Pallas kernels, run(): pl.pallas_call(kernel, out_shape=shapes, in_specs=[vmem] * len(args), out...  24 us
    all_to_all x2, waiting for transfers between devices, exchange(): return lax.all_to_all(array, ('gz', 'xy'), 0, 0, tiled=True)  22.6 us
    all_to_all x2, starting transfers between devices, exchange(): return lax.all_to_all(array, ('gz', 'xy'), 0, 0, tiled=True)  15.8 us
    ppermute x6, starting transfers between devices, swap(): return lax.ppermute(array, axis, pairs + [(j, i) for i, j in pairs])  10.7 us
    ppermute x6, waiting for transfers between devices, swap(): return lax.ppermute(array, axis, pairs + [(j, i) for i, j in pairs])  2.78 us
  transfers between devices with their start and end apart: 8, of which 3 were waited for; matrix products, arithmetic and copies ran while one was open for 1% of the time, Pallas kernels for 8%

profile of v6, /device:TPU:1, one launch (start us, length us, event | category | flops | bytes accessed | tf_op | source)
XLA Modules:
  0.0 104.0 jit_solution(5310029537863034802)
XLA Ops:
  0.7 2.1 %shard_map.119 = bf16[1280,128]{1,0:T(8,128)(2,1)} custom-call(bf16[1,64,2048]{2,1,0:T(8,128)(2,1)} %feat_ref.1, s32[1,2048]{1,0:T(1,128)} %cell_ref.1, s32[1,128]{1,0:T(1,128)} %count_ref.1), custom_call_target="tpu_custom_call" | custom-call | tf_op jit(solution)/shard_map/pallas_call | solution.py:82
  2.8 11.5 %all-to-all-start = ((bf16[128,5,2,128]{3,2,1,0:T(2,128)(2,1)}), bf16[128,5,2,128]{3,2,1,0:T(2,128)(2,1)S(1)}, u32[]{:S(2)}, u32[]{:S(2)}) async-start(bf16[128,5,2,128]{3,2,1,0:T(2,128)(2,1)} %bitcast), calls=%async_computation | async-start | bytes 655360 | tf_op jit(solution)/shard_map/all_to_all | solution.py:553
  14.6 0.7 shard_map.120
  15.3 10.9 %all-to-all-done = bf16[128,5,2,128]{3,2,1,0:T(2,128)(2,1)S(1)} async-done(((bf16[128,5,2,128]{3,2,1,0:T(2,128)(2,1)}), bf16[128,5,2,128]{3,2,1,0:T(2,128)(2,1)S(1)}, u32[]{:S(2)}, u32[]{:S(2)}) %all-to-all-start) | async-done | bytes 327712 | tf_op jit(solution)/shard_map/all_to_all | solution.py:553
  26.1 1.0 shard_map.121
  27.1 0.8 collective-permute-start
  28.0 2.1 %collective-permute-start.1 = (bf16[3,8,128]{2,1,0:T(8,128)(2,1)S(1)}, bf16[3,8,128]{2,1,0:T(8,128)(2,1)S(1)}, u32[]{:S(2)}, u32[]{:S(2)}) collective-permute-start(bf16[3,8,128]{2,1,0:T(8,128)(2,1)S(1)} %get-tuple-element.81), channel_id=1, source_target_pairs={{16,32},{48,64},{80,96},{32,16},{64,48},{96,80},{17,33},{49,65},{8... | collective-permute-start | bytes 18440 | tf_op jit(solution)/shard_map/ppermute | solution.py:545
  30.1 2.8 %collective-permute-done.1 = bf16[3,8,128]{2,1,0:T(8,128)(2,1)S(1)} collective-permute-done((bf16[3,8,128]{2,1,0:T(8,128)(2,1)S(1)}, bf16[3,8,128]{2,1,0:T(8,128)(2,1)S(1)}, u32[]{:S(2)}, u32[]{:S(2)}) %collective-permute-start.1) | collective-permute-done | bytes 6176 | tf_op jit(solution)/shard_map/ppermute | solution.py:545
  33.0 0.7 collective-permute-start.2
  33.6 1.9 %collective-permute-start.3 = (bf16[34,8,128]{2,1,0:T(8,128)(2,1)S(1)}, bf16[34,8,128]{2,1,0:T(8,128)(2,1)S(1)}, u32[]{:S(2)}, u32[]{:S(2)}) collective-permute-start(bf16[34,8,128]{2,1,0:T(8,128)(2,1)S(1)} %pad_maximum_fusion.1.rec_ref), channel_id=1, source_target_pairs={{0,1},{2,3},{4,5},{6,7},{8,9},{10,11},{12,13},{14,15},{1,0},{3,2},... | collective-permute-start | bytes 208904 | tf_op jit(solution)/shard_map/ppermute | solution.py:545
  35.5 1.9 %shard_map.122 = (f32[68,2,8,128]{3,2,1,0:T(8,128)S(1)}, f32[68,2,8,128]{3,2,1,0:T(8,128)S(1)}, f32[3,136,8,256]{3,2,1,0:T(8,128)S(1)}, bf16[384,768]{1,0:T(8,128)(2,1)S(1)}) custom-call(bf16[34,8,128]{2,1,0:T(8,128)(2,1)S(1)} %pad_maximum_fusion.1.rec_ref, bf16[544,272]{1,0:T(8,128)(2,1)S(1)} %get-tuple-element.45.spread_ref, ...), custom_call_target="tpu_custom_call" | custom-call | tf_op jit(solution)/shard_map/pallas_call | solution.py:82
  37.5 4.9 %shard_map.123 = (bf16[134,8,256]{2,1,0:T(8,128)(2,1)S(1)}, bf16[132,8,128]{2,1,0:T(8,128)(2,1)S(1)}, bf16[132,8,128]{2,1,0:T(8,128)(2,1)S(1)}, f32[134,8,256]{2...) custom-call(bf16[34,8,128]{2,1,0:T(8,128)(2,1)S(1)} %collective-perm, ...), custom_call_target="tpu_custom_call" | custom-call | tf_op jit(solution)/shard_map/pallas_call | solution.py:82
  42.4 0.7 collective-permute-start.4
  43.0 4.5 %collective-permute-start.5 = (bf16[132,8,128]{2,1,0:T(8,128)(2,1)S(1)}, bf16[132,8,128]{2,1,0:T(8,128)(2,1)S(1)}, u32[]{:S(2)}, u32[]{:S(2)}) collective-permute-start(bf16[132,8,128]{2,1,0:T(8,128)(2,1)S(1)} %get-tuple-element.53.delta_ref), channel_id=1, source_target_pairs={{0,1},{2,3},{4,5},{6,7},{8,9},{10,11},{12,13},{14,15},{1,0},{3,2},... | collective-permute-start | bytes 811016 | tf_op jit(solution)/shard_map/ppermute | solution.py:545
  47.6 4.6 %shard_map.124 = (bf16[27,32,128]{2,1,0:T(8,128)(2,1)S(1)}, bf16[1024,512]{1,0:T(8,128)(2,1)S(1)}, f32[3,132,8,256]{3,2,1,0:T(8,128)S(1)}, bf16[1056,768]{1,0:T(...) custom-call(bf16[134,8,256]{2,1,0:T(8,128)(2,1)S(1)} %get-tuple-elem, ...), custom_call_target="tpu_custom_call" | custom-call | tf_op jit(solution)/shard_map/pallas_call | solution.py:82
  52.2 5.3 %shard_map.125 = bf16[128,24,128]{2,1,0:T(8,128)(2,1)S(1)} custom-call(bf16[132,8,128]{2,1,0:T(8,128)(2,1)S(1)} %collective-permute-done.4.far_ref, bf16[132,8,128]{2,1,0:T(8,128)(2,1)S(1)} %collective-permute-done.5.near_ref, s32[8,128]{1,0:T(8,128)S(1)} %iota.7.side_ref, f32[134,8,256]{2,1,0:T(8,128)S(1)} %get-tuple-element.59.slope_ref, ...), custom_call_target="tpu_custom_call" | custom-call | tf_op jit(solution)/shard_map/pallas_call | solution.py:82
  57.5 25.7 %all_to_all.15.recv_ref = bf16[128,24,128]{2,1,0:T(8,128)(2,1)S(1)} all-to-all(bf16[128,24,128]{2,1,0:T(8,128)(2,1)S(1)} %shard_map.125), channel_id=1, replica_groups=mesh['gz'=8,'xy'=16] {'gz','xy'}, dimensions={0} | all-to-all | bytes 1572864 | tf_op jit(solution)/shard_map/all_to_all | solution.py:553
  83.2 1.0 shard_map.127
  84.2 4.3 %all-to-all-start.2 = ((bf16[128,16,128]{2,1,0:T(8,128)(2,1)}), bf16[128,16,128]{2,1,0:T(8,128)(2,1)S(1)}, u32[]{:S(2)}, u32[]{:S(2)}) async-start(bf16[128,16,128]{2,1,0:T(8,128)(2,1)} %shard_map.127), calls=%async_computation.2 | async-start | bytes 1048576 | tf_op jit(solution)/shard_map/all_to_all | solution.py:553
  88.5 0.2 copy.18
  88.8 0.9 copy.19
  89.6 1.2 %shard_map.126 = bf16[1,64,2048]{2,1,0:T(8,128)(2,1)} custom-call(bf16[128,24,128]{2,1,0:T(8,128)(2,1)S(1)} %all_to_all.15.recv_ref), custom_call_target="tpu_custom_call" | custom-call | tf_op jit(solution)/shard_map/pallas_call | solution.py:82
  90.8 11.7 %all-to-all-done.2.recv_ref = bf16[128,16,128]{2,1,0:T(8,128)(2,1)S(1)} async-done(((bf16[128,16,128]{2,1,0:T(8,128)(2,1)}), bf16[128,16,128]{2,1,0:T(8,128)(2,1)S(1)}, u32[]{:S(2)}, u32[]{:S(2)}) %all-to-all-start.2) | async-done | bytes 524320 | tf_op jit(solution)/shard_map/all_to_all | solution.py:553
  102.5 1.5 %shard_map.128 = (f32[27,64,64]{2,1,0:T(8,128)}, f32[27,64,64]{2,1,0:T(8,128)}, f32[8,64,64]{2,1,0:T(8,128)}) custom-call(bf16[128,16,128]{2,1,0:T(8,128)(2,1)S(1)} %all-to-all-done.2.recv_ref), custom_call_target="tpu_custom_call" | custom-call | tf_op jit(solution)/shard_map/pallas_call | solution.py:82
  (27 shorter events, 0.4 us)
Async XLA Ops:
  0.6 13.9 %copy-start.3 = (s32[2,8,128]{2,1,0:T(8,128)S(1)}, s32[2,8,128]{2,1,0:T(8,128)}, u32[]{:S(2)}) copy-start(s32[2,8,128]{2,1,0:T(8,128)} %mask_ref) | copy-start | bytes 24580
  0.6 13.6 %copy-start.4 = (bf16[64,2,8,128]{3,2,1,0:T(8,128)(2,1)S(1)}, bf16[64,2,8,128]{3,2,1,0:T(8,128)(2,1)}, u32[]{:S(2)}) copy-start(bf16[64,2,8,128]{3,2,1,0:T(8,128)(2,1)} %param.15) | copy-start | bytes 786436
  0.7 13.9 %copy-start.2 = (bf16[8,64,64]{2,1,0:T(8,128)(2,1)S(1)}, bf16[8,64,64]{2,1,0:T(8,128)(2,1)}, u32[]{:S(2)}) copy-start(bf16[8,64,64]{2,1,0:T(8,128)(2,1)} %up_ref.3) | copy-start | bytes 196612
  0.7 13.9 %copy-start = (bf16[27,64,64]{2,1,0:T(8,128)(2,1)S(1)}, bf16[27,64,64]{2,1,0:T(8,128)(2,1)}, u32[]{:S(2)}) copy-start(bf16[27,64,64]{2,1,0:T(8,128)(2,1)} %one_ref.5) | copy-start | bytes 663556
  2.8 23.4 %all-to-all-start = ((bf16[128,5,2,128]{3,2,1,0:T(2,128)(2,1)}), bf16[128,5,2,128]{3,2,1,0:T(2,128)(2,1)S(1)}, u32[]{:S(2)}, u32[]{:S(2)}) async-start(bf16[128,5,2,128]{3,2,1,0:T(2,128)(2,1)} %bitcast), calls=%async_computation | async-start | bytes 655360 | tf_op jit(solution)/shard_map/all_to_all | solution.py:553
  14.3 21.2 %copy-start.1 = (bf16[27,64,64]{2,1,0:T(8,128)(2,1)S(1)}, bf16[27,64,64]{2,1,0:T(8,128)(2,1)}, u32[]{:S(2)}) copy-start(bf16[27,64,64]{2,1,0:T(8,128)(2,1)} %two_ref.3) | copy-start | bytes 663556
  27.1 3.0 %collective-permute-start = (bf16[3,8,128]{2,1,0:T(8,128)(2,1)S(1)}, bf16[3,8,128]{2,1,0:T(8,128)(2,1)S(1)}, u32[]{:S(2)}, u32[]{:S(2)}) collective-permute-start(bf16[3,8,128]{2,1,0:T(8,128)(2,1)S(1)} %get-tuple-element.80), channel_id=1, source_target_pairs={{0,16},{32,48},{64,80},{96,112},{16,0},{48,32},{80,64},{112,96},{1... | collective-permute-start | bytes 18440 | tf_op jit(solution)/shard_map/ppermute | solution.py:545
  28.0 4.9 %collective-permute-start.1 = (bf16[3,8,128]{2,1,0:T(8,128)(2,1)S(1)}, bf16[3,8,128]{2,1,0:T(8,128)(2,1)S(1)}, u32[]{:S(2)}, u32[]{:S(2)}) collective-permute-start(bf16[3,8,128]{2,1,0:T(8,128)(2,1)S(1)} %get-tuple-element.81), channel_id=1, source_target_pairs={{16,32},{48,64},{80,96},{32,16},{64,48},{96,80},{17,33},{49,65},{8... | collective-permute-start | bytes 18440 | tf_op jit(solution)/shard_map/ppermute | solution.py:545
  33.0 4.5 %collective-permute-start.2 = (bf16[34,8,128]{2,1,0:T(8,128)(2,1)S(1)}, bf16[34,8,128]{2,1,0:T(8,128)(2,1)S(1)}, u32[]{:S(2)}, u32[]{:S(2)}) collective-permute-start(bf16[34,8,128]{2,1,0:T(8,128)(2,1)S(1)} %pad_maximum_fusion.1.rec_ref), channel_id=1, source_target_pairs={{1,2},{3,4},{5,6},{7,8},{9,10},{11,12},{13,14},{2,1},{4,3},{6,5},{... | collective-permute-start | bytes 208904 | tf_op jit(solution)/shard_map/ppermute | solution.py:545
  33.6 3.8 %collective-permute-start.3 = (bf16[34,8,128]{2,1,0:T(8,128)(2,1)S(1)}, bf16[34,8,128]{2,1,0:T(8,128)(2,1)S(1)}, u32[]{:S(2)}, u32[]{:S(2)}) collective-permute-start(bf16[34,8,128]{2,1,0:T(8,128)(2,1)S(1)} %pad_maximum_fusion.1.rec_ref), channel_id=1, source_target_pairs={{0,1},{2,3},{4,5},{6,7},{8,9},{10,11},{12,13},{14,15},{1,0},{3,2},... | collective-permute-start | bytes 208904 | tf_op jit(solution)/shard_map/ppermute | solution.py:545
  42.4 9.8 %collective-permute-start.4 = (bf16[132,8,128]{2,1,0:T(8,128)(2,1)S(1)}, bf16[132,8,128]{2,1,0:T(8,128)(2,1)S(1)}, u32[]{:S(2)}, u32[]{:S(2)}) collective-permute-start(bf16[132,8,128]{2,1,0:T(8,128)(2,1)S(1)} %get-tuple-element.53.delta_ref), channel_id=1, source_target_pairs={{1,2},{3,4},{5,6},{7,8},{9,10},{11,12},{13,14},{2,1},{4,3},{6,5},{... | collective-permute-start | bytes 811016 | tf_op jit(solution)/shard_map/ppermute | solution.py:545
  43.0 9.1 %collective-permute-start.5 = (bf16[132,8,128]{2,1,0:T(8,128)(2,1)S(1)}, bf16[132,8,128]{2,1,0:T(8,128)(2,1)S(1)}, u32[]{:S(2)}, u32[]{:S(2)}) collective-permute-start(bf16[132,8,128]{2,1,0:T(8,128)(2,1)S(1)} %get-tuple-element.53.delta_ref), channel_id=1, source_target_pairs={{0,1},{2,3},{4,5},{6,7},{8,9},{10,11},{12,13},{14,15},{1,0},{3,2},... | collective-permute-start | bytes 811016 | tf_op jit(solution)/shard_map/ppermute | solution.py:545
  84.2 18.3 %all-to-all-start.2 = ((bf16[128,16,128]{2,1,0:T(8,128)(2,1)}), bf16[128,16,128]{2,1,0:T(8,128)(2,1)S(1)}, u32[]{:S(2)}, u32[]{:S(2)}) async-start(bf16[128,16,128]{2,1,0:T(8,128)(2,1)} %shard_map.127), calls=%async_computation.2 | async-start | bytes 1048576 | tf_op jit(solution)/shard_map/all_to_all | solution.py:553
